TPU v7x, 512 devices: a whole 4x8x8 slice. The times are simulated.
512 devices in a mesh: obs: 8 (over y), grid: 64 (over z, x, core).
Axes of the slice: x: 4, y: 8, z: 8, core: 2. Of those that a mesh axis runs over, the one named last changes fastest.
Arguments:
- adjoint_start: float32 [256, 8, 1024, 128], P('obs', None, 'grid'), may hold values from -2 to 2
- conductance: float32 [2, 8, 1024, 128], P(None, 'obs', 'grid'), may hold values from 0.2 to 5
- storage: float32 [8, 1024, 128], P('obs', 'grid'), may hold values from 0.5 to 2
- head: float32 [8, 1024, 128], P('obs', 'grid'), may hold values from -6 to 6
- layer_open: int32 [8, 1024, 128], P(None, 'grid'), may hold values 0 or 1
- krig_weight: float32 [4, 8, 1024, 128], P(None, 'obs', 'grid'), may hold values from 0.05 to 0.45
- krig_pilot: int32 [4, 8, 1024, 128], P(None, None, 'grid'), may hold values from 0 to 8191, as said below
- obs_cell: int32 [256, 2], P('obs'), may hold values from 0 to 1048575
- obs_weight: float32 [256, 2], P('obs'), may hold values from -8 to 8
Outputs:
- jacobian: float32 [2, 256, 8192], P(None, 'obs', 'grid')
Inputs may be any that keep to these rules, and one draw needn't show every extreme that they name: `krig_pilot`: owner block b holds the pilot points b * 128 to (b + 1) * 128 - 1. Every stencil member of a cell in column x lies in an owner block from t - 2 to t + 2, with t = x // 16.
All inputs are finite; a program needn't handle non-finite values. No bound on the sum of `layer_open` on one device may be relied on, other than what follows from the above.
Results may differ from a plain program's by a relative error of at most 0.00026.
Values sent between devices are 32-bit elements; how exact they have to be, the bound alone decides.
No kernel may reach another device: no remote copies, remote signals or barrier semaphores. Data moves between devices by JAX's collectives and lax.ppermute only.
A program may use at most 64 MiB of HBM per device.

v0:
```python
import jax
import jax.numpy as jnp
from jax import lax
from jax.sharding import PartitionSpec as P

NK = 4
RADIUS = 2
P_DEV = 128


OMEGA = 0.8


def extended(block, sides, width):
    for axis, dim in sides:
        count = lax.axis_size(axis)
        forward = [(i, i + 1) for i in range(count - 1)]
        backward = [(target, source) for source, target in forward]
        low = lax.ppermute(
            lax.slice_in_dim(block, block.shape[dim] - width, None, axis=dim), axis, forward
        )
        high = lax.ppermute(lax.slice_in_dim(block, 0, width, axis=dim), axis, backward)
        block = jnp.concatenate([low, block, high], axis=dim)
    return block


def from_behind(shard, axis, by):
    length = lax.axis_size(axis)
    pairs = [(i, i + by) for i in range(length) if 0 <= i + by < length]
    return lax.ppermute(shard, axis, pairs)


def harmonic(k_first, k_second):
    total = k_first + k_second
    return (
        2.0 * k_first * k_second / total,
        2.0 * k_first * k_second * k_second / (total * total),
        2.0 * k_second * k_first * k_first / (total * total),
    )


def lower_upper(face, axis):
    low_pad = [(0, 0)] * face.ndim
    high_pad = [(0, 0)] * face.ndim
    low_pad[axis] = (0, 1)
    high_pad[axis] = (1, 0)
    return (jnp.pad(face, low_pad), jnp.pad(face, high_pad))


def apply_darcy(adjoint, medium, live):
    live_b = live[None, :, None]
    k_horiz = jnp.where(live_b > 0, medium[0], 1.0)
    k_vert = jnp.where(live_b > 0, medium[1], 1.0)
    storage_c = jnp.where(live_b > 0, medium[2], 1.0)
    face_x = harmonic(k_horiz[:, :-1], k_horiz[:, 1:])[0] * live_b[:, :-1] * live_b[:, 1:]
    face_y = harmonic(k_horiz[:, :, :-1], k_horiz[:, :, 1:])[0]
    face_z = harmonic(k_vert[:-1], k_vert[1:])[0] * medium[4][:-1]
    pair_x = lower_upper(face_x, 1)
    pair_y = lower_upper(face_y, 2)
    pair_z = lower_upper(face_z, 0)
    diagonal = storage_c + pair_x[0] + pair_x[1] + pair_y[0] + pair_y[1] + pair_z[0] + pair_z[1]
    flux_x = lower_upper(face_x * (adjoint[:, :, :-1] - adjoint[:, :, 1:]), 2)
    flux_y = lower_upper(face_y * (adjoint[:, :, :, :-1] - adjoint[:, :, :, 1:]), 3)
    flux_z = lower_upper(face_z * (adjoint[:, :-1] - adjoint[:, 1:]), 1)
    applied = (
        storage_c * adjoint + flux_x[0] - flux_x[1] + flux_y[0] - flux_y[1] + flux_z[0] - flux_z[1]
    )
    return (applied, diagonal)


def jacobi(adjoint, medium, live, source):
    applied, diagonal = apply_darcy(adjoint, medium, live)
    return (adjoint + OMEGA * (source - applied) / diagonal) * live[None, None, :, None]


def sensitivity(adjoint, medium, live):
    live_b = live[None, :, None]
    k_horiz = jnp.where(live_b > 0, medium[0], 1.0)
    k_vert = jnp.where(live_b > 0, medium[1], 1.0)
    head_c = medium[3]
    unused_x, lower_x, upper_x = harmonic(k_horiz[:, :-1], k_horiz[:, 1:])
    mask_x = live_b[:, :-1] * live_b[:, 1:]
    prod_x = (adjoint[:, :, :-1] - adjoint[:, :, 1:]) * (head_c[:, :-1] - head_c[:, 1:]) * mask_x
    unused_y, lower_y, upper_y = harmonic(k_horiz[:, :, :-1], k_horiz[:, :, 1:])
    prod_y = (adjoint[:, :, :, :-1] - adjoint[:, :, :, 1:]) * (head_c[:, :, :-1] - head_c[:, :, 1:])
    unused_z, lower_z, upper_z = harmonic(k_vert[:-1], k_vert[1:])
    prod_z = (adjoint[:, :-1] - adjoint[:, 1:]) * (head_c[:-1] - head_c[1:]) * medium[4][:-1]
    horiz = (
        lower_upper(lower_x * prod_x, 2)[0]
        + lower_upper(upper_x * prod_x, 2)[1]
        + lower_upper(lower_y * prod_y, 3)[0]
        + lower_upper(upper_y * prod_y, 3)[1]
    )
    vert = lower_upper(lower_z * prod_z, 1)[0] + lower_upper(upper_z * prod_z, 1)[1]
    return jnp.stack([-horiz, -vert])


def shards(
    adjoint_start,
    conductance,
    storage,
    head,
    layer_open,
    krig_weight,
    krig_pilot,
    obs_cell,
    obs_weight,
):
    cond_all, storage_all, head_all, weight_all = (
        lax.all_gather(conductance, "obs", axis=1, tiled=True),
        lax.all_gather(storage, "obs", axis=0, tiled=True),
        lax.all_gather(head, "obs", axis=0, tiled=True),
        lax.all_gather(krig_weight, "obs", axis=1, tiled=True),
    )
    medium = jnp.stack(
        [cond_all[0], cond_all[1], storage_all, head_all, layer_open.astype(jnp.float32)]
    )
    obs_dev, layers, tile_x, tile_y = adjoint_start.shape
    grid_count = lax.axis_size("grid")
    tile_index = lax.axis_index("grid")
    whole_x = tile_x * grid_count
    medium_one = extended(medium, (("grid", 2),), 1)
    global_x = tile_index * tile_x + jnp.arange(-1, tile_x + 1, dtype=jnp.int32)
    live_one = ((global_x >= 0) & (global_x < whole_x)).astype(jnp.float32)
    global_x = tile_index * tile_x + jnp.arange(-1, tile_x + 1, dtype=jnp.int32)
    layer_idx = jnp.arange(layers, dtype=jnp.int32)[:, None, None]
    column = jnp.arange(tile_y, dtype=jnp.int32)[None, None, :]
    flat = (layer_idx * whole_x + global_x[None, :, None]) * tile_y + column
    hits = (flat[None, None] == obs_cell[:, :, None, None, None]).astype(jnp.float32)
    source_one = jnp.sum(hits * obs_weight[:, :, None, None, None], axis=1)

    def rimmed(field):
        return extended(field, (("grid", 2),), 1)

    adjoint = adjoint_start
    for sweep in range(2):
        adjoint = jacobi(rimmed(adjoint), medium_one, live_one, source_one)[:, :, 1:-1]
    sens = sensitivity(rimmed(adjoint), medium_one, live_one)[:, :, :, 1:-1]
    span = (2 * RADIUS + 1) * P_DEV
    base = (tile_index - RADIUS) * P_DEV
    sens_rows = jnp.moveaxis(sens.reshape(2 * obs_dev, layers, tile_x, tile_y), 2, 0).reshape(
        tile_x, 2 * obs_dev, layers * tile_y
    )
    relative = jnp.moveaxis(krig_pilot, 2, 0).reshape(tile_x, NK, layers * tile_y) - base
    weights = jnp.moveaxis(weight_all, 2, 0).reshape(tile_x, NK, layers * tile_y)
    columns = jnp.arange(span, dtype=jnp.int32)

    def accumulate(total, item):
        block, rel_block, weight_block = item
        matrix = jnp.zeros((block.shape[1], span), jnp.float32)
        for member in range(NK):
            matrix = matrix + weight_block[member][:, None] * (
                rel_block[member][:, None] == columns[None, :]
            ).astype(jnp.float32)
        return (
            total
            + jnp.dot(
                block, matrix, precision=lax.Precision.HIGHEST, preferred_element_type=jnp.float32
            ),
            None,
        )

    partial_sum, unused = lax.scan(
        accumulate, jnp.zeros((2 * obs_dev, span), jnp.float32), (sens_rows, relative, weights)
    )
    partial_sum = partial_sum.reshape(2, obs_dev, span)
    owned = jnp.zeros((2, obs_dev, P_DEV), jnp.float32)
    for offset in range(2 * RADIUS + 1):
        piece = partial_sum[:, :, offset * P_DEV : (offset + 1) * P_DEV]
        if offset == RADIUS:
            owned = owned + piece
        else:
            owned = owned + from_behind(piece, "grid", offset - RADIUS)
    return owned


def solution(mesh):
    return jax.shard_map(
        shards,
        mesh=mesh,
        in_specs=(
            P("obs", None, "grid", None),
            P(None, "obs", "grid", None),
            P("obs", "grid", None),
            P("obs", "grid", None),
            P(None, "grid", None),
            P(None, "obs", "grid", None),
            P(None, None, "grid", None),
            P("obs", None),
            P("obs", None),
        ),
        out_specs=P(None, "obs", "grid"),
        check_vma=False,
    )
```

profile of v0, /device:TPU:199, one launch (start us, length us, event | category | flops | bytes accessed | tf_op | source)
XLA Modules:
  0.0 289.4 jit_solution(1963081828648442636)
XLA Ops:
  0.0 20.3 %all_gather.12 = f32[2,8,16,128]{3,2,0,1:T(8,128)S(1)} all-gather(f32[2,1,16,128]{3,2,0,1:T(8,128)} %bitcast.111), channel_id=1, replica_groups=mesh['obs'=8,'grid'=64] {'obs'}, dimensions={1}, use_global_device_ids=true | all-gather | bytes 147456 | tf_op jit(solution)/shard_map/all_gather | solution.py:110
  20.4 18.5 %all_gather.14 = f32[8,16,128]{2,1,0:T(8,128)S(1)} all-gather(f32[1,16,128]{2,1,0:T(8,128)} %param.14), channel_id=1, replica_groups=mesh['obs'=8,'grid'=64] {'obs'}, dimensions={0}, use_global_device_ids=true | all-gather | bytes 73728 | tf_op jit(solution)/shard_map/all_gather | solution.py:112
  38.9 18.8 %all_gather.13 = f32[8,16,128]{2,1,0:T(8,128)S(1)} all-gather(f32[1,16,128]{2,1,0:T(8,128)} %param.13), channel_id=1, replica_groups=mesh['obs'=8,'grid'=64] {'obs'}, dimensions={0}, use_global_device_ids=true | all-gather | bytes 73728 | tf_op jit(solution)/shard_map/all_gather | solution.py:111
  58.6 24.1 %collective-permute-start = (f32[5,8,1,128]{3,1,2,0:T(8,128)S(1)}, f32[5,8,1,128]{3,1,2,0:T(8,128)S(1)}, u32[]{:S(2)}, u32[]{:S(2)}) collective-permute-start(f32[5,8,1,128]{3,1,2,0:T(8,128)S(1)} %get-tuple-element.121), channel_id=1, source_target_pairs={{0,1},{1,2},{2,3},{3,4},{4,5},{5,6},{6,7},{7,8},{8,9},{9,10},{10,1... | collective-permute-start | bytes 61448 | tf_op jit(solution)/shard_map/ppermute | solution.py:19
  89.4 7.0 %collective-permute-start.2 = (f32[32,8,1,128]{3,1,2,0:T(8,128)}, f32[32,8,1,128]{3,1,2,0:T(8,128)}, u32[]{:S(2)}, u32[]{:S(2)}) collective-permute-start(f32[32,8,1,128]{3,1,2,0:T(8,128)} %get-tuple-element.114), channel_id=1, source_target_pairs={{0,1},{1,2},{2,3},{3,4},{4,5},{5,6},{6,7},{7,8},{8,9},{9,10},{10,1... | collective-permute-start | bytes 393224 | tf_op jit(solution)/shard_map/ppermute | solution.py:19
  99.8 18.8 %all_gather.15 = f32[4,8,16,128]{3,2,1,0:T(8,128)S(1)} all-gather(f32[4,1,16,128]{3,2,1,0:T(8,128)S(1)} %copy-done.5), channel_id=1, replica_groups=mesh['obs'=8,'grid'=64] {'obs'}, dimensions={1}, use_global_device_ids=true | all-gather | bytes 294912 | tf_op jit(solution)/shard_map/all_gather | solution.py:113
  131.5 13.1 %collective-permute-start.4 = (f32[32,8,1,128]{3,1,2,0:T(8,128)S(1)}, f32[32,8,1,128]{3,1,2,0:T(8,128)S(1)}, u32[]{:S(2)}, u32[]{:S(2)}) collective-permute-start(f32[32,8,1,128]{3,1,2,0:T(8,128)S(1)} %get-tuple-element.111), channel_id=1, source_target_pairs={{0,1},{1,2},{2,3},{3,4},{4,5},{5,6},{6,7},{7,8},{8,9},{9,10},{10,1... | collective-permute-start | bytes 393224 | tf_op jit(solution)/shard_map/ppermute | solution.py:19
  146.9 7.3 %collective-permute-done.5 = f32[32,8,1,128]{3,1,2,0:T(8,128)S(1)} collective-permute-done((f32[32,8,1,128]{3,1,2,0:T(8,128)S(1)}, f32[32,8,1,128]{3,1,2,0:T(8,128)S(1)}, u32[]{:S(2)}, u32[]{:S(2)}) %collective-permute-start.5) | collective-permute-done | bytes 131104 | tf_op jit(solution)/shard_map/ppermute | solution.py:22
  159.4 2.6 collective-permute-start.7
  162.2 6.7 %collective-permute-done.7 = f32[32,8,1,128]{3,1,2,0:T(8,128)S(1)} collective-permute-done((f32[32,8,1,128]{3,1,2,0:T(8,128)S(1)}, f32[32,8,1,128]{3,1,2,0:T(8,128)S(1)}, u32[]{:S(2)}, u32[]{:S(2)}) %collective-permute-start.7) | collective-permute-done | bytes 131104 | tf_op jit(solution)/shard_map/ppermute | solution.py:22
  172.2 2.5 pad_maximum_fusion
  174.7 4.9 %reshape.142 = f32[16,64,1024]{2,0,1:T(8,128)} reshape(f32[16,64,8,128]{3,2,0,1:T(8,128)} %bitcast.95) | data formatting | bytes 8388608 | tf_op jit(solution)/shard_map/reshape | solution.py:141
  179.6 93.4 %while.12 = (s32[]{:T(128)}, f32[64,640]{1,0:T(8,128)S(1)}, f32[16,64,1024]{2,0,1:T(8,128)}, s32[16,4,1024]{2,1,0:T(4,128)}, f32[16,4,1024]{2,1,0:T(4,128)S(1)}, /*index=5*/s32[]{:T(128)}, s32[]{:T(128)}, s32[]{}, s32[]{}, s32[]{}) while((s32[]{:T(128)}, f32[64,640]{1,0:T(8,128)S(1)}, f32[16,64,1024]{2,0,1:T(8,128)}, ...), condition=%wide.region_2.3_spmd.clone.clone, body=%wide.region_1.2_spmd.clone.clone.sunk | while | flops 510607360 | bytes 1212599 | solution.py:163
  182.4 3.1 %fusion.56 = f32[64,640]{1,0:T(8,128)S(1)} fusion(f32[1024]{0:T(1024)S(1)} %bitcast.106, s32[1024]{0:T(1024)S(1)} %bitcast.110, f32[1024]{0:T(1024)S(1)} %bitcast.104, s32[1024]{0:T(1024)S(1)} %bitcast.108, f32[1024]{0:T(1024)S(1)} %bitcast.105, s32[1024]{0:T(1024)S(1)} %bitcast.109, f32[1024]{0:T(1024)S(1)} %bitcast.103, s32[1024]{0:T(1024)S(1)} %bitcast.107, ...), kind=kOutput, calls=%fused_computation.22.clone.1 | convolution fusion | flops 510607360 | bytes 622593 | tf_op jit(solution)/shard_map/while/body/eval_jaxpr/dot_general | solution.py:157
  188.2 3.1 %fusion.56 = f32[64,640]{1,0:T(8,128)S(1)} fusion(f32[1024]{0:T(1024)S(1)} %bitcast.106, s32[1024]{0:T(1024)S(1)} %bitcast.110, f32[1024]{0:T(1024)S(1)} %bitcast.104, s32[1024]{0:T(1024)S(1)} %bitcast.108, f32[1024]{0:T(1024)S(1)} %bitcast.105, s32[1024]{0:T(1024)S(1)} %bitcast.109, f32[1024]{0:T(1024)S(1)} %bitcast.103, s32[1024]{0:T(1024)S(1)} %bitcast.107, ...), kind=kOutput, calls=%fused_computation.22.clone.1 | convolution fusion | flops 510607360 | bytes 622593 | tf_op jit(solution)/shard_map/while/body/eval_jaxpr/dot_general | solution.py:157
  194.1 3.1 %fusion.56 = f32[64,640]{1,0:T(8,128)S(1)} fusion(f32[1024]{0:T(1024)S(1)} %bitcast.106, s32[1024]{0:T(1024)S(1)} %bitcast.110, f32[1024]{0:T(1024)S(1)} %bitcast.104, s32[1024]{0:T(1024)S(1)} %bitcast.108, f32[1024]{0:T(1024)S(1)} %bitcast.105, s32[1024]{0:T(1024)S(1)} %bitcast.109, f32[1024]{0:T(1024)S(1)} %bitcast.103, s32[1024]{0:T(1024)S(1)} %bitcast.107, ...), kind=kOutput, calls=%fused_computation.22.clone.1 | convolution fusion | flops 510607360 | bytes 622593 | tf_op jit(solution)/shard_map/while/body/eval_jaxpr/dot_general | solution.py:157
  199.9 3.1 %fusion.56 = f32[64,640]{1,0:T(8,128)S(1)} fusion(f32[1024]{0:T(1024)S(1)} %bitcast.106, s32[1024]{0:T(1024)S(1)} %bitcast.110, f32[1024]{0:T(1024)S(1)} %bitcast.104, s32[1024]{0:T(1024)S(1)} %bitcast.108, f32[1024]{0:T(1024)S(1)} %bitcast.105, s32[1024]{0:T(1024)S(1)} %bitcast.109, f32[1024]{0:T(1024)S(1)} %bitcast.103, s32[1024]{0:T(1024)S(1)} %bitcast.107, ...), kind=kOutput, calls=%fused_computation.22.clone.1 | convolution fusion | flops 510607360 | bytes 622593 | tf_op jit(solution)/shard_map/while/body/eval_jaxpr/dot_general | solution.py:157
  205.7 3.1 %fusion.56 = f32[64,640]{1,0:T(8,128)S(1)} fusion(f32[1024]{0:T(1024)S(1)} %bitcast.106, s32[1024]{0:T(1024)S(1)} %bitcast.110, f32[1024]{0:T(1024)S(1)} %bitcast.104, s32[1024]{0:T(1024)S(1)} %bitcast.108, f32[1024]{0:T(1024)S(1)} %bitcast.105, s32[1024]{0:T(1024)S(1)} %bitcast.109, f32[1024]{0:T(1024)S(1)} %bitcast.103, s32[1024]{0:T(1024)S(1)} %bitcast.107, ...), kind=kOutput, calls=%fused_computation.22.clone.1 | convolution fusion | flops 510607360 | bytes 622593 | tf_op jit(solution)/shard_map/while/body/eval_jaxpr/dot_general | solution.py:157
  211.6 3.1 %fusion.56 = f32[64,640]{1,0:T(8,128)S(1)} fusion(f32[1024]{0:T(1024)S(1)} %bitcast.106, s32[1024]{0:T(1024)S(1)} %bitcast.110, f32[1024]{0:T(1024)S(1)} %bitcast.104, s32[1024]{0:T(1024)S(1)} %bitcast.108, f32[1024]{0:T(1024)S(1)} %bitcast.105, s32[1024]{0:T(1024)S(1)} %bitcast.109, f32[1024]{0:T(1024)S(1)} %bitcast.103, s32[1024]{0:T(1024)S(1)} %bitcast.107, ...), kind=kOutput, calls=%fused_computation.22.clone.1 | convolution fusion | flops 510607360 | bytes 622593 | tf_op jit(solution)/shard_map/while/body/eval_jaxpr/dot_general | solution.py:157
  217.4 3.1 %fusion.56 = f32[64,640]{1,0:T(8,128)S(1)} fusion(f32[1024]{0:T(1024)S(1)} %bitcast.106, s32[1024]{0:T(1024)S(1)} %bitcast.110, f32[1024]{0:T(1024)S(1)} %bitcast.104, s32[1024]{0:T(1024)S(1)} %bitcast.108, f32[1024]{0:T(1024)S(1)} %bitcast.105, s32[1024]{0:T(1024)S(1)} %bitcast.109, f32[1024]{0:T(1024)S(1)} %bitcast.103, s32[1024]{0:T(1024)S(1)} %bitcast.107, ...), kind=kOutput, calls=%fused_computation.22.clone.1 | convolution fusion | flops 510607360 | bytes 622593 | tf_op jit(solution)/shard_map/while/body/eval_jaxpr/dot_general | solution.py:157
  223.2 3.1 %fusion.56 = f32[64,640]{1,0:T(8,128)S(1)} fusion(f32[1024]{0:T(1024)S(1)} %bitcast.106, s32[1024]{0:T(1024)S(1)} %bitcast.110, f32[1024]{0:T(1024)S(1)} %bitcast.104, s32[1024]{0:T(1024)S(1)} %bitcast.108, f32[1024]{0:T(1024)S(1)} %bitcast.105, s32[1024]{0:T(1024)S(1)} %bitcast.109, f32[1024]{0:T(1024)S(1)} %bitcast.103, s32[1024]{0:T(1024)S(1)} %bitcast.107, ...), kind=kOutput, calls=%fused_computation.22.clone.1 | convolution fusion | flops 510607360 | bytes 622593 | tf_op jit(solution)/shard_map/while/body/eval_jaxpr/dot_general | solution.py:157
  229.1 3.1 %fusion.56 = f32[64,640]{1,0:T(8,128)S(1)} fusion(f32[1024]{0:T(1024)S(1)} %bitcast.106, s32[1024]{0:T(1024)S(1)} %bitcast.110, f32[1024]{0:T(1024)S(1)} %bitcast.104, s32[1024]{0:T(1024)S(1)} %bitcast.108, f32[1024]{0:T(1024)S(1)} %bitcast.105, s32[1024]{0:T(1024)S(1)} %bitcast.109, f32[1024]{0:T(1024)S(1)} %bitcast.103, s32[1024]{0:T(1024)S(1)} %bitcast.107, ...), kind=kOutput, calls=%fused_computation.22.clone.1 | convolution fusion | flops 510607360 | bytes 622593 | tf_op jit(solution)/shard_map/while/body/eval_jaxpr/dot_general | solution.py:157
  234.9 3.1 %fusion.56 = f32[64,640]{1,0:T(8,128)S(1)} fusion(f32[1024]{0:T(1024)S(1)} %bitcast.106, s32[1024]{0:T(1024)S(1)} %bitcast.110, f32[1024]{0:T(1024)S(1)} %bitcast.104, s32[1024]{0:T(1024)S(1)} %bitcast.108, f32[1024]{0:T(1024)S(1)} %bitcast.105, s32[1024]{0:T(1024)S(1)} %bitcast.109, f32[1024]{0:T(1024)S(1)} %bitcast.103, s32[1024]{0:T(1024)S(1)} %bitcast.107, ...), kind=kOutput, calls=%fused_computation.22.clone.1 | convolution fusion | flops 510607360 | bytes 622593 | tf_op jit(solution)/shard_map/while/body/eval_jaxpr/dot_general | solution.py:157
  240.7 3.1 %fusion.56 = f32[64,640]{1,0:T(8,128)S(1)} fusion(f32[1024]{0:T(1024)S(1)} %bitcast.106, s32[1024]{0:T(1024)S(1)} %bitcast.110, f32[1024]{0:T(1024)S(1)} %bitcast.104, s32[1024]{0:T(1024)S(1)} %bitcast.108, f32[1024]{0:T(1024)S(1)} %bitcast.105, s32[1024]{0:T(1024)S(1)} %bitcast.109, f32[1024]{0:T(1024)S(1)} %bitcast.103, s32[1024]{0:T(1024)S(1)} %bitcast.107, ...), kind=kOutput, calls=%fused_computation.22.clone.1 | convolution fusion | flops 510607360 | bytes 622593 | tf_op jit(solution)/shard_map/while/body/eval_jaxpr/dot_general | solution.py:157
  246.6 3.1 %fusion.56 = f32[64,640]{1,0:T(8,128)S(1)} fusion(f32[1024]{0:T(1024)S(1)} %bitcast.106, s32[1024]{0:T(1024)S(1)} %bitcast.110, f32[1024]{0:T(1024)S(1)} %bitcast.104, s32[1024]{0:T(1024)S(1)} %bitcast.108, f32[1024]{0:T(1024)S(1)} %bitcast.105, s32[1024]{0:T(1024)S(1)} %bitcast.109, f32[1024]{0:T(1024)S(1)} %bitcast.103, s32[1024]{0:T(1024)S(1)} %bitcast.107, ...), kind=kOutput, calls=%fused_computation.22.clone.1 | convolution fusion | flops 510607360 | bytes 622593 | tf_op jit(solution)/shard_map/while/body/eval_jaxpr/dot_general | solution.py:157
  252.4 3.1 %fusion.56 = f32[64,640]{1,0:T(8,128)S(1)} fusion(f32[1024]{0:T(1024)S(1)} %bitcast.106, s32[1024]{0:T(1024)S(1)} %bitcast.110, f32[1024]{0:T(1024)S(1)} %bitcast.104, s32[1024]{0:T(1024)S(1)} %bitcast.108, f32[1024]{0:T(1024)S(1)} %bitcast.105, s32[1024]{0:T(1024)S(1)} %bitcast.109, f32[1024]{0:T(1024)S(1)} %bitcast.103, s32[1024]{0:T(1024)S(1)} %bitcast.107, ...), kind=kOutput, calls=%fused_computation.22.clone.1 | convolution fusion | flops 510607360 | bytes 622593 | tf_op jit(solution)/shard_map/while/body/eval_jaxpr/dot_general | solution.py:157
  258.2 3.1 %fusion.56 = f32[64,640]{1,0:T(8,128)S(1)} fusion(f32[1024]{0:T(1024)S(1)} %bitcast.106, s32[1024]{0:T(1024)S(1)} %bitcast.110, f32[1024]{0:T(1024)S(1)} %bitcast.104, s32[1024]{0:T(1024)S(1)} %bitcast.108, f32[1024]{0:T(1024)S(1)} %bitcast.105, s32[1024]{0:T(1024)S(1)} %bitcast.109, f32[1024]{0:T(1024)S(1)} %bitcast.103, s32[1024]{0:T(1024)S(1)} %bitcast.107, ...), kind=kOutput, calls=%fused_computation.22.clone.1 | convolution fusion | flops 510607360 | bytes 622593 | tf_op jit(solution)/shard_map/while/body/eval_jaxpr/dot_general | solution.py:157
  264.1 3.1 %fusion.56 = f32[64,640]{1,0:T(8,128)S(1)} fusion(f32[1024]{0:T(1024)S(1)} %bitcast.106, s32[1024]{0:T(1024)S(1)} %bitcast.110, f32[1024]{0:T(1024)S(1)} %bitcast.104, s32[1024]{0:T(1024)S(1)} %bitcast.108, f32[1024]{0:T(1024)S(1)} %bitcast.105, s32[1024]{0:T(1024)S(1)} %bitcast.109, f32[1024]{0:T(1024)S(1)} %bitcast.103, s32[1024]{0:T(1024)S(1)} %bitcast.107, ...), kind=kOutput, calls=%fused_computation.22.clone.1 | convolution fusion | flops 510607360 | bytes 622593 | tf_op jit(solution)/shard_map/while/body/eval_jaxpr/dot_general | solution.py:157
  269.9 3.1 %fusion.56 = f32[64,640]{1,0:T(8,128)S(1)} fusion(f32[1024]{0:T(1024)S(1)} %bitcast.106, s32[1024]{0:T(1024)S(1)} %bitcast.110, f32[1024]{0:T(1024)S(1)} %bitcast.104, s32[1024]{0:T(1024)S(1)} %bitcast.108, f32[1024]{0:T(1024)S(1)} %bitcast.105, s32[1024]{0:T(1024)S(1)} %bitcast.109, f32[1024]{0:T(1024)S(1)} %bitcast.103, s32[1024]{0:T(1024)S(1)} %bitcast.107, ...), kind=kOutput, calls=%fused_computation.22.clone.1 | convolution fusion | flops 510607360 | bytes 622593 | tf_op jit(solution)/shard_map/while/body/eval_jaxpr/dot_general | solution.py:157
  276.9 3.4 %collective-permute-start.8 = (f32[2,32,128]{2,1,0:T(8,128)S(1)}, f32[2,32,128]{2,1,0:T(8,128)S(1)}, u32[]{:S(2)}, u32[]{:S(2)}) collective-permute-start(f32[2,32,128]{2,1,0:T(8,128)S(1)} %get-tuple-element.126), channel_id=1, source_target_pairs={{2,0},{3,1},{4,2},{5,3},{6,4},{7,5},{8,6},{9,7},{10,8},{11,9},{12,... | collective-permute-start | bytes 98312 | tf_op jit(solution)/shard_map/ppermute | solution.py:30
  280.2 3.0 %collective-permute-start.9 = (f32[2,32,128]{2,1,0:T(8,128)S(1)}, f32[2,32,128]{2,1,0:T(8,128)S(1)}, u32[]{:S(2)}, u32[]{:S(2)}) collective-permute-start(f32[2,32,128]{2,1,0:T(8,128)S(1)} %get-tuple-element.123), channel_id=1, source_target_pairs={{1,0},{2,1},{3,2},{4,3},{5,4},{6,5},{7,6},{8,7},{9,8},{10,9},{11,1... | collective-permute-start | bytes 98312 | tf_op jit(solution)/shard_map/ppermute | solution.py:30
  284.8 3.9 %collective-permute-done.9 = f32[2,32,128]{2,1,0:T(8,128)S(1)} collective-permute-done((f32[2,32,128]{2,1,0:T(8,128)S(1)}, f32[2,32,128]{2,1,0:T(8,128)S(1)}, u32[]{:S(2)}, u32[]{:S(2)}) %collective-permute-start.9) | collective-permute-done | bytes 32800 | tf_op jit(solution)/shard_map/ppermute | solution.py:30
  (140 shorter events, 84.4 us)
Async XLA Ops:
  58.6 62.1 %collective-permute-start = (f32[5,8,1,128]{3,1,2,0:T(8,128)S(1)}, f32[5,8,1,128]{3,1,2,0:T(8,128)S(1)}, u32[]{:S(2)}, u32[]{:S(2)}) collective-permute-start(f32[5,8,1,128]{3,1,2,0:T(8,128)S(1)} %get-tuple-element.121), channel_id=1, source_target_pairs={{0,1},{1,2},{2,3},{3,4},{4,5},{5,6},{6,7},{7,8},{8,9},{9,10},{10,1... | collective-permute-start | bytes 61448 | tf_op jit(solution)/shard_map/ppermute | solution.py:19
  82.7 17.0 %copy-start.8 = (s32[32,2]{0,1:T(2,128)S(1)}, s32[32,2]{0,1:T(2,128)}, u32[]{:S(2)}) copy-start(s32[32,2]{0,1:T(2,128)} %param.18) | copy-start | bytes 772
  82.7 17.0 %copy-start.9 = (f32[32,2]{0,1:T(2,128)S(1)}, f32[32,2]{0,1:T(2,128)}, u32[]{:S(2)}) copy-start(f32[32,2]{0,1:T(2,128)} %param.19) | copy-start | bytes 772
  82.7 17.1 %copy-start.5 = (f32[4,1,16,128]{3,2,1,0:T(8,128)S(1)}, f32[4,1,16,128]{3,2,1,0:T(8,128)}, u32[]{:S(2)}) copy-start(f32[4,1,16,128]{3,2,1,0:T(8,128)} %param.16) | copy-start | bytes 98308
  82.7 35.9 %copy-start.3 = (s32[4,8,16,128]{3,2,1,0:T(8,128)S(1)}, s32[4,8,16,128]{3,2,1,0:T(8,128)}, u32[]{:S(2)}) copy-start(s32[4,8,16,128]{3,2,1,0:T(8,128)} %param.17) | copy-start | bytes 786436
  82.7 38.0 %collective-permute-start.1 = (f32[5,8,1,128]{3,1,2,0:T(8,128)S(1)}, f32[5,8,1,128]{3,1,2,0:T(8,128)S(1)}, u32[]{:S(2)}, u32[]{:S(2)}) collective-permute-start(f32[5,8,1,128]{3,1,2,0:T(8,128)S(1)} %get-tuple-element.122), channel_id=1, source_target_pairs={{1,0},{2,1},{3,2},{4,3},{5,4},{6,5},{7,6},{8,7},{9,8},{10,9},{11,1... | collective-permute-start | bytes 61448 | tf_op jit(solution)/shard_map/ppermute | solution.py:22
  87.3 1.4 copy-start
  89.4 34.7 %collective-permute-start.2 = (f32[32,8,1,128]{3,1,2,0:T(8,128)}, f32[32,8,1,128]{3,1,2,0:T(8,128)}, u32[]{:S(2)}, u32[]{:S(2)}) collective-permute-start(f32[32,8,1,128]{3,1,2,0:T(8,128)} %get-tuple-element.114), channel_id=1, source_target_pairs={{0,1},{1,2},{2,3},{3,4},{4,5},{5,6},{6,7},{7,8},{8,9},{9,10},{10,1... | collective-permute-start | bytes 393224 | tf_op jit(solution)/shard_map/ppermute | solution.py:19
  96.3 29.5 %collective-permute-start.3 = (f32[32,8,1,128]{3,1,2,0:T(8,128)}, f32[32,8,1,128]{3,1,2,0:T(8,128)}, u32[]{:S(2)}, u32[]{:S(2)}) collective-permute-start(f32[32,8,1,128]{3,1,2,0:T(8,128)} %get-tuple-element.113), channel_id=1, source_target_pairs={{1,0},{2,1},{3,2},{4,3},{5,4},{6,5},{7,6},{8,7},{9,8},{10,9},{11,1... | collective-permute-start | bytes 393224 | tf_op jit(solution)/shard_map/ppermute | solution.py:22
  120.7 4.2 %copy-start.2 = (f32[32,8,16,128]{3,2,1,0:T(8,128)S(1)}, f32[32,8,16,128]{3,2,1,0:T(8,128)}, u32[]{:S(2)}) copy-start(f32[32,8,16,128]{3,2,1,0:T(8,128)} %param.11) | copy-start | bytes 6291460
  127.1 1.6 copy-start.1
  128.7 1.2 copy-start.6
  131.5 15.3 %collective-permute-start.4 = (f32[32,8,1,128]{3,1,2,0:T(8,128)S(1)}, f32[32,8,1,128]{3,1,2,0:T(8,128)S(1)}, u32[]{:S(2)}, u32[]{:S(2)}) collective-permute-start(f32[32,8,1,128]{3,1,2,0:T(8,128)S(1)} %get-tuple-element.111), channel_id=1, source_target_pairs={{0,1},{1,2},{2,3},{3,4},{4,5},{5,6},{6,7},{7,8},{8,9},{9,10},{10,1... | collective-permute-start | bytes 393224 | tf_op jit(solution)/shard_map/ppermute | solution.py:19
  144.6 9.6 %collective-permute-start.5 = (f32[32,8,1,128]{3,1,2,0:T(8,128)S(1)}, f32[32,8,1,128]{3,1,2,0:T(8,128)S(1)}, u32[]{:S(2)}, u32[]{:S(2)}) collective-permute-start(f32[32,8,1,128]{3,1,2,0:T(8,128)S(1)} %get-tuple-element.112), channel_id=1, source_target_pairs={{1,0},{2,1},{3,2},{4,3},{5,4},{6,5},{7,6},{8,7},{9,8},{10,9},{11,1... | collective-permute-start | bytes 393224 | tf_op jit(solution)/shard_map/ppermute | solution.py:22
  157.4 4.8 %collective-permute-start.6 = (f32[32,8,1,128]{3,1,2,0:T(8,128)S(1)}, f32[32,8,1,128]{3,1,2,0:T(8,128)S(1)}, u32[]{:S(2)}, u32[]{:S(2)}) collective-permute-start(f32[32,8,1,128]{3,1,2,0:T(8,128)S(1)} %get-tuple-element.109), channel_id=1, source_target_pairs={{0,1},{1,2},{2,3},{3,4},{4,5},{5,6},{6,7},{7,8},{8,9},{9,10},{10,1... | collective-permute-start | bytes 393224 | tf_op jit(solution)/shard_map/ppermute | solution.py:19
  159.4 9.6 %collective-permute-start.7 = (f32[32,8,1,128]{3,1,2,0:T(8,128)S(1)}, f32[32,8,1,128]{3,1,2,0:T(8,128)S(1)}, u32[]{:S(2)}, u32[]{:S(2)}) collective-permute-start(f32[32,8,1,128]{3,1,2,0:T(8,128)S(1)} %get-tuple-element.110), channel_id=1, source_target_pairs={{1,0},{2,1},{3,2},{4,3},{5,4},{6,5},{7,6},{8,7},{9,8},{10,9},{11,1... | collective-permute-start | bytes 393224 | tf_op jit(solution)/shard_map/ppermute | solution.py:22
  169.9 0.6 copy-start.7
  174.7 4.9 %copy-start.4 = (f32[64,640]{1,0:T(8,128)S(1)}, f32[64,640]{1,0:T(8,128)}, u32[]{:S(2)}) copy-start(f32[64,640]{1,0:T(8,128)} %custom-call) | copy-start | bytes 491524
  273.0 10.2 %collective-permute-start.10 = (f32[2,32,128]{2,1,0:T(8,128)S(1)}, f32[2,32,128]{2,1,0:T(8,128)S(1)}, u32[]{:S(2)}, u32[]{:S(2)}) collective-permute-start(f32[2,32,128]{2,1,0:T(8,128)S(1)} %get-tuple-element.125), channel_id=1, source_target_pairs={{0,1},{1,2},{2,3},{3,4},{4,5},{5,6},{6,7},{7,8},{8,9},{9,10},{10,1... | collective-permute-start | bytes 98312 | tf_op jit(solution)/shard_map/ppermute | solution.py:30
  274.9 8.3 %collective-permute-start.11 = (f32[2,32,128]{2,1,0:T(8,128)S(1)}, f32[2,32,128]{2,1,0:T(8,128)S(1)}, u32[]{:S(2)}, u32[]{:S(2)}) collective-permute-start(f32[2,32,128]{2,1,0:T(8,128)S(1)} %get-tuple-element.124), channel_id=1, source_target_pairs={{0,2},{1,3},{2,4},{3,5},{4,6},{5,7},{6,8},{7,9},{8,10},{9,11},{10,... | collective-permute-start | bytes 98312 | tf_op jit(solution)/shard_map/ppermute | solution.py:30
  276.9 8.0 %collective-permute-start.8 = (f32[2,32,128]{2,1,0:T(8,128)S(1)}, f32[2,32,128]{2,1,0:T(8,128)S(1)}, u32[]{:S(2)}, u32[]{:S(2)}) collective-permute-start(f32[2,32,128]{2,1,0:T(8,128)S(1)} %get-tuple-element.126), channel_id=1, source_target_pairs={{2,0},{3,1},{4,2},{5,3},{6,4},{7,5},{8,6},{9,7},{10,8},{11,9},{12,... | collective-permute-start | bytes 98312 | tf_op jit(solution)/shard_map/ppermute | solution.py:30
  280.2 8.6 %collective-permute-start.9 = (f32[2,32,128]{2,1,0:T(8,128)S(1)}, f32[2,32,128]{2,1,0:T(8,128)S(1)}, u32[]{:S(2)}, u32[]{:S(2)}) collective-permute-start(f32[2,32,128]{2,1,0:T(8,128)S(1)} %get-tuple-element.123), channel_id=1, source_target_pairs={{1,0},{2,1},{3,2},{4,3},{5,4},{6,5},{7,6},{8,7},{9,8},{10,9},{11,1... | collective-permute-start | bytes 98312 | tf_op jit(solution)/shard_map/ppermute | solution.py:30
where the time goes:
time: 292 us; the launch traced here: 289 us
  blocking collectives  76.4 us (26%)
  starting transfers between devices  64.7 us (22%)
  local copies, waits for them, and re-layouts  58.8 us (20%)
  matrix products  48.9 us (17%)
  other arithmetic  19.7 us (7%)
  waiting for transfers between devices  19.7 us (7%)
    dot_general x16, matrix products, accumulate(): jnp.dot(block, matrix, precision=lax.Precision.HIGHEST, preferred_element...  48.9 us
    ppermute x4, starting transfers between devices, extended(): lax.ppermute(lax.slice_in_dim(block, block.shape[dim] - width, None, axis...  46 us
    dynamic_slice x16, local copies, waits for them, and re-layouts, shards(): lax.scan(accumulate, jnp.zeros((2 * obs_dev, span), jnp.float32), (sens_r...  29.1 us
    all_gather x1, blocking collectives, shards(): lax.all_gather(conductance, 'obs', axis=1, tiled=True)  20.3 us
    all_gather x1, blocking collectives, shards(): lax.all_gather(krig_weight, 'obs', axis=1, tiled=True)  18.8 us
    all_gather x1, blocking collectives, shards(): lax.all_gather(storage, 'obs', axis=0, tiled=True)  18.8 us
    all_gather x1, blocking collectives, shards(): lax.all_gather(head, 'obs', axis=0, tiled=True)  18.5 us
    slice x16, local copies, waits for them, and re-layouts, accumulate(): rel_block[member][:, None] == columns[None, :]  14.3 us
  transfers between devices with their start and end apart: 12, of which 4 were waited for; matrix products, arithmetic and copies ran while one was open for 4% of the time, Pallas kernels for 0%

commit v1 on v0

v1 whole, which is shorter than its diff:
```python
import jax
import jax.numpy as jnp
from jax import lax
from jax.experimental import pallas as pl
from jax.experimental.pallas import tpu as pltpu
from jax.sharding import PartitionSpec as P

NK = 4
RADIUS = 2
P_DEV = 128
OMEGA = 0.8
LAY = 8
OBS = 32
TX = 16
TY = 128
HALO = 3
SPAN = (2 * RADIUS + 1) * P_DEV
OFF = 8
EXT = 32
KX = 4

F32 = jnp.float32
BF16 = jnp.bfloat16
I16 = jnp.int16
VMEM = pl.BlockSpec(memory_space=pltpu.VMEM)
SMEM = pl.BlockSpec(memory_space=pltpu.SMEM)


def edges_kernel(adj_ref, low_ref, high_ref):
    stride = LAY * TX

    def body(layer, carry):
        for j in range(HALO):
            low_ref[layer, j] = adj_ref[pl.ds(layer * TX + j, OBS, stride=stride), :]
            high_ref[layer, j] = adj_ref[
                pl.ds(layer * TX + TX - HALO + j, OBS, stride=stride), :
            ]
        return carry

    lax.fori_loop(0, LAY, body, 0)


def medium_edges_kernel(med_ref, open_ref, low_ref, high_ref):
    for layer in range(LAY):
        for field in range(5):
            if field < 4:
                tile = med_ref[layer, field]
            else:
                tile = open_ref[layer].astype(F32)
            low_ref[layer, pl.ds(field * HALO, HALO), :] = tile[:HALO]
            high_ref[layer, pl.ds(field * HALO, HALO), :] = tile[TX - HALO :]
        low_ref[layer, pl.ds(15, 1), :] = jnp.zeros((1, TY), F32)
        high_ref[layer, pl.ds(15, 1), :] = jnp.zeros((1, TY), F32)


def stencil_kernel(
    tile_ref,
    adj_ref,
    low_ref,
    high_ref,
    med_ref,
    open_ref,
    med_low_ref,
    med_high_ref,
    cell_ref,
    weight_ref,
    out_ref,
    ext_ref,
    coef_ref,
    grad_ref,
    start_ref,
    one_ref,
    two_ref,
):
    tile = tile_ref[0, 0]
    n_tiles = tile_ref[0, 1]
    whole_x = n_tiles * TX

    row = lax.broadcasted_iota(jnp.int32, (EXT, TY), 0)
    lane = lax.broadcasted_iota(jnp.int32, (EXT, TY), 1)
    global_x = tile * TX + row - OFF
    live = (global_x >= 0) & (global_x < whole_x)
    live_next = (global_x + 1 >= 0) & (global_x + 1 < whole_x)
    both = jnp.where(live & live_next, 1.0, 0.0).astype(F32)
    for layer in range(LAY):
        for field in range(5):
            fill = jnp.ones((OFF, TY), F32)
            ext_ref[field, layer, pl.ds(0, OFF), :] = fill
            ext_ref[field, layer, pl.ds(OFF + TX, OFF), :] = fill
            own = med_ref[layer, field] if field < 4 else open_ref[layer].astype(F32)
            ext_ref[field, layer, pl.ds(OFF, TX), :] = own
            ext_ref[field, layer, pl.ds(OFF - HALO, HALO), :] = med_low_ref[
                layer, pl.ds(field * HALO, HALO), :
            ]
            ext_ref[field, layer, pl.ds(OFF + TX, HALO), :] = med_high_ref[
                layer, pl.ds(field * HALO, HALO), :
            ]

    stride = LAY * TX

    def gather(layer, carry):
        for j in range(HALO):
            start_ref[layer, j] = low_ref[layer, j]
            start_ref[layer, HALO + TX + j] = high_ref[layer, j]
        for x in range(TX):
            start_ref[layer, HALO + x] = adj_ref[pl.ds(layer * TX + x, OBS, stride=stride), :]
        return carry

    lax.fori_loop(0, LAY, gather, 0)

    def medium(field, layer):
        value = ext_ref[field, layer]
        if field < 3:
            return jnp.where(live, value, 1.0)
        return value

    def below(value):
        return pltpu.roll(value, 1, 0)

    def above(value):
        return pltpu.roll(value, EXT - 1, 0)

    def west(value):
        return pltpu.roll(value, 1, 1)

    def east(value):
        return pltpu.roll(value, TY - 1, 1)

    has_west = jnp.where(lane > 0, 1.0, 0.0).astype(F32)
    has_east = jnp.where(lane < TY - 1, 1.0, 0.0).astype(F32)
    before = below(both)

    def pair(mine, other):
        inv = 1.0 / (mine + other)
        face = 2.0 * mine * other * inv
        return face, face * other * inv

    for layer in range(LAY):
        k = medium(0, layer)
        kv = medium(1, layer)
        head = medium(3, layer)
        fxm, gxm = pair(k, below(k))
        fxp, gxp = pair(k, above(k))
        fym, gym = pair(k, west(k))
        fyp, gyp = pair(k, east(k))
        fxm = fxm * before
        fxp = fxp * both
        fym = fym * has_west
        fyp = fyp * has_east
        diag = medium(2, layer) + fxm + fxp + fym + fyp
        zero = jnp.zeros((EXT, TY), F32)
        fzm = fzp = gzm = gzp = zero
        if layer > 0:
            fzm, gzm = pair(kv, medium(1, layer - 1))
            gate = ext_ref[4, layer - 1]
            fzm = fzm * gate
            gzm = gzm * gate * (head - medium(3, layer - 1))
        if layer < LAY - 1:
            fzp, gzp = pair(kv, medium(1, layer + 1))
            gate = ext_ref[4, layer]
            fzp = fzp * gate
            gzp = gzp * gate * (head - medium(3, layer + 1))
        diag = diag + fzm + fzp
        scale = OMEGA / diag
        for n, value in enumerate((fxm, fxp, fym, fyp, fzm, fzp)):
            coef_ref[n, layer] = value * scale
        coef_ref[6, layer] = scale
        grad_ref[0, layer] = gxm * before * (head - below(head))
        grad_ref[1, layer] = gxp * both * (head - above(head))
        grad_ref[2, layer] = gym * has_west * (head - west(head))
        grad_ref[3, layer] = gyp * has_east * (head - east(head))
        grad_ref[4, layer] = gzm
        grad_ref[5, layer] = gzp

    lanes = lax.broadcasted_iota(jnp.int32, (OBS, TY), 1)
    target = [
        jnp.broadcast_to(cell_ref[:, pl.ds(m, 1)], (OBS, TY)) - lanes for m in range(2)
    ]
    amount = [jnp.broadcast_to(weight_ref[:, pl.ds(m, 1)], (OBS, TY)) for m in range(2)]

    def rows(ref, n, layer, x):
        return jnp.broadcast_to(ref[n, layer, pl.ds(x + OFF, 1), :], (OBS, TY))

    def sweep(src_ref, dst_ref, margin):
        def body(layer, carry):
            down = jnp.maximum(layer - 1, 0)
            up = jnp.minimum(layer + 1, LAY - 1)
            for x in range(-margin, TX + margin):
                j = x + margin + 1
                mid = src_ref[layer, j]
                base = (layer * whole_x + tile * TX + x) * TY
                source = jnp.where(target[0] == base, amount[0], 0.0) + jnp.where(
                    target[1] == base, amount[1], 0.0
                )
                value = (1.0 - OMEGA) * mid + rows(coef_ref, 6, layer, x) * source
                value += rows(coef_ref, 0, layer, x) * src_ref[layer, j - 1]
                value += rows(coef_ref, 1, layer, x) * src_ref[layer, j + 1]
                value += rows(coef_ref, 2, layer, x) * pltpu.roll(mid, 1, 1)
                value += rows(coef_ref, 3, layer, x) * pltpu.roll(mid, TY - 1, 1)
                value += rows(coef_ref, 4, layer, x) * src_ref[down, j]
                value += rows(coef_ref, 5, layer, x) * src_ref[up, j]
                dst_ref[layer, j - 1] = value
            return carry

        lax.fori_loop(0, LAY, body, 0)

    sweep(start_ref, one_ref, 2)
    sweep(one_ref, two_ref, 1)

    def split(value):
        high = value.astype(BF16)
        return high, (value - high.astype(F32)).astype(BF16)

    def sense(layer, carry):
        down = jnp.maximum(layer - 1, 0)
        up = jnp.minimum(layer + 1, LAY - 1)
        for x in range(TX):
            j = x + 1
            mid = two_ref[layer, j]
            horiz = rows(grad_ref, 0, layer, x) * (two_ref[layer, j - 1] - mid)
            horiz += rows(grad_ref, 1, layer, x) * (two_ref[layer, j + 1] - mid)
            horiz += rows(grad_ref, 2, layer, x) * (pltpu.roll(mid, 1, 1) - mid)
            horiz += rows(grad_ref, 3, layer, x) * (pltpu.roll(mid, TY - 1, 1) - mid)
            vert = rows(grad_ref, 4, layer, x) * (two_ref[down, j] - mid)
            vert += rows(grad_ref, 5, layer, x) * (two_ref[up, j] - mid)
            chunk = layer * (TX // 2) + x // 2
            half = pl.ds((x % 2) * TY, TY)
            for field, value in enumerate((horiz, vert)):
                high, low = split(value)
                out_ref[chunk, pl.ds(field * OBS, OBS), half] = high
                out_ref[chunk, pl.ds((2 + field) * OBS, OBS), half] = low
        return carry

    lax.fori_loop(0, LAY, sense, 0)


def krig_kernel(tile_ref, sens_ref, pilot_ref, weight_ref, *rest):
    outs = rest[:5]
    index_ref, share_ref, first_ref, second_ref, total_ref = rest[5:]
    base = (tile_ref[0, 0] - RADIUS) * P_DEV
    chunks = LAY * TX // KX

    for layer in range(LAY):
        index = [pilot_ref[k, layer] - base for k in range(NK)]
        share = [weight_ref[layer, k] for k in range(NK)]
        for k in range(1, NK):
            for j in range(k):
                same = index[j] == index[k]
                share[j] = share[j] + jnp.where(same, share[k], 0.0)
                index[k] = jnp.where(same, -1, index[k])
        for k in range(NK):
            index_ref[pl.ds(layer * TX, TX), k, :] = index[k]
            share_ref[pl.ds(layer * TX, TX), k, :] = share[k]

    iota = lax.broadcasted_iota(I16, (16, TY), 0)

    def build(chunk, matrix_ref):
        for s in range(KX):
            row = chunk * KX + s
            index = []
            high = []
            low = []
            for k in range(NK):
                index.append(
                    jnp.broadcast_to(index_ref[row, pl.ds(k, 1), :], (16, TY)).astype(I16)
                )
                share = jnp.broadcast_to(share_ref[row, pl.ds(k, 1), :], (16, TY))
                top = share.astype(BF16)
                high.append(top)
                low.append((share - top.astype(F32)).astype(BF16))
            for i in range(SPAN // 16):
                pilot = iota + I16(16 * i)
                upper = jnp.zeros((16, TY), BF16)
                lower = jnp.zeros((16, TY), BF16)
                for k in range(NK):
                    hit = index[k] == pilot
                    upper = jnp.where(hit, high[k], upper)
                    lower = jnp.where(hit, low[k], lower)
                matrix_ref[pl.ds(16 * i, 16), pl.ds(TY * s, TY)] = upper
                matrix_ref[pl.ds(SPAN + 16 * i, 16), pl.ds(TY * s, TY)] = lower

    def add(chunk, matrix_ref):
        sens = jnp.concatenate([sens_ref[chunk * (KX // 2) + q] for q in range(KX // 2)], axis=1)
        total_ref[...] += lax.dot_general(
            matrix_ref[...], sens, (((1,), (1,)), ((), ())), preferred_element_type=F32
        )

    total_ref[...] = jnp.zeros_like(total_ref)
    build(0, first_ref)

    def body(i, carry):
        add(2 * i, first_ref)
        build(2 * i + 1, second_ref)
        add(2 * i + 1, second_ref)
        build(jnp.minimum(2 * i + 2, chunks - 1), first_ref)
        return carry

    lax.fori_loop(0, chunks // 2, body, 0)
    for o in range(5):
        piece = total_ref[pl.ds(o * P_DEV, P_DEV), :] + total_ref[pl.ds(SPAN + o * P_DEV, P_DEV), :]
        piece = piece.T
        outs[o][...] = piece[: 2 * OBS] + piece[2 * OBS :]


def shift(block, axis, by):
    count = lax.axis_size(axis)
    pairs = [(i, i + by) for i in range(count) if 0 <= i + by < count]
    return lax.ppermute(block, axis, pairs)


def gathered(block, axis):
    count = lax.axis_size(axis)
    return lax.all_to_all(
        jnp.broadcast_to(block[None], (count,) + block.shape), axis, 0, 0, tiled=False
    )


def shards(
    adjoint_start,
    conductance,
    storage,
    head,
    layer_open,
    krig_weight,
    krig_pilot,
    obs_cell,
    obs_weight,
):
    sds = jax.ShapeDtypeStruct
    limit = pltpu.CompilerParams(vmem_limit_bytes=52 * 2**20)
    tile = jnp.stack(
        [lax.axis_index("grid"), jnp.int32(lax.axis_size("grid"))]
    ).reshape(1, 2)

    own = jnp.concatenate([conductance[:, 0], storage, head], axis=0)
    medium = gathered(own, "obs")

    flat_adjoint = adjoint_start.reshape(OBS * LAY * TX, TY)
    edge = sds((LAY, HALO, OBS, TY), F32)
    low, high = pl.pallas_call(
        edges_kernel, out_shape=(edge, edge), in_specs=[VMEM], out_specs=(VMEM, VMEM)
    )(flat_adjoint)
    from_low = shift(high, "grid", 1)
    from_high = shift(low, "grid", -1)

    share = gathered(krig_weight[:, 0], "obs")

    edge = sds((LAY, 16, TY), F32)
    med_low, med_high = pl.pallas_call(
        medium_edges_kernel,
        out_shape=(edge, edge),
        in_specs=[VMEM, VMEM],
        out_specs=(VMEM, VMEM),
    )(medium, layer_open)
    med_from_low = shift(med_high, "grid", 1)
    med_from_high = shift(med_low, "grid", -1)

    sens = pl.pallas_call(
        stencil_kernel,
        out_shape=sds((LAY * TX // 2, 4 * OBS, 2 * TY), BF16),
        in_specs=[SMEM] + [VMEM] * 9,
        out_specs=VMEM,
        scratch_shapes=[
            pltpu.VMEM((5, LAY, EXT, TY), F32),
            pltpu.VMEM((7, LAY, EXT, TY), F32),
            pltpu.VMEM((6, LAY, EXT, TY), F32),
            pltpu.VMEM((LAY, TX + 6, OBS, TY), F32),
            pltpu.VMEM((LAY, TX + 4, OBS, TY), F32),
            pltpu.VMEM((LAY, TX + 2, OBS, TY), F32),
        ],
        compiler_params=limit,
    )(
        tile,
        flat_adjoint,
        from_low,
        from_high,
        medium,
        layer_open,
        med_from_low,
        med_from_high,
        obs_cell,
        obs_weight,
    )

    piece = sds((2 * OBS, P_DEV), F32)
    pieces = pl.pallas_call(
        krig_kernel,
        out_shape=[piece] * 5,
        in_specs=[SMEM] + [VMEM] * 3,
        out_specs=[VMEM] * 5,
        scratch_shapes=[
            pltpu.VMEM((LAY * TX, NK, TY), jnp.int32),
            pltpu.VMEM((LAY * TX, NK, TY), F32),
            pltpu.VMEM((2 * SPAN, KX * TY), BF16),
            pltpu.VMEM((2 * SPAN, KX * TY), BF16),
            pltpu.VMEM((2 * SPAN, 4 * OBS), F32),
        ],
        compiler_params=limit,
    )(tile, sens, krig_pilot, share)

    owned = pieces[RADIUS]
    for offset in (0, 4, 1, 3):
        owned = owned + shift(pieces[offset], "grid", offset - RADIUS)
    return owned.reshape(2, OBS, P_DEV)


def solution(mesh):
    return jax.shard_map(
        shards,
        mesh=mesh,
        in_specs=(
            P("obs", None, "grid", None),
            P(None, "obs", "grid", None),
            P("obs", "grid", None),
            P("obs", "grid", None),
            P(None, "grid", None),
            P(None, "obs", "grid", None),
            P(None, None, "grid", None),
            P("obs", None),
            P("obs", None),
        ),
        out_specs=P(None, "obs", "grid"),
        check_vma=False,
    )
```

time: 292 us -> 111 us (0.38)
  the two profiles are of different devices: /device:TPU:199 before, /device:TPU:264 now
where the time goes in v1:
time: 111 us; the launch traced here: 110 us
  starting transfers between devices  40.1 us (36%)
  Pallas kernels  38.1 us (34%)
  blocking collectives  17.9 us (16%)
  waiting for transfers between devices  8.73 us (8%)
  local copies, waits for them, and re-layouts  3.98 us (4%)
  other arithmetic  1.49 us (1%)
    ppermute x8, starting transfers between devices, shift(): return lax.ppermute(block, axis, pairs)  35.3 us
    pallas_call x1, Pallas kernels, shards(): pl.pallas_call(krig_kernel, out_shape=[piece] * 5, in_specs=[SMEM] + [VME...  22.6 us
    all_to_all x1, blocking collectives, gathered(): lax.all_to_all(jnp.broadcast_to(block[None], (count,) + block.shape), axi...  17.9 us
    pallas_call x1, Pallas kernels, shards(): pl.pallas_call(stencil_kernel, out_shape=sds((LAY * TX // 2, 4 * OBS, 2 *...  10.9 us
    ppermute x8, waiting for transfers between devices, shift(): return lax.ppermute(block, axis, pairs)  8.72 us
    all_to_all x1, starting transfers between devices, gathered(): lax.all_to_all(jnp.broadcast_to(block[None], (count,) + block.shape), axi...  4.77 us
    pallas_call x1, Pallas kernels, shards(): pl.pallas_call(edges_kernel, out_shape=(edge, edge), in_specs=[VMEM], out...  2.99 us
    unnamed x8, local copies, waits for them, and re-layouts  2.48 us
  transfers between devices with their start and end apart: 9, of which 3 were waited for; matrix products, arithmetic and copies ran while one was open for 1% of the time, Pallas kernels for 14%

profile of v1, /device:TPU:264, one launch (start us, length us, event | category | flops | bytes accessed | tf_op | source)
XLA Modules:
  0.0 110.4 jit_solution(175394476910088015)
XLA Ops:
  0.0 0.8 pad_maximum_fusion
  0.8 17.9 %all_to_all.10.med_ref = f32[8,4,16,128]{3,2,1,0:T(8,128)} all-to-all(f32[8,4,16,128]{3,2,1,0:T(8,128)S(1)} %broadcast_in_dim.6), channel_id=1, replica_groups=mesh['obs'=8,'grid'=64] {'obs'}, dimensions={0} | all-to-all | bytes 524288 | tf_op jit(solution)/shard_map/all_to_all | solution.py:313
  18.7 1.5 %broadcast_in_dim.15 = f32[8,4,16,128]{3,2,1,0:T(8,128)} broadcast(f32[4,16,128]{2,1,0:T(8,128)} %bitcast.9), dimensions={1,2,3} | broadcast | bytes 294912 | tf_op jit(solution)/shard_map/broadcast_in_dim | solution.py:314
  20.2 4.8 %all-to-all-start.1 = ((f32[8,4,16,128]{3,2,1,0:T(8,128)}), f32[8,4,16,128]{3,2,1,0:T(8,128)S(1)}, u32[]{:S(2)}, u32[]{:S(2)}) async-start(f32[8,4,16,128]{3,2,1,0:T(8,128)} %broadcast_in_dim.15), calls=%async_computation.1 | async-start | bytes 524288 | tf_op jit(solution)/shard_map/all_to_all | solution.py:313
  24.9 3.0 %shard_map.91 = (f32[8,3,32,128]{3,2,1,0:T(8,128)}, f32[8,3,32,128]{3,2,1,0:T(8,128)}) custom-call(f32[4096,128]{1,0:T(8,128)} %bitcast.7), custom_call_target="tpu_custom_call" | custom-call | tf_op jit(solution)/shard_map/pallas_call | solution.py:340
  27.9 2.0 %collective-permute-start = (f32[8,3,32,128]{3,2,1,0:T(8,128)}, f32[8,3,32,128]{3,2,1,0:T(8,128)S(1)}, u32[]{:S(2)}, u32[]{:S(2)}) collective-permute-start(f32[8,3,32,128]{3,2,1,0:T(8,128)} %get-tuple-element.14), channel_id=1, source_target_pairs={{0,1},{1,2},{2,3},{3,4},{4,5},{5,6},{6,7},{7,8},{8,9},{9,10},{10,1... | collective-permute-start | bytes 1179656 | tf_op jit(solution)/shard_map/ppermute | solution.py:308
  30.0 7.0 %collective-permute-start.1 = (f32[8,3,32,128]{3,2,1,0:T(8,128)}, f32[8,3,32,128]{3,2,1,0:T(8,128)S(1)}, u32[]{:S(2)}, u32[]{:S(2)}) collective-permute-start(f32[8,3,32,128]{3,2,1,0:T(8,128)} %get-tuple-element.15), channel_id=1, source_target_pairs={{1,0},{2,1},{3,2},{4,3},{5,4},{6,5},{7,6},{8,7},{9,8},{10,9},{11,1... | collective-permute-start | bytes 1179656 | tf_op jit(solution)/shard_map/ppermute | solution.py:308
  36.9 0.8 copy.10.cell_ref
  37.7 0.8 copy.11.weight_ref
  38.5 1.6 %shard_map.92 = (f32[8,16,128]{2,1,0:T(8,128)}, f32[8,16,128]{2,1,0:T(8,128)}) custom-call(f32[8,4,16,128]{3,2,1,0:T(8,128)} %all_to_all.10.med_ref, s32[8,16,128]{2,1,0:T(8,128)} %open_ref.3), custom_call_target="tpu_custom_call" | custom-call | tf_op jit(solution)/shard_map/pallas_call | solution.py:349
  40.1 1.9 %collective-permute-start.2 = (f32[8,16,128]{2,1,0:T(8,128)}, f32[8,16,128]{2,1,0:T(8,128)S(1)}, u32[]{:S(2)}, u32[]{:S(2)}) collective-permute-start(f32[8,16,128]{2,1,0:T(8,128)} %get-tuple-element.16), channel_id=1, source_target_pairs={{0,1},{1,2},{2,3},{3,4},{4,5},{5,6},{6,7},{7,8},{8,9},{9,10},{10,1... | collective-permute-start | bytes 196616 | tf_op jit(solution)/shard_map/ppermute | solution.py:308
  42.0 7.0 %collective-permute-start.3 = (f32[8,16,128]{2,1,0:T(8,128)}, f32[8,16,128]{2,1,0:T(8,128)S(1)}, u32[]{:S(2)}, u32[]{:S(2)}) collective-permute-start(f32[8,16,128]{2,1,0:T(8,128)} %get-tuple-element.17), channel_id=1, source_target_pairs={{1,0},{2,1},{3,2},{4,3},{5,4},{6,5},{7,6},{8,7},{9,8},{10,9},{11,1... | collective-permute-start | bytes 196616 | tf_op jit(solution)/shard_map/ppermute | solution.py:308
  49.0 0.1 add_bitcast_fusion.tile_ref
  49.1 0.0 collective-permute-done.low_ref
  49.1 0.0 collective-permute-done.1.high_ref
  49.1 0.1 collective-permute-done.2.med_low_ref
  49.2 2.0 %collective-permute-done.3.med_high_ref = f32[8,16,128]{2,1,0:T(8,128)S(1)} collective-permute-done((f32[8,16,128]{2,1,0:T(8,128)}, f32[8,16,128]{2,1,0:T(8,128)S(1)}, u32[]{:S(2)}, u32[]{:S(2)}) %collective-permute-start.3) | collective-permute-done | bytes 65568 | tf_op jit(solution)/shard_map/ppermute | solution.py:308
  51.2 0.0 copy-done.1
  51.2 0.9 copy-done
  52.1 10.9 %shard_map.93.sens_ref = bf16[64,128,256]{2,1,0:T(8,128)(2,1)} custom-call(s32[1,2]{1,0:T(1,128)S(1)} %add_bitcast_fusion.tile_ref, f32[4096,128]{1,0:T(8,128)} %bitcast.8, f32[8,3,32,128]{3,2,1,0:T(8,128)S(1)} %collective-permute-done.low_ref, f32[8,3,32,128]{3,2,1,0:T(8,128)S(1)} %collective-permute-done.1.high_ref, f32[8,4,16,128]{3,2,1,0:T(8,128)S(1)} %copy-done, ...), custom_call_target="tpu_custom_call" | custom-call | tf_op jit(solution)/shard_map/pallas_call | solution.py:358
  63.0 0.0 all-to-all-done.1.weight_ref
  63.0 0.0 copy-done.2
  63.0 22.6 %shard_map.94 = (f32[64,128]{1,0:T(8,128)S(1)}, f32[64,128]{1,0:T(8,128)S(1)}, f32[64,128]{1,0:T(8,128)S(1)}, f32[64,128]{1,0:T(8,128)S(1)}, f32[64,128]{1,0:T(8,128)S(1)}) custom-call(s32[1,2]{1,0:T(1,128)S(1)} %add_bitcast_fusion.tile_ref, bf16[64,128,256]{2,1,0:T(8,128)(2,1)} %shard_map.93.sens_ref, s32[4,8,16,128]{3,2,1,0:T(8,128)S(1)} %copy-done.2, ...), custom_call_target="tpu_custom_call" | custom-call | tf_op jit(solution)/shard_map/pallas_call | solution.py:386
  85.7 1.9 %collective-permute-start.4 = (f32[64,128]{1,0:T(8,128)S(1)}, f32[64,128]{1,0:T(8,128)S(1)}, u32[]{:S(2)}, u32[]{:S(2)}) collective-permute-start(f32[64,128]{1,0:T(8,128)S(1)} %get-tuple-element.19), channel_id=1, source_target_pairs={{2,0},{3,1},{4,2},{5,3},{6,4},{7,5},{8,6},{9,7},{10,8},{11,9},{12,... | collective-permute-start | bytes 98312 | tf_op jit(solution)/shard_map/ppermute | solution.py:308
  87.6 3.9 %collective-permute-start.5 = (f32[64,128]{1,0:T(8,128)S(1)}, f32[64,128]{1,0:T(8,128)S(1)}, u32[]{:S(2)}, u32[]{:S(2)}) collective-permute-start(f32[64,128]{1,0:T(8,128)S(1)} %get-tuple-element.20), channel_id=1, source_target_pairs={{0,2},{1,3},{2,4},{3,5},{4,6},{5,7},{6,8},{7,9},{8,10},{9,11},{10,... | collective-permute-start | bytes 98312 | tf_op jit(solution)/shard_map/ppermute | solution.py:308
  91.5 9.7 %collective-permute-start.6 = (f32[64,128]{1,0:T(8,128)S(1)}, f32[64,128]{1,0:T(8,128)S(1)}, u32[]{:S(2)}, u32[]{:S(2)}) collective-permute-start(f32[64,128]{1,0:T(8,128)S(1)} %get-tuple-element.21), channel_id=1, source_target_pairs={{1,0},{2,1},{3,2},{4,3},{5,4},{6,5},{7,6},{8,7},{9,8},{10,9},{11,1... | collective-permute-start | bytes 98312 | tf_op jit(solution)/shard_map/ppermute | solution.py:308
  101.2 1.9 %collective-permute-start.7 = (f32[64,128]{1,0:T(8,128)S(1)}, f32[64,128]{1,0:T(8,128)S(1)}, u32[]{:S(2)}, u32[]{:S(2)}) collective-permute-start(f32[64,128]{1,0:T(8,128)S(1)} %get-tuple-element.22), channel_id=1, source_target_pairs={{0,1},{1,2},{2,3},{3,4},{4,5},{5,6},{6,7},{7,8},{8,9},{9,10},{10,1... | collective-permute-start | bytes 98312 | tf_op jit(solution)/shard_map/ppermute | solution.py:308
  103.1 0.0 collective-permute-done.4
  103.1 0.0 collective-permute-done.5
  103.2 0.0 collective-permute-done.6
  103.2 6.6 %collective-permute-done.7 = f32[64,128]{1,0:T(8,128)S(1)} collective-permute-done((f32[64,128]{1,0:T(8,128)S(1)}, f32[64,128]{1,0:T(8,128)S(1)}, u32[]{:S(2)}, u32[]{:S(2)}) %collective-permute-start.7) | collective-permute-done | bytes 32800 | tf_op jit(solution)/shard_map/ppermute | solution.py:308
  109.8 0.6 add_add_fusion
  (4 shorter events, 0.0 us)
Async XLA Ops:
  0.0 51.2 %copy-start.1 = (s32[8,16,128]{2,1,0:T(8,128)S(1)}, s32[8,16,128]{2,1,0:T(8,128)}, u32[]{:S(2)}) copy-start(s32[8,16,128]{2,1,0:T(8,128)} %open_ref.3) | copy-start | bytes 196612
  20.2 42.9 %all-to-all-start.1 = ((f32[8,4,16,128]{3,2,1,0:T(8,128)}), f32[8,4,16,128]{3,2,1,0:T(8,128)S(1)}, u32[]{:S(2)}, u32[]{:S(2)}) async-start(f32[8,4,16,128]{3,2,1,0:T(8,128)} %broadcast_in_dim.15), calls=%async_computation.1 | async-start | bytes 524288 | tf_op jit(solution)/shard_map/all_to_all | solution.py:313
  27.9 35.1 %copy-start.2 = (s32[4,8,16,128]{3,2,1,0:T(8,128)S(1)}, s32[4,8,16,128]{3,2,1,0:T(8,128)}, u32[]{:S(2)}) copy-start(s32[4,8,16,128]{3,2,1,0:T(8,128)} %pilot_ref.1) | copy-start | bytes 786436
  27.9 21.1 %collective-permute-start = (f32[8,3,32,128]{3,2,1,0:T(8,128)}, f32[8,3,32,128]{3,2,1,0:T(8,128)S(1)}, u32[]{:S(2)}, u32[]{:S(2)}) collective-permute-start(f32[8,3,32,128]{3,2,1,0:T(8,128)} %get-tuple-element.14), channel_id=1, source_target_pairs={{0,1},{1,2},{2,3},{3,4},{4,5},{5,6},{6,7},{7,8},{8,9},{9,10},{10,1... | collective-permute-start | bytes 1179656 | tf_op jit(solution)/shard_map/ppermute | solution.py:308
  30.0 19.1 %collective-permute-start.1 = (f32[8,3,32,128]{3,2,1,0:T(8,128)}, f32[8,3,32,128]{3,2,1,0:T(8,128)S(1)}, u32[]{:S(2)}, u32[]{:S(2)}) collective-permute-start(f32[8,3,32,128]{3,2,1,0:T(8,128)} %get-tuple-element.15), channel_id=1, source_target_pairs={{1,0},{2,1},{3,2},{4,3},{5,4},{6,5},{7,6},{8,7},{9,8},{10,9},{11,1... | collective-permute-start | bytes 1179656 | tf_op jit(solution)/shard_map/ppermute | solution.py:308
  40.1 9.1 %collective-permute-start.2 = (f32[8,16,128]{2,1,0:T(8,128)}, f32[8,16,128]{2,1,0:T(8,128)S(1)}, u32[]{:S(2)}, u32[]{:S(2)}) collective-permute-start(f32[8,16,128]{2,1,0:T(8,128)} %get-tuple-element.16), channel_id=1, source_target_pairs={{0,1},{1,2},{2,3},{3,4},{4,5},{5,6},{6,7},{7,8},{8,9},{9,10},{10,1... | collective-permute-start | bytes 196616 | tf_op jit(solution)/shard_map/ppermute | solution.py:308
  42.0 9.2 %collective-permute-start.3 = (f32[8,16,128]{2,1,0:T(8,128)}, f32[8,16,128]{2,1,0:T(8,128)S(1)}, u32[]{:S(2)}, u32[]{:S(2)}) collective-permute-start(f32[8,16,128]{2,1,0:T(8,128)} %get-tuple-element.17), channel_id=1, source_target_pairs={{1,0},{2,1},{3,2},{4,3},{5,4},{6,5},{7,6},{8,7},{9,8},{10,9},{11,1... | collective-permute-start | bytes 196616 | tf_op jit(solution)/shard_map/ppermute | solution.py:308
  51.2 1.0 copy-start
  85.7 17.5 %collective-permute-start.4 = (f32[64,128]{1,0:T(8,128)S(1)}, f32[64,128]{1,0:T(8,128)S(1)}, u32[]{:S(2)}, u32[]{:S(2)}) collective-permute-start(f32[64,128]{1,0:T(8,128)S(1)} %get-tuple-element.19), channel_id=1, source_target_pairs={{2,0},{3,1},{4,2},{5,3},{6,4},{7,5},{8,6},{9,7},{10,8},{11,9},{12,... | collective-permute-start | bytes 98312 | tf_op jit(solution)/shard_map/ppermute | solution.py:308
  87.6 15.5 %collective-permute-start.5 = (f32[64,128]{1,0:T(8,128)S(1)}, f32[64,128]{1,0:T(8,128)S(1)}, u32[]{:S(2)}, u32[]{:S(2)}) collective-permute-start(f32[64,128]{1,0:T(8,128)S(1)} %get-tuple-element.20), channel_id=1, source_target_pairs={{0,2},{1,3},{2,4},{3,5},{4,6},{5,7},{6,8},{7,9},{8,10},{9,11},{10,... | collective-permute-start | bytes 98312 | tf_op jit(solution)/shard_map/ppermute | solution.py:308
  91.5 11.6 %collective-permute-start.6 = (f32[64,128]{1,0:T(8,128)S(1)}, f32[64,128]{1,0:T(8,128)S(1)}, u32[]{:S(2)}, u32[]{:S(2)}) collective-permute-start(f32[64,128]{1,0:T(8,128)S(1)} %get-tuple-element.21), channel_id=1, source_target_pairs={{1,0},{2,1},{3,2},{4,3},{5,4},{6,5},{7,6},{8,7},{9,8},{10,9},{11,1... | collective-permute-start | bytes 98312 | tf_op jit(solution)/shard_map/ppermute | solution.py:308
  101.2 8.6 %collective-permute-start.7 = (f32[64,128]{1,0:T(8,128)S(1)}, f32[64,128]{1,0:T(8,128)S(1)}, u32[]{:S(2)}, u32[]{:S(2)}) collective-permute-start(f32[64,128]{1,0:T(8,128)S(1)} %get-tuple-element.22), channel_id=1, source_target_pairs={{0,1},{1,2},{2,3},{3,4},{4,5},{5,6},{6,7},{7,8},{8,9},{9,10},{10,1... | collective-permute-start | bytes 98312 | tf_op jit(solution)/shard_map/ppermute | solution.py:308

commit v2 on v1

v2 whole, which is shorter than its diff:
```python
import jax
import jax.numpy as jnp
from jax import lax
from jax.experimental import pallas as pl
from jax.experimental.pallas import tpu as pltpu
from jax.sharding import PartitionSpec as P

NK = 4
RADIUS = 2
P_DEV = 128
OMEGA = 0.8
LAY = 8
OBS = 32
TX = 16
TY = 128
HALO = 3
SPAN = (2 * RADIUS + 1) * P_DEV
OFF = 8
EXT = 32
KX = 16

F32 = jnp.float32
BF16 = jnp.bfloat16
I16 = jnp.int16
VMEM = pl.BlockSpec(memory_space=pltpu.VMEM)
SMEM = pl.BlockSpec(memory_space=pltpu.SMEM)


def turn_kernel(tile_ref, adj_ref, turned_ref, pair_ref, other_ref):
    stride = LAY * TX
    odd = tile_ref[0, 0] % 2
    pair_start = (1 - odd) * (TX - HALO)
    other_start = odd * (TX - HALO)

    def body(layer, carry):
        for x in range(TX):
            turned_ref[layer, x] = adj_ref[pl.ds(layer * TX + x, OBS, stride=stride), :]
        for j in range(HALO):
            pair_ref[layer, j] = turned_ref[layer, pair_start + j]
            other_ref[layer, j] = turned_ref[layer, other_start + j]
        return carry

    lax.fori_loop(0, LAY, body, 0)


def medium_edges_kernel(tile_ref, med_ref, open_ref, pair_ref, other_ref):
    odd = tile_ref[0, 0] % 2 == 1
    for layer in range(LAY):
        for field in range(5):
            if field < 4:
                tile = med_ref[layer, field]
            else:
                tile = open_ref[layer].astype(F32)
            low = tile[:HALO]
            high = tile[TX - HALO :]
            rows = pl.ds(field * HALO, HALO)
            pair_ref[layer, rows, :] = jnp.where(odd, low, high)
            other_ref[layer, rows, :] = jnp.where(odd, high, low)
        pair_ref[layer, pl.ds(15, 1), :] = jnp.zeros((1, TY), F32)
        other_ref[layer, pl.ds(15, 1), :] = jnp.zeros((1, TY), F32)


def stencil_kernel(
    tile_ref,
    turned_ref,
    pair_ref,
    other_ref,
    med_ref,
    open_ref,
    med_pair_ref,
    med_other_ref,
    cell_ref,
    weight_ref,
    out_ref,
    ext_ref,
    coef_ref,
    grad_ref,
    halo_ref,
    one_ref,
    two_ref,
):
    tile = tile_ref[0, 0]
    n_tiles = tile_ref[0, 1]
    whole_x = n_tiles * TX
    odd = tile % 2

    row = lax.broadcasted_iota(jnp.int32, (EXT, TY), 0)
    lane = lax.broadcasted_iota(jnp.int32, (EXT, TY), 1)
    global_x = tile * TX + row - OFF
    live = (global_x >= 0) & (global_x < whole_x)
    live_next = (global_x + 1 >= 0) & (global_x + 1 < whole_x)
    both = jnp.where(live & live_next, 1.0, 0.0).astype(F32)
    for layer in range(LAY):
        for field in range(5):
            fill = jnp.ones((OFF, TY), F32)
            ext_ref[field, layer, pl.ds(0, OFF), :] = fill
            ext_ref[field, layer, pl.ds(OFF + TX, OFF), :] = fill
            own = med_ref[layer, field] if field < 4 else open_ref[layer].astype(F32)
            ext_ref[field, layer, pl.ds(OFF, TX), :] = own
            pair = med_pair_ref[layer, pl.ds(field * HALO, HALO), :]
            other = med_other_ref[layer, pl.ds(field * HALO, HALO), :]
            ext_ref[field, layer, pl.ds(OFF - HALO, HALO), :] = jnp.where(odd == 1, pair, other)
            ext_ref[field, layer, pl.ds(OFF + TX, HALO), :] = jnp.where(odd == 1, other, pair)

    def place(layer, carry):
        for j in range(HALO):
            halo_ref[layer, HALO * (1 - odd) + j] = pair_ref[layer, j]
            halo_ref[layer, HALO * odd + j] = other_ref[layer, j]
        return carry

    lax.fori_loop(0, LAY, place, 0)

    def medium(field, layer):
        value = ext_ref[field, layer]
        if field < 3:
            return jnp.where(live, value, 1.0)
        return value

    def below(value):
        return pltpu.roll(value, 1, 0)

    def above(value):
        return pltpu.roll(value, EXT - 1, 0)

    def west(value):
        return pltpu.roll(value, 1, 1)

    def east(value):
        return pltpu.roll(value, TY - 1, 1)

    has_west = jnp.where(lane > 0, 1.0, 0.0).astype(F32)
    has_east = jnp.where(lane < TY - 1, 1.0, 0.0).astype(F32)
    before = below(both)

    def faces(mine, other):
        inv = 1.0 / (mine + other)
        face = 2.0 * mine * other * inv
        return face, face * other * inv

    for layer in range(LAY):
        k = medium(0, layer)
        kv = medium(1, layer)
        head = medium(3, layer)
        fxm, gxm = faces(k, below(k))
        fxp, gxp = faces(k, above(k))
        fym, gym = faces(k, west(k))
        fyp, gyp = faces(k, east(k))
        fxm = fxm * before
        fxp = fxp * both
        fym = fym * has_west
        fyp = fyp * has_east
        diag = medium(2, layer) + fxm + fxp + fym + fyp
        zero = jnp.zeros((EXT, TY), F32)
        fzm = fzp = gzm = gzp = zero
        if layer > 0:
            fzm, gzm = faces(kv, medium(1, layer - 1))
            gate = ext_ref[4, layer - 1]
            fzm = fzm * gate
            gzm = gzm * gate * (head - medium(3, layer - 1))
        if layer < LAY - 1:
            fzp, gzp = faces(kv, medium(1, layer + 1))
            gate = ext_ref[4, layer]
            fzp = fzp * gate
            gzp = gzp * gate * (head - medium(3, layer + 1))
        diag = diag + fzm + fzp
        scale = OMEGA / diag
        for n, value in enumerate((fxm, fxp, fym, fyp, fzm, fzp)):
            coef_ref[n, layer] = value * scale
        coef_ref[6, layer] = scale
        grad_ref[0, layer] = gxm * before * (head - below(head))
        grad_ref[1, layer] = gxp * both * (head - above(head))
        grad_ref[2, layer] = gym * has_west * (head - west(head))
        grad_ref[3, layer] = gyp * has_east * (head - east(head))
        grad_ref[4, layer] = gzm
        grad_ref[5, layer] = gzp

    lanes = lax.broadcasted_iota(jnp.int32, (OBS, TY), 1)
    eye = lax.broadcasted_iota(jnp.int32, (OBS, OBS), 0) == lax.broadcasted_iota(
        jnp.int32, (OBS, OBS), 1
    )

    def column(row):
        square = jnp.where(eye, jnp.broadcast_to(row, (OBS, OBS)), 0.0)
        return jnp.broadcast_to(jnp.sum(square, axis=1, keepdims=True), (OBS, TY))

    target = [
        column(cell_ref[pl.ds(m, 1), :].astype(F32)).astype(jnp.int32) - lanes for m in range(2)
    ]
    amount = [column(weight_ref[pl.ds(m, 1), :]) for m in range(2)]

    def rows(ref, n, layer, x):
        return jnp.broadcast_to(ref[n, layer, pl.ds(x + OFF, 1), :], (OBS, TY))

    def start(layer, j):
        if j < HALO:
            return halo_ref[layer, j]
        if j < HALO + TX:
            return turned_ref[layer, j - HALO]
        return halo_ref[layer, j - TX]

    def sweep(src, dst_ref, margin):
        def body(layer, carry):
            down = jnp.maximum(layer - 1, 0)
            up = jnp.minimum(layer + 1, LAY - 1)
            for x in range(-margin, TX + margin):
                j = x + margin + 1
                mid = src(layer, j)
                base = (layer * whole_x + tile * TX + x) * TY
                source = jnp.where(target[0] == base, amount[0], 0.0) + jnp.where(
                    target[1] == base, amount[1], 0.0
                )
                value = (1.0 - OMEGA) * mid + rows(coef_ref, 6, layer, x) * source
                value += rows(coef_ref, 0, layer, x) * src(layer, j - 1)
                value += rows(coef_ref, 1, layer, x) * src(layer, j + 1)
                value += rows(coef_ref, 2, layer, x) * pltpu.roll(mid, 1, 1)
                value += rows(coef_ref, 3, layer, x) * pltpu.roll(mid, TY - 1, 1)
                value += rows(coef_ref, 4, layer, x) * src(down, j)
                value += rows(coef_ref, 5, layer, x) * src(up, j)
                dst_ref[layer, j - 1] = value
            return carry

        lax.fori_loop(0, LAY, body, 0)

    sweep(start, one_ref, 2)
    sweep(lambda layer, j: one_ref[layer, j], two_ref, 1)

    def sense(layer, carry):
        down = jnp.maximum(layer - 1, 0)
        up = jnp.minimum(layer + 1, LAY - 1)
        for x in range(TX):
            j = x + 1
            mid = two_ref[layer, j]
            horiz = rows(grad_ref, 0, layer, x) * (two_ref[layer, j - 1] - mid)
            horiz += rows(grad_ref, 1, layer, x) * (two_ref[layer, j + 1] - mid)
            horiz += rows(grad_ref, 2, layer, x) * (pltpu.roll(mid, 1, 1) - mid)
            horiz += rows(grad_ref, 3, layer, x) * (pltpu.roll(mid, TY - 1, 1) - mid)
            vert = rows(grad_ref, 4, layer, x) * (two_ref[down, j] - mid)
            vert += rows(grad_ref, 5, layer, x) * (two_ref[up, j] - mid)
            chunk = layer * (TX // 2) + x // 2
            half = pl.ds((x % 2) * TY, TY)
            out_ref[chunk, pl.ds(0, OBS), half] = horiz
            out_ref[chunk, pl.ds(OBS, OBS), half] = vert
        return carry

    lax.fori_loop(0, LAY, sense, 0)


def krig_kernel(tile_ref, sens_ref, pilot_ref, med_ref, *rest):
    swap_ref, send_ref, late_ref, own_ref, index_ref, share_ref, total_ref = rest
    tile = tile_ref[0, 0]
    base = (tile - RADIUS) * P_DEV
    chunks = LAY * TX // KX

    for layer in range(LAY):
        index = [pilot_ref[k, layer] - base for k in range(NK)]
        share = [med_ref[layer, 4 + k] for k in range(NK)]
        for k in range(1, NK):
            for j in range(k):
                same = index[j] == index[k]
                share[j] = share[j] + jnp.where(same, share[k], 0.0)
                index[k] = jnp.where(same, -1, index[k])
        for k in range(NK):
            index_ref[k, pl.ds(layer * TX, TX), :] = index[k]
            share_ref[k, pl.ds(layer * TX, TX), :] = share[k]

    iota = lax.broadcasted_iota(I16, (16, TY), 0)
    total_ref[...] = jnp.zeros_like(total_ref)

    def split(value):
        high = value.astype(BF16)
        return high, (value - high.astype(F32)).astype(BF16)

    def body(chunk, carry):
        columns = []
        for s in range(KX):
            row = pl.ds(chunk * KX + s, 1)
            index = []
            high = []
            low = []
            for k in range(NK):
                index.append(jnp.broadcast_to(index_ref[k, row, :], (16, TY)).astype(I16))
                first, second = split(jnp.broadcast_to(share_ref[k, row, :], (16, TY)))
                high.append(first)
                low.append(second)
            uppers = []
            lowers = []
            for i in range(SPAN // 16):
                pilot = iota + I16(16 * i)
                upper = jnp.zeros((16, TY), BF16)
                lower = jnp.zeros((16, TY), BF16)
                for k in range(NK):
                    hit = index[k] == pilot
                    upper = jnp.where(hit, high[k], upper)
                    lower = jnp.where(hit, low[k], lower)
                uppers.append(upper)
                lowers.append(lower)
            columns.append(jnp.concatenate(uppers + lowers, axis=0))
        sens = []
        for q in range(KX // 2):
            sens.append(jnp.concatenate(split(sens_ref[chunk * (KX // 2) + q]), axis=0))
        total_ref[...] += lax.dot_general(
            jnp.concatenate(columns, axis=1),
            jnp.concatenate(sens, axis=1),
            (((1,), (1,)), ((), ())),
            preferred_element_type=F32,
        )
        return carry

    lax.fori_loop(0, chunks, body, 0)

    def piece(o):
        start = pl.multiple_of(o * P_DEV, P_DEV)
        value = total_ref[pl.ds(start, P_DEV), :] + total_ref[pl.ds(SPAN + start, P_DEV), :]
        value = value.T
        return value[: 2 * OBS] + value[2 * OBS :]

    odd = tile % 2
    swap_ref[...] = piece((1 - odd) * 4)
    send_ref[pl.ds(0, 2 * OBS), :] = piece(1 + 2 * odd)
    send_ref[pl.ds(2 * OBS, 2 * OBS), :] = piece(4 * odd)
    late_ref[...] = piece(3 - 2 * odd)
    own_ref[...] = piece(RADIUS)


def swapped(block):
    count = lax.axis_size("grid")
    return lax.ppermute(block, "grid", [(i, i ^ 1) for i in range(count)])


def crossed(block):
    count = lax.axis_size("grid")
    pairs = [(i, i + 1 if i % 2 else i - 1) for i in range(1, count - 1)]
    return lax.ppermute(block, "grid", pairs)


def gathered(block, axis):
    count = lax.axis_size(axis)
    return lax.all_to_all(
        jnp.broadcast_to(block[None], (count,) + block.shape), axis, 0, 0, tiled=False
    )


def shards(
    adjoint_start,
    conductance,
    storage,
    head,
    layer_open,
    krig_weight,
    krig_pilot,
    obs_cell,
    obs_weight,
):
    sds = jax.ShapeDtypeStruct
    tile = jnp.stack([lax.axis_index("grid"), jnp.int32(lax.axis_size("grid"))]).reshape(1, 2)

    own = jnp.concatenate([conductance[:, 0], storage, head, krig_weight[:, 0]], axis=0)
    medium = gathered(own, "obs")

    edge = sds((LAY, HALO, OBS, TY), F32)
    turned, pair, other = pl.pallas_call(
        turn_kernel,
        out_shape=(sds((LAY, TX, OBS, TY), F32), edge, edge),
        in_specs=[SMEM, VMEM],
        out_specs=(VMEM, VMEM, VMEM),
        compiler_params=pltpu.CompilerParams(vmem_limit_bytes=12 * 2**20),
    )(tile, adjoint_start.reshape(OBS * LAY * TX, TY))
    other = crossed(other)
    pair = swapped(pair)

    edge = sds((LAY, 16, TY), F32)
    med_pair, med_other = pl.pallas_call(
        medium_edges_kernel,
        out_shape=(edge, edge),
        in_specs=[SMEM, VMEM, VMEM],
        out_specs=(VMEM, VMEM),
        compiler_params=pltpu.CompilerParams(vmem_limit_bytes=8 * 2**20),
    )(tile, medium, layer_open)
    med_other = crossed(med_other)
    med_pair = swapped(med_pair)

    sens = pl.pallas_call(
        stencil_kernel,
        out_shape=sds((LAY * TX // 2, 2 * OBS, 2 * TY), F32),
        in_specs=[SMEM] + [VMEM] * 9,
        out_specs=VMEM,
        scratch_shapes=[
            pltpu.VMEM((5, LAY, EXT, TY), F32),
            pltpu.VMEM((7, LAY, EXT, TY), F32),
            pltpu.VMEM((6, LAY, EXT, TY), F32),
            pltpu.VMEM((LAY, 2 * HALO, OBS, TY), F32),
            pltpu.VMEM((LAY, TX + 4, OBS, TY), F32),
            pltpu.VMEM((LAY, TX + 2, OBS, TY), F32),
        ],
        compiler_params=pltpu.CompilerParams(vmem_limit_bytes=24 * 2**20),
    )(tile, turned, pair, other, medium, layer_open, med_pair, med_other, obs_cell.T, obs_weight.T)

    piece = sds((2 * OBS, P_DEV), F32)
    swap, send, late, owned = pl.pallas_call(
        krig_kernel,
        out_shape=(piece, sds((4 * OBS, P_DEV), F32), piece, piece),
        in_specs=[SMEM] + [VMEM] * 3,
        out_specs=(VMEM,) * 4,
        scratch_shapes=[
            pltpu.VMEM((NK, LAY * TX, TY), jnp.int32),
            pltpu.VMEM((NK, LAY * TX, TY), F32),
            pltpu.VMEM((2 * SPAN, 4 * OBS), F32),
        ],
        compiler_params=pltpu.CompilerParams(vmem_limit_bytes=28 * 2**20),
    )(tile, sens, krig_pilot, medium)

    half = 2 * OBS
    arrived = crossed(jnp.concatenate([send[:half] + swapped(swap), send[half:]], axis=0))
    owned = owned + arrived[:half] + swapped(late + arrived[half:])
    return owned.reshape(2, OBS, P_DEV)


def solution(mesh):
    return jax.shard_map(
        shards,
        mesh=mesh,
        in_specs=(
            P("obs", None, "grid", None),
            P(None, "obs", "grid", None),
            P("obs", "grid", None),
            P("obs", "grid", None),
            P(None, "grid", None),
            P(None, "obs", "grid", None),
            P(None, None, "grid", None),
            P("obs", None),
            P("obs", None),
        ),
        out_specs=P(None, "obs", "grid"),
        check_vma=False,
    )
```

time: 111 us -> 76.4 us (0.69)
  the two profiles are of different devices: /device:TPU:264 before, /device:TPU:199 now
where the time goes in v2:
time: 76.4 us; the launch traced here: 75.9 us
  starting transfers between devices  31 us (41%)
  Pallas kernels  25.1 us (33%)
  waiting for transfers between devices  15.7 us (21%)
  local copies, waits for them, and re-layouts  2.44 us (3%)
  other arithmetic  1.53 us (2%)
    pallas_call x1, Pallas kernels, shards(): pl.pallas_call(krig_kernel, out_shape=(piece, sds((4 * OBS, P_DEV), F32),...  15.3 us
    ppermute x3, starting transfers between devices, crossed(): return lax.ppermute(block, 'grid', pairs)  15.1 us
    ppermute x4, starting transfers between devices, swapped(): return lax.ppermute(block, 'grid', [(i, i ^ 1) for i in range(count)])  9.08 us
    ppermute x3, waiting for transfers between devices, crossed(): return lax.ppermute(block, 'grid', pairs)  7.71 us
    all_to_all x1, starting transfers between devices, gathered(): lax.all_to_all(jnp.broadcast_to(block[None], (count,) + block.shape), axi...  6.82 us
    pallas_call x1, Pallas kernels, shards(): pl.pallas_call(stencil_kernel, out_shape=sds((LAY * TX // 2, 2 * OBS, 2 *...  6.5 us
    all_to_all x1, waiting for transfers between devices, gathered(): lax.all_to_all(jnp.broadcast_to(block[None], (count,) + block.shape), axi...  5.66 us
    pallas_call x1, Pallas kernels, shards(): pl.pallas_call(turn_kernel, out_shape=(sds((LAY, TX, OBS, TY), F32), edge...  2.74 us
  transfers between devices with their start and end apart: 8, of which 5 were waited for; matrix products, arithmetic and copies ran while one was open for 0% of the time, Pallas kernels for 4%

profile of v2, /device:TPU:199, one launch (start us, length us, event | category | flops | bytes accessed | tf_op | source)
XLA Modules:
  0.0 75.9 jit_solution(12133089805995458335)
XLA Ops:
  0.0 0.0 copy-start.1
  0.0 0.8 %pad_maximum_fusion = f32[8,16,128]{2,1,0:T(8,128)S(1)} fusion(f32[4,16,128]{2,1,0:T(8,128)} %bitcast.12, f32[1,16,128]{2,1,0:T(8,128)} %param.12, f32[1,16,128]{2,1,0:T(8,128)} %param.11, f32[2,16,128]{2,1,0:T(8,128)} %bitcast.13), kind=kLoop, calls=%fused_computation | loop fusion | flops 49152 | bytes 131072 | tf_op jit(solution)/shard_map/concatenate | solution.py:357
  0.8 0.0 copy-start.3
  0.8 0.0 copy-start.4
  0.8 0.8 %broadcast_in_dim.2 = f32[8,8,16,128]{3,2,1,0:T(8,128)} broadcast(f32[8,16,128]{2,1,0:T(8,128)S(1)} %pad_maximum_fusion), dimensions={1,2,3} | broadcast | bytes 589824 | tf_op jit(solution)/shard_map/broadcast_in_dim | solution.py:339
  1.7 6.8 %all-to-all-start = ((f32[8,8,16,128]{3,2,1,0:T(8,128)}), f32[8,8,16,128]{3,2,1,0:T(8,128)S(1)}, u32[]{:S(2)}, u32[]{:S(2)}) async-start(f32[8,8,16,128]{3,2,1,0:T(8,128)} %broadcast_in_dim.2), calls=%async_computation | async-start | bytes 1048576 | tf_op jit(solution)/shard_map/all_to_all | solution.py:338
  8.5 0.1 add_bitcast_fusion.tile_ref
  8.6 1.6 %copy-done = f32[32,8,16,128]{3,2,1,0:T(8,128)S(1)} copy-done((f32[32,8,16,128]{3,2,1,0:T(8,128)S(1)}, f32[32,8,16,128]{3,2,1,0:T(8,128)}, u32[]{:S(2)}) %copy-start) | copy-done | bytes 2097176
  10.2 2.7 %shard_map.91 = (f32[8,16,32,128]{3,2,1,0:T(8,128)S(1)}, f32[8,3,32,128]{3,2,1,0:T(8,128)}, f32[8,3,32,128]{3,2,1,0:T(8,128)}) custom-call(s32[1,2]{1,0:T(1,128)S(1)} %add_bitcast_fusion.tile_ref, f32[4096,128]{1,0:T(8,128)S(1)} %bitcast.9), custom_call_target="tpu_custom_call" | custom-call | tf_op jit(solution)/shard_map/pallas_call | solution.py:361
  12.9 2.9 %collective-permute-start = (f32[8,3,32,128]{3,2,1,0:T(8,128)}, f32[8,3,32,128]{3,2,1,0:T(8,128)S(1)}, u32[]{:S(2)}, u32[]{:S(2)}) collective-permute-start(f32[8,3,32,128]{3,2,1,0:T(8,128)} %get-tuple-element.15), channel_id=1, source_target_pairs={{0,1},{1,0},{2,3},{3,2},{4,5},{5,4},{6,7},{7,6},{8,9},{9,8},{10,11... | collective-permute-start | bytes 1179656 | tf_op jit(solution)/shard_map/ppermute | solution.py:327
  15.8 5.0 %collective-permute-start.1 = (f32[8,3,32,128]{3,2,1,0:T(8,128)}, f32[8,3,32,128]{3,2,1,0:T(8,128)S(1)}, u32[]{:S(2)}, u32[]{:S(2)}) collective-permute-start(f32[8,3,32,128]{3,2,1,0:T(8,128)} %get-tuple-element.16), channel_id=1, source_target_pairs={{1,2},{2,1},{3,4},{4,3},{5,6},{6,5},{7,8},{8,7},{9,10},{10,9},{11,... | collective-permute-start | bytes 1179656 | tf_op jit(solution)/shard_map/ppermute | solution.py:333
  20.8 5.7 %all-to-all-done.med_ref = f32[8,8,16,128]{3,2,1,0:T(8,128)S(1)} async-done(((f32[8,8,16,128]{3,2,1,0:T(8,128)}), f32[8,8,16,128]{3,2,1,0:T(8,128)S(1)}, u32[]{:S(2)}, u32[]{:S(2)}) %all-to-all-start) | async-done | bytes 524320 | tf_op jit(solution)/shard_map/all_to_all | solution.py:338
  26.4 0.0 copy-done.1
  26.5 0.6 shard_map.92
  27.0 2.4 %collective-permute-start.2 = (f32[8,16,128]{2,1,0:T(8,128)S(1)}, f32[8,16,128]{2,1,0:T(8,128)S(1)}, u32[]{:S(2)}, u32[]{:S(2)}) collective-permute-start(f32[8,16,128]{2,1,0:T(8,128)S(1)} %get-tuple-element.17), channel_id=1, source_target_pairs={{0,1},{1,0},{2,3},{3,2},{4,5},{5,4},{6,7},{7,6},{8,9},{9,8},{10,11... | collective-permute-start | bytes 196616 | tf_op jit(solution)/shard_map/ppermute | solution.py:327
  29.4 5.0 %collective-permute-start.3 = (f32[8,16,128]{2,1,0:T(8,128)S(1)}, f32[8,16,128]{2,1,0:T(8,128)S(1)}, u32[]{:S(2)}, u32[]{:S(2)}) collective-permute-start(f32[8,16,128]{2,1,0:T(8,128)S(1)} %get-tuple-element.18), channel_id=1, source_target_pairs={{1,2},{2,1},{3,4},{4,3},{5,6},{6,5},{7,8},{8,7},{9,10},{10,9},{11,... | collective-permute-start | bytes 196616 | tf_op jit(solution)/shard_map/ppermute | solution.py:333
  34.5 0.0 collective-permute-done.pair_ref
  34.5 0.0 collective-permute-done.1.other_ref
  34.5 0.0 collective-permute-done.2.med_pair_ref
  34.5 3.8 %collective-permute-done.3.med_other_ref = f32[8,16,128]{2,1,0:T(8,128)S(1)} collective-permute-done((f32[8,16,128]{2,1,0:T(8,128)S(1)}, f32[8,16,128]{2,1,0:T(8,128)S(1)}, u32[]{:S(2)}, u32[]{:S(2)}) %collective-permute-start.3) | collective-permute-done | bytes 65568 | tf_op jit(solution)/shard_map/ppermute | solution.py:333
  38.4 0.0 copy-done.3
  38.4 0.0 copy-done.4
  38.4 6.5 %shard_map.93.sens_ref = f32[64,64,256]{2,1,0:T(8,128)S(1)} custom-call(s32[1,2]{1,0:T(1,128)S(1)} %add_bitcast_fusion.tile_ref, f32[8,16,32,128]{3,2,1,0:T(8,128)S(1)} %get-tuple-element.14.turned_ref, f32[8,3,32,128]{3,2,1,0:T(8,128)S(1)} %collective-permute-done.pair_ref, f32[8,3,32,128]{3,2,1,0:T(8,128)S(1)} %collective-permute-done.1.other_ref, ...), custom_call_target="tpu_custom_call" | custom-call | tf_op jit(solution)/shard_map/pallas_call | solution.py:382
  44.9 0.0 copy-done.2
  44.9 15.3 %shard_map.94 = (f32[64,128]{1,0:T(8,128)S(1)}, f32[128,128]{1,0:T(8,128)S(1)}, f32[64,128]{1,0:T(8,128)S(1)}, f32[64,128]{1,0:T(8,128)S(1)}) custom-call(s32[1,2]{1,0:T(1,128)S(1)} %add_bitcast_fusion.tile_ref, f32[64,64,256]{2,1,0:T(8,128)S(1)} %shard_map.93.sens_ref, s32[4,8,16,128]{3,2,1,0:T(8,128)S(1)} %copy-done.2, ...), custom_call_target="tpu_custom_call" | custom-call | tf_op jit(solution)/shard_map/pallas_call | solution.py:399
  60.2 1.9 %collective-permute-start.4 = (f32[64,128]{1,0:T(8,128)S(1)}, f32[64,128]{1,0:T(8,128)S(1)}, u32[]{:S(2)}, u32[]{:S(2)}) collective-permute-start(f32[64,128]{1,0:T(8,128)S(1)} %get-tuple-element.21), channel_id=1, source_target_pairs={{0,1},{1,0},{2,3},{3,2},{4,5},{5,4},{6,7},{7,6},{8,9},{9,8},{10,11... | collective-permute-start | bytes 98312 | tf_op jit(solution)/shard_map/ppermute | solution.py:327
  62.1 1.2 %collective-permute-done.4 = f32[64,128]{1,0:T(8,128)S(1)} collective-permute-done((f32[64,128]{1,0:T(8,128)S(1)}, f32[64,128]{1,0:T(8,128)S(1)}, u32[]{:S(2)}, u32[]{:S(2)}) %collective-permute-start.4) | collective-permute-done | bytes 32800 | tf_op jit(solution)/shard_map/ppermute | solution.py:327
  63.3 5.0 %collective-permute-start.5 = (f32[128,128]{1,0:T(8,128)S(1)}, f32[128,128]{1,0:T(8,128)S(1)}, u32[]{:S(2)}, u32[]{:S(2)}) collective-permute-start(f32[128,128]{1,0:T(8,128)S(1)} %pad_maximum_fusion.1), channel_id=1, source_target_pairs={{1,2},{2,1},{3,4},{4,3},{5,6},{6,5},{7,8},{8,7},{9,10},{10,9},{11,... | collective-permute-start | bytes 196616 | tf_op jit(solution)/shard_map/ppermute | solution.py:333
  68.3 3.9 %collective-permute-done.5 = f32[128,128]{1,0:T(8,128)S(1)} collective-permute-done((f32[128,128]{1,0:T(8,128)S(1)}, f32[128,128]{1,0:T(8,128)S(1)}, u32[]{:S(2)}, u32[]{:S(2)}) %collective-permute-start.5) | collective-permute-done | bytes 65568 | tf_op jit(solution)/shard_map/ppermute | solution.py:333
  72.2 1.9 %collective-permute-start.6 = (f32[64,128]{1,0:T(8,128)S(1)}, f32[64,128]{1,0:T(8,128)S(1)}, u32[]{:S(2)}, u32[]{:S(2)}) collective-permute-start(f32[64,128]{1,0:T(8,128)S(1)} %slice_add_fusion), channel_id=1, source_target_pairs={{0,1},{1,0},{2,3},{3,2},{4,5},{5,4},{6,7},{7,6},{8,9},{9,8},{10,11... | collective-permute-start | bytes 98312 | tf_op jit(solution)/shard_map/ppermute | solution.py:327
  74.1 1.2 %collective-permute-done.6 = f32[64,128]{1,0:T(8,128)S(1)} collective-permute-done((f32[64,128]{1,0:T(8,128)S(1)}, f32[64,128]{1,0:T(8,128)S(1)}, u32[]{:S(2)}, u32[]{:S(2)}) %collective-permute-start.6) | collective-permute-done | bytes 32800 | tf_op jit(solution)/shard_map/ppermute | solution.py:327
  75.3 0.6 fusion
  (5 shorter events, 0.0 us)
Async XLA Ops:
  0.0 26.5 %copy-start.1 = (s32[8,16,128]{2,1,0:T(8,128)S(1)}, s32[8,16,128]{2,1,0:T(8,128)}, u32[]{:S(2)}) copy-start(s32[8,16,128]{2,1,0:T(8,128)} %open_ref.3) | copy-start | bytes 196612
  0.8 37.5 %copy-start.3 = (s32[32,2]{0,1:T(2,128)S(1)}, s32[32,2]{0,1:T(2,128)}, u32[]{:S(2)}) copy-start(s32[32,2]{0,1:T(2,128)} %param.16) | copy-start | bytes 772
  0.8 37.5 %copy-start.4 = (f32[32,2]{0,1:T(2,128)S(1)}, f32[32,2]{0,1:T(2,128)}, u32[]{:S(2)}) copy-start(f32[32,2]{0,1:T(2,128)} %param.17) | copy-start | bytes 772
  1.7 24.8 %all-to-all-start = ((f32[8,8,16,128]{3,2,1,0:T(8,128)}), f32[8,8,16,128]{3,2,1,0:T(8,128)S(1)}, u32[]{:S(2)}, u32[]{:S(2)}) async-start(f32[8,8,16,128]{3,2,1,0:T(8,128)} %broadcast_in_dim.2), calls=%async_computation | async-start | bytes 1048576 | tf_op jit(solution)/shard_map/all_to_all | solution.py:338
  8.6 1.6 %copy-start = (f32[32,8,16,128]{3,2,1,0:T(8,128)S(1)}, f32[32,8,16,128]{3,2,1,0:T(8,128)}, u32[]{:S(2)}) copy-start(f32[32,8,16,128]{3,2,1,0:T(8,128)} %param.9) | copy-start | bytes 6291460
  12.9 21.6 %collective-permute-start = (f32[8,3,32,128]{3,2,1,0:T(8,128)}, f32[8,3,32,128]{3,2,1,0:T(8,128)S(1)}, u32[]{:S(2)}, u32[]{:S(2)}) collective-permute-start(f32[8,3,32,128]{3,2,1,0:T(8,128)} %get-tuple-element.15), channel_id=1, source_target_pairs={{0,1},{1,0},{2,3},{3,2},{4,5},{5,4},{6,7},{7,6},{8,9},{9,8},{10,11... | collective-permute-start | bytes 1179656 | tf_op jit(solution)/shard_map/ppermute | solution.py:327
  15.8 18.7 %collective-permute-start.1 = (f32[8,3,32,128]{3,2,1,0:T(8,128)}, f32[8,3,32,128]{3,2,1,0:T(8,128)S(1)}, u32[]{:S(2)}, u32[]{:S(2)}) collective-permute-start(f32[8,3,32,128]{3,2,1,0:T(8,128)} %get-tuple-element.16), channel_id=1, source_target_pairs={{1,2},{2,1},{3,4},{4,3},{5,6},{6,5},{7,8},{8,7},{9,10},{10,9},{11,... | collective-permute-start | bytes 1179656 | tf_op jit(solution)/shard_map/ppermute | solution.py:333
  27.0 7.5 %collective-permute-start.2 = (f32[8,16,128]{2,1,0:T(8,128)S(1)}, f32[8,16,128]{2,1,0:T(8,128)S(1)}, u32[]{:S(2)}, u32[]{:S(2)}) collective-permute-start(f32[8,16,128]{2,1,0:T(8,128)S(1)} %get-tuple-element.17), channel_id=1, source_target_pairs={{0,1},{1,0},{2,3},{3,2},{4,5},{5,4},{6,7},{7,6},{8,9},{9,8},{10,11... | collective-permute-start | bytes 196616 | tf_op jit(solution)/shard_map/ppermute | solution.py:327
  29.4 8.9 %collective-permute-start.3 = (f32[8,16,128]{2,1,0:T(8,128)S(1)}, f32[8,16,128]{2,1,0:T(8,128)S(1)}, u32[]{:S(2)}, u32[]{:S(2)}) collective-permute-start(f32[8,16,128]{2,1,0:T(8,128)S(1)} %get-tuple-element.18), channel_id=1, source_target_pairs={{1,2},{2,1},{3,4},{4,3},{5,6},{6,5},{7,8},{8,7},{9,10},{10,9},{11,... | collective-permute-start | bytes 196616 | tf_op jit(solution)/shard_map/ppermute | solution.py:333
  38.4 6.5 %copy-start.2 = (s32[4,8,16,128]{3,2,1,0:T(8,128)S(1)}, s32[4,8,16,128]{3,2,1,0:T(8,128)}, u32[]{:S(2)}) copy-start(s32[4,8,16,128]{3,2,1,0:T(8,128)} %pilot_ref.1) | copy-start | bytes 786436
  60.2 3.1 %collective-permute-start.4 = (f32[64,128]{1,0:T(8,128)S(1)}, f32[64,128]{1,0:T(8,128)S(1)}, u32[]{:S(2)}, u32[]{:S(2)}) collective-permute-start(f32[64,128]{1,0:T(8,128)S(1)} %get-tuple-element.21), channel_id=1, source_target_pairs={{0,1},{1,0},{2,3},{3,2},{4,5},{5,4},{6,7},{7,6},{8,9},{9,8},{10,11... | collective-permute-start | bytes 98312 | tf_op jit(solution)/shard_map/ppermute | solution.py:327
  63.3 8.9 %collective-permute-start.5 = (f32[128,128]{1,0:T(8,128)S(1)}, f32[128,128]{1,0:T(8,128)S(1)}, u32[]{:S(2)}, u32[]{:S(2)}) collective-permute-start(f32[128,128]{1,0:T(8,128)S(1)} %pad_maximum_fusion.1), channel_id=1, source_target_pairs={{1,2},{2,1},{3,4},{4,3},{5,6},{6,5},{7,8},{8,7},{9,10},{10,9},{11,... | collective-permute-start | bytes 196616 | tf_op jit(solution)/shard_map/ppermute | solution.py:333
  72.2 3.1 %collective-permute-start.6 = (f32[64,128]{1,0:T(8,128)S(1)}, f32[64,128]{1,0:T(8,128)S(1)}, u32[]{:S(2)}, u32[]{:S(2)}) collective-permute-start(f32[64,128]{1,0:T(8,128)S(1)} %slice_add_fusion), channel_id=1, source_target_pairs={{0,1},{1,0},{2,3},{3,2},{4,5},{5,4},{6,7},{7,6},{8,9},{9,8},{10,11... | collective-permute-start | bytes 98312 | tf_op jit(solution)/shard_map/ppermute | solution.py:327

commit v3 on v2

--- a/solution.py
+++ b/solution.py
@@ -4,6 +4,7 @@
 from jax.experimental import pallas as pl
 from jax.experimental.pallas import tpu as pltpu
 from jax.sharding import PartitionSpec as P
+
 
 NK = 4
 RADIUS = 2
@@ -24,17 +25,57 @@
 I16 = jnp.int16
 VMEM = pl.BlockSpec(memory_space=pltpu.VMEM)
 SMEM = pl.BlockSpec(memory_space=pltpu.SMEM)
-
-
-def turn_kernel(tile_ref, adj_ref, turned_ref, pair_ref, other_ref):
-    stride = LAY * TX
+HBM = pl.BlockSpec(memory_space=pltpu.HBM)
+
+
+def spread_kernel(
+    cond_ref, storage_ref, head_ref, krig_ref, med_ref, share_ref, own_ref, in_ref, out_ref
+):
+    parts = (
+        (cond_ref.at[:, 0], own_ref.at[pl.ds(0, 2)]),
+        (storage_ref, own_ref.at[pl.ds(2, 1)]),
+        (head_ref, own_ref.at[pl.ds(3, 1)]),
+        (krig_ref.at[:, 0], own_ref.at[pl.ds(4, NK)]),
+    )
+    loads = [
+        pltpu.make_async_copy(part, place, in_ref.at[i]) for i, (part, place) in enumerate(parts)
+    ]
+    for load in loads:
+        load.start()
+    for load in loads:
+        load.wait()
+    stores = []
+    for layer in range(LAY):
+        for i, ref in enumerate((med_ref, share_ref)):
+            stores.append(
+                pltpu.make_async_copy(
+                    own_ref.at[pl.ds(4 * i, 4)], ref.at[layer], out_ref.at[2 * layer + i]
+                )
+            )
+    for store in stores:
+        store.start()
+    for store in stores:
+        store.wait()
+
+
+def turn_kernel(tile_ref, adj_ref, turned_ref, pair_ref, other_ref, buf_ref, sem_ref):
     odd = tile_ref[0, 0] % 2
     pair_start = (1 - odd) * (TX - HALO)
     other_start = odd * (TX - HALO)
 
+    def fetch(layer):
+        return pltpu.make_async_copy(
+            adj_ref.at[:, layer], buf_ref.at[layer], sem_ref.at[layer]
+        )
+
+    for layer in range(LAY):
+        fetch(layer).start()
+
     def body(layer, carry):
+        fetch(layer).wait()
+        rows_ref = buf_ref.at[layer].reshape(OBS * TX, TY)
         for x in range(TX):
-            turned_ref[layer, x] = adj_ref[pl.ds(layer * TX + x, OBS, stride=stride), :]
+            turned_ref[layer, x] = rows_ref[pl.ds(x, OBS, stride=TX), :]
         for j in range(HALO):
             pair_ref[layer, j] = turned_ref[layer, pair_start + j]
             other_ref[layer, j] = turned_ref[layer, other_start + j]
@@ -71,13 +112,15 @@
     med_other_ref,
     cell_ref,
     weight_ref,
-    out_ref,
+    sens_ref,
     ext_ref,
     coef_ref,
     grad_ref,
     halo_ref,
     one_ref,
     two_ref,
+    out_ref,
+    sem_ref,
 ):
     tile = tile_ref[0, 0]
     n_tiles = tile_ref[0, 1]
@@ -224,6 +267,10 @@
     sweep(start, one_ref, 2)
     sweep(lambda layer, j: one_ref[layer, j], two_ref, 1)
 
+    def store(layer):
+        part = pl.ds(layer * (TX // 2), TX // 2)
+        return pltpu.make_async_copy(out_ref.at[part], sens_ref.at[part], sem_ref.at[layer])
+
     def sense(layer, carry):
         down = jnp.maximum(layer - 1, 0)
         up = jnp.minimum(layer + 1, LAY - 1)
@@ -240,20 +287,30 @@
             half = pl.ds((x % 2) * TY, TY)
             out_ref[chunk, pl.ds(0, OBS), half] = horiz
             out_ref[chunk, pl.ds(OBS, OBS), half] = vert
+        store(layer).start()
         return carry
 
     lax.fori_loop(0, LAY, sense, 0)
-
-
-def krig_kernel(tile_ref, sens_ref, pilot_ref, med_ref, *rest):
-    swap_ref, send_ref, late_ref, own_ref, index_ref, share_ref, total_ref = rest
+    for layer in range(LAY):
+        store(layer).wait()
+
+
+def krig_kernel(tile_ref, far_ref, pilot_ref, weight_ref, *rest):
+    swap_ref, send_ref, late_ref, own_ref, index_ref, share_ref, total_ref, sens_ref, sem_ref = rest
+
+    def fetch(chunk):
+        part = pl.ds(chunk * (KX // 2), KX // 2)
+        return pltpu.make_async_copy(far_ref.at[part], sens_ref.at[part], sem_ref.at[chunk])
+
+    for chunk in range(LAY * TX // KX):
+        fetch(chunk).start()
     tile = tile_ref[0, 0]
     base = (tile - RADIUS) * P_DEV
     chunks = LAY * TX // KX
 
     for layer in range(LAY):
         index = [pilot_ref[k, layer] - base for k in range(NK)]
-        share = [med_ref[layer, 4 + k] for k in range(NK)]
+        share = [weight_ref[layer, k] for k in range(NK)]
         for k in range(1, NK):
             for j in range(k):
                 same = index[j] == index[k]
@@ -295,6 +352,7 @@
                 uppers.append(upper)
                 lowers.append(lower)
             columns.append(jnp.concatenate(uppers + lowers, axis=0))
+        fetch(chunk).wait()
         sens = []
         for q in range(KX // 2):
             sens.append(jnp.concatenate(split(sens_ref[chunk * (KX // 2) + q]), axis=0))
@@ -322,6 +380,10 @@
     own_ref[...] = piece(RADIUS)
 
 
+def in_hbm(array):
+    return pltpu.with_memory_space_constraint(array, pltpu.HBM)
+
+
 def swapped(block):
     count = lax.axis_size("grid")
     return lax.ppermute(block, "grid", [(i, i ^ 1) for i in range(count)])
@@ -333,14 +395,11 @@
     return lax.ppermute(block, "grid", pairs)
 
 
-def gathered(block, axis):
-    count = lax.axis_size(axis)
-    return lax.all_to_all(
-        jnp.broadcast_to(block[None], (count,) + block.shape), axis, 0, 0, tiled=False
-    )
-
-
-def shards(
+def gathered(copies, axis):
+    return lax.all_to_all(copies, axis, 0, 0, tiled=False)
+
+
+def local(
     adjoint_start,
     conductance,
     storage,
@@ -354,17 +413,33 @@
     sds = jax.ShapeDtypeStruct
     tile = jnp.stack([lax.axis_index("grid"), jnp.int32(lax.axis_size("grid"))]).reshape(1, 2)
 
-    own = jnp.concatenate([conductance[:, 0], storage, head, krig_weight[:, 0]], axis=0)
-    medium = gathered(own, "obs")
+    copies = pltpu.HBM((LAY, 4, TX, TY), F32)
+    med_copies, share_copies = pl.pallas_call(
+        spread_kernel,
+        out_shape=(copies, copies),
+        in_specs=[HBM] * 4,
+        out_specs=(HBM, HBM),
+        scratch_shapes=[
+            pltpu.VMEM((4 + NK, TX, TY), F32),
+            pltpu.SemaphoreType.DMA((4,)),
+            pltpu.SemaphoreType.DMA((2 * LAY,)),
+        ],
+        compiler_params=pltpu.CompilerParams(vmem_limit_bytes=4 * 2**20),
+    )(*map(in_hbm, (conductance, storage, head, krig_weight)))
+    medium = gathered(med_copies, "obs")
 
     edge = sds((LAY, HALO, OBS, TY), F32)
     turned, pair, other = pl.pallas_call(
         turn_kernel,
         out_shape=(sds((LAY, TX, OBS, TY), F32), edge, edge),
-        in_specs=[SMEM, VMEM],
+        in_specs=[SMEM, HBM],
         out_specs=(VMEM, VMEM, VMEM),
+        scratch_shapes=[
+            pltpu.VMEM((LAY, OBS, TX, TY), F32),
+            pltpu.SemaphoreType.DMA((LAY,)),
+        ],
         compiler_params=pltpu.CompilerParams(vmem_limit_bytes=12 * 2**20),
-    )(tile, adjoint_start.reshape(OBS * LAY * TX, TY))
+    )(tile, in_hbm(adjoint_start))
     other = crossed(other)
     pair = swapped(pair)
 
@@ -378,12 +453,13 @@
     )(tile, medium, layer_open)
     med_other = crossed(med_other)
     med_pair = swapped(med_pair)
+    share = gathered(share_copies, "obs")
 
     sens = pl.pallas_call(
         stencil_kernel,
-        out_shape=sds((LAY * TX // 2, 2 * OBS, 2 * TY), F32),
+        out_shape=pltpu.HBM((LAY * TX // 2, 2 * OBS, 2 * TY), F32),
         in_specs=[SMEM] + [VMEM] * 9,
-        out_specs=VMEM,
+        out_specs=HBM,
         scratch_shapes=[
             pltpu.VMEM((5, LAY, EXT, TY), F32),
             pltpu.VMEM((7, LAY, EXT, TY), F32),
@@ -391,6 +467,8 @@
             pltpu.VMEM((LAY, 2 * HALO, OBS, TY), F32),
             pltpu.VMEM((LAY, TX + 4, OBS, TY), F32),
             pltpu.VMEM((LAY, TX + 2, OBS, TY), F32),
+            pltpu.VMEM((LAY * TX // 2, 2 * OBS, 2 * TY), F32),
+            pltpu.SemaphoreType.DMA((LAY,)),
         ],
         compiler_params=pltpu.CompilerParams(vmem_limit_bytes=24 * 2**20),
     )(tile, turned, pair, other, medium, layer_open, med_pair, med_other, obs_cell.T, obs_weight.T)
@@ -399,15 +477,17 @@
     swap, send, late, owned = pl.pallas_call(
         krig_kernel,
         out_shape=(piece, sds((4 * OBS, P_DEV), F32), piece, piece),
-        in_specs=[SMEM] + [VMEM] * 3,
+        in_specs=[SMEM, HBM, VMEM, VMEM],
         out_specs=(VMEM,) * 4,
         scratch_shapes=[
             pltpu.VMEM((NK, LAY * TX, TY), jnp.int32),
             pltpu.VMEM((NK, LAY * TX, TY), F32),
             pltpu.VMEM((2 * SPAN, 4 * OBS), F32),
+            pltpu.VMEM((LAY * TX // 2, 2 * OBS, 2 * TY), F32),
+            pltpu.SemaphoreType.DMA((LAY * TX // KX,)),
         ],
-        compiler_params=pltpu.CompilerParams(vmem_limit_bytes=28 * 2**20),
-    )(tile, sens, krig_pilot, medium)
+        compiler_params=pltpu.CompilerParams(vmem_limit_bytes=24 * 2**20),
+    )(tile, in_hbm(sens), krig_pilot, share)
 
     half = 2 * OBS
     arrived = crossed(jnp.concatenate([send[:half] + swapped(swap), send[half:]], axis=0))
@@ -417,7 +497,7 @@
 
 def solution(mesh):
     return jax.shard_map(
-        shards,
+        local,
         mesh=mesh,
         in_specs=(
             P("obs", None, "grid", None),

time: 76.4 us -> 91.6 us (1.20)
  the two profiles are of different devices: /device:TPU:199 before, /device:TPU:207 now
where the time goes in v3:
time: 91.6 us; the launch traced here: 91.1 us
  starting transfers between devices  35.4 us (39%)
  Pallas kernels  34 us (37%)
  waiting for transfers between devices  20.9 us (23%)
    pallas_call x1, Pallas kernels, local(): pl.pallas_call(krig_kernel, out_shape=(piece, sds((4 * OBS, P_DEV), F32),...  21.7 us
    ppermute x3, starting transfers between devices, crossed(): return lax.ppermute(block, 'grid', pairs)  12.7 us
    all_to_all x2, starting transfers between devices, gathered(): return lax.all_to_all(copies, axis, 0, 0, tiled=False)  12.4 us
    ppermute x4, starting transfers between devices, swapped(): return lax.ppermute(block, 'grid', [(i, i ^ 1) for i in range(count)])  10.3 us
    ppermute x3, waiting for transfers between devices, crossed(): return lax.ppermute(block, 'grid', pairs)  10.1 us
    all_to_all x2, waiting for transfers between devices, gathered(): return lax.all_to_all(copies, axis, 0, 0, tiled=False)  8.46 us
    pallas_call x1, Pallas kernels, local(): pl.pallas_call(stencil_kernel, out_shape=pltpu.HBM((LAY * TX // 2, 2 * OB...  7.61 us
    ppermute x4, waiting for transfers between devices, swapped(): return lax.ppermute(block, 'grid', [(i, i ^ 1) for i in range(count)])  2.35 us
  transfers between devices with their start and end apart: 9, of which 6 were waited for; matrix products, arithmetic and copies ran while one was open for 0% of the time, Pallas kernels for 12%

profile of v3, /device:TPU:207, one launch (start us, length us, event | category | flops | bytes accessed | tf_op | source)
XLA Modules:
  0.0 91.1 jit_solution(3504069905697547702)
XLA Ops:
  0.0 0.0 copy-start
  0.0 0.0 copy-start.2
  0.0 1.8 %shard_map.92 = (f32[8,4,16,128]{3,2,1,0:T(8,128)}, f32[8,4,16,128]{3,2,1,0:T(8,128)}) custom-call(f32[2,1,16,128]{3,2,1,0:T(8,128)} %cond_ref.1, f32[1,16,128]{2,1,0:T(8,128)} %storage_ref.1, f32[1,16,128]{2,1,0:T(8,128)} %head_ref.1, f32[4,1,16,128]{3,2,1,0:T(8,128)} %krig_ref.1), custom_call_target="tpu_custom_call" | custom-call | tf_op jit(solution)/shard_map/pallas_call | solution.py:417
  1.8 7.0 %all-to-all-start = ((f32[8,4,16,128]{3,2,1,0:T(8,128)}), f32[8,4,16,128]{3,2,1,0:T(8,128)S(1)}, u32[]{:S(2)}, u32[]{:S(2)}) async-start(f32[8,4,16,128]{3,2,1,0:T(8,128)} %get-tuple-element.19), calls=%async_computation | async-start | bytes 524288 | tf_op jit(solution)/shard_map/all_to_all | solution.py:399
  8.8 8.5 %all-to-all-done.med_ref = f32[8,4,16,128]{3,2,1,0:T(8,128)S(1)} async-done(((f32[8,4,16,128]{3,2,1,0:T(8,128)}), f32[8,4,16,128]{3,2,1,0:T(8,128)S(1)}, u32[]{:S(2)}, u32[]{:S(2)}) %all-to-all-start) | async-done | bytes 262176 | tf_op jit(solution)/shard_map/all_to_all | solution.py:399
  17.2 5.4 %all-to-all-start.1 = ((f32[8,4,16,128]{3,2,1,0:T(8,128)}), f32[8,4,16,128]{3,2,1,0:T(8,128)S(1)}, u32[]{:S(2)}, u32[]{:S(2)}) async-start(f32[8,4,16,128]{3,2,1,0:T(8,128)} %get-tuple-element.22), calls=%async_computation.1 | async-start | bytes 524288 | tf_op jit(solution)/shard_map/all_to_all | solution.py:399
  22.6 0.1 add_bitcast_fusion.tile_ref
  22.7 2.3 %shard_map.91 = (f32[8,16,32,128]{3,2,1,0:T(8,128)S(1)}, f32[8,3,32,128]{3,2,1,0:T(8,128)S(1)}, f32[8,3,32,128]{3,2,1,0:T(8,128)S(1)}) custom-call(s32[1,2]{1,0:T(1,128)S(1)} %add_bitcast_fusion.tile_ref, f32[32,8,16,128]{3,2,1,0:T(8,128)} %adj_ref.1), custom_call_target="tpu_custom_call" | custom-call | tf_op jit(solution)/shard_map/pallas_call | solution.py:432
  25.0 4.5 %collective-permute-start = (f32[8,3,32,128]{3,2,1,0:T(8,128)S(1)}, f32[8,3,32,128]{3,2,1,0:T(8,128)S(1)}, u32[]{:S(2)}, u32[]{:S(2)}) collective-permute-start(f32[8,3,32,128]{3,2,1,0:T(8,128)S(1)} %get-tuple-element.17), channel_id=1, source_target_pairs={{0,1},{1,0},{2,3},{3,2},{4,5},{5,4},{6,7},{7,6},{8,9},{9,8},{10,11... | collective-permute-start | bytes 1179656 | tf_op jit(solution)/shard_map/ppermute | solution.py:389
  29.5 5.0 %collective-permute-start.1 = (f32[8,3,32,128]{3,2,1,0:T(8,128)S(1)}, f32[8,3,32,128]{3,2,1,0:T(8,128)S(1)}, u32[]{:S(2)}, u32[]{:S(2)}) collective-permute-start(f32[8,3,32,128]{3,2,1,0:T(8,128)S(1)} %get-tuple-element.18), channel_id=1, source_target_pairs={{1,2},{2,1},{3,4},{4,3},{5,6},{6,5},{7,8},{8,7},{9,10},{10,9},{11,... | collective-permute-start | bytes 1179656 | tf_op jit(solution)/shard_map/ppermute | solution.py:395
  34.5 0.0 copy-done
  34.5 0.6 shard_map.93
  35.1 1.9 %collective-permute-start.2 = (f32[8,16,128]{2,1,0:T(8,128)S(1)}, f32[8,16,128]{2,1,0:T(8,128)S(1)}, u32[]{:S(2)}, u32[]{:S(2)}) collective-permute-start(f32[8,16,128]{2,1,0:T(8,128)S(1)} %get-tuple-element.20), channel_id=1, source_target_pairs={{0,1},{1,0},{2,3},{3,2},{4,5},{5,4},{6,7},{7,6},{8,9},{9,8},{10,11... | collective-permute-start | bytes 196616 | tf_op jit(solution)/shard_map/ppermute | solution.py:389
  37.1 3.9 %collective-permute-start.3 = (f32[8,16,128]{2,1,0:T(8,128)S(1)}, f32[8,16,128]{2,1,0:T(8,128)S(1)}, u32[]{:S(2)}, u32[]{:S(2)}) collective-permute-start(f32[8,16,128]{2,1,0:T(8,128)S(1)} %get-tuple-element.21), channel_id=1, source_target_pairs={{1,2},{2,1},{3,4},{4,3},{5,6},{6,5},{7,8},{8,7},{9,10},{10,9},{11,... | collective-permute-start | bytes 196616 | tf_op jit(solution)/shard_map/ppermute | solution.py:395
  40.9 0.0 collective-permute-done.pair_ref
  40.9 1.0 %collective-permute-done.1.other_ref = f32[8,3,32,128]{3,2,1,0:T(8,128)S(1)} collective-permute-done((f32[8,3,32,128]{3,2,1,0:T(8,128)S(1)}, f32[8,3,32,128]{3,2,1,0:T(8,128)S(1)}, u32[]{:S(2)}, u32[]{:S(2)}) %collective-permute-start.1) | collective-permute-done | bytes 393248 | tf_op jit(solution)/shard_map/ppermute | solution.py:395
  41.9 0.0 collective-permute-done.2.med_pair_ref
  41.9 4.0 %collective-permute-done.3.med_other_ref = f32[8,16,128]{2,1,0:T(8,128)S(1)} collective-permute-done((f32[8,16,128]{2,1,0:T(8,128)S(1)}, f32[8,16,128]{2,1,0:T(8,128)S(1)}, u32[]{:S(2)}, u32[]{:S(2)}) %collective-permute-start.3) | collective-permute-done | bytes 65568 | tf_op jit(solution)/shard_map/ppermute | solution.py:395
  46.0 0.0 copy-done.3
  46.0 0.0 copy-done.2
  46.0 0.0 copy-start.1
  46.0 7.6 %shard_map.94.far_ref = f32[64,64,256]{2,1,0:T(8,128)} custom-call(s32[1,2]{1,0:T(1,128)S(1)} %add_bitcast_fusion.tile_ref, f32[8,16,32,128]{3,2,1,0:T(8,128)S(1)} %get-tuple-element.16.turned_ref, f32[8,3,32,128]{3,2,1,0:T(8,128)S(1)} %collective-permute-done.pair_ref, f32[8,3,32,128]{3,2,1,0:T(8,128)S(1)} %collective-permute-done.1.other_ref, ...), custom_call_target="tpu_custom_call" | custom-call | tf_op jit(solution)/shard_map/pallas_call | solution.py:458
  53.6 0.0 all-to-all-done.1.weight_ref
  53.6 0.0 copy-done.1
  53.6 21.7 %shard_map.95 = (f32[64,128]{1,0:T(8,128)S(1)}, f32[128,128]{1,0:T(8,128)S(1)}, f32[64,128]{1,0:T(8,128)S(1)}, f32[64,128]{1,0:T(8,128)S(1)}) custom-call(s32[1,2]{1,0:T(1,128)S(1)} %add_bitcast_fusion.tile_ref, f32[64,64,256]{2,1,0:T(8,128)} %shard_map.94.far_ref, s32[4,8,16,128]{3,2,1,0:T(8,128)S(1)} %copy-done.1, ...), custom_call_target="tpu_custom_call" | custom-call | tf_op jit(solution)/shard_map/pallas_call | solution.py:477
  75.4 1.9 %collective-permute-start.4 = (f32[64,128]{1,0:T(8,128)S(1)}, f32[64,128]{1,0:T(8,128)S(1)}, u32[]{:S(2)}, u32[]{:S(2)}) collective-permute-start(f32[64,128]{1,0:T(8,128)S(1)} %get-tuple-element.25), channel_id=1, source_target_pairs={{0,1},{1,0},{2,3},{3,2},{4,5},{5,4},{6,7},{7,6},{8,9},{9,8},{10,11... | collective-permute-start | bytes 98312 | tf_op jit(solution)/shard_map/ppermute | solution.py:389
  77.3 1.2 %collective-permute-done.4 = f32[64,128]{1,0:T(8,128)S(1)} collective-permute-done((f32[64,128]{1,0:T(8,128)S(1)}, f32[64,128]{1,0:T(8,128)S(1)}, u32[]{:S(2)}, u32[]{:S(2)}) %collective-permute-start.4) | collective-permute-done | bytes 32800 | tf_op jit(solution)/shard_map/ppermute | solution.py:389
  78.5 3.9 %collective-permute-start.5 = (f32[128,128]{1,0:T(8,128)S(1)}, f32[128,128]{1,0:T(8,128)S(1)}, u32[]{:S(2)}, u32[]{:S(2)}) collective-permute-start(f32[128,128]{1,0:T(8,128)S(1)} %pad_maximum_fusion), channel_id=1, source_target_pairs={{1,2},{2,1},{3,4},{4,3},{5,6},{6,5},{7,8},{8,7},{9,10},{10,9},{11,... | collective-permute-start | bytes 196616 | tf_op jit(solution)/shard_map/ppermute | solution.py:395
  82.4 5.0 %collective-permute-done.5 = f32[128,128]{1,0:T(8,128)S(1)} collective-permute-done((f32[128,128]{1,0:T(8,128)S(1)}, f32[128,128]{1,0:T(8,128)S(1)}, u32[]{:S(2)}, u32[]{:S(2)}) %collective-permute-start.5) | collective-permute-done | bytes 65568 | tf_op jit(solution)/shard_map/ppermute | solution.py:395
  87.4 1.9 %collective-permute-start.6 = (f32[64,128]{1,0:T(8,128)S(1)}, f32[64,128]{1,0:T(8,128)S(1)}, u32[]{:S(2)}, u32[]{:S(2)}) collective-permute-start(f32[64,128]{1,0:T(8,128)S(1)} %slice_add_fusion), channel_id=1, source_target_pairs={{0,1},{1,0},{2,3},{3,2},{4,5},{5,4},{6,7},{7,6},{8,9},{9,8},{10,11... | collective-permute-start | bytes 98312 | tf_op jit(solution)/shard_map/ppermute | solution.py:389
  89.3 1.2 %collective-permute-done.6 = f32[64,128]{1,0:T(8,128)S(1)} collective-permute-done((f32[64,128]{1,0:T(8,128)S(1)}, f32[64,128]{1,0:T(8,128)S(1)}, u32[]{:S(2)}, u32[]{:S(2)}) %collective-permute-start.6) | collective-permute-done | bytes 32800 | tf_op jit(solution)/shard_map/ppermute | solution.py:389
  90.5 0.6 fusion
  (4 shorter events, 0.0 us)
Async XLA Ops:
  0.0 34.5 %copy-start = (s32[8,16,128]{2,1,0:T(8,128)S(1)}, s32[8,16,128]{2,1,0:T(8,128)}, u32[]{:S(2)}) copy-start(s32[8,16,128]{2,1,0:T(8,128)} %open_ref.3) | copy-start | bytes 196612
  0.0 46.0 %copy-start.3 = (f32[32,2]{0,1:T(2,128)S(1)}, f32[32,2]{0,1:T(2,128)}, u32[]{:S(2)}) copy-start(f32[32,2]{0,1:T(2,128)} %param.17) | copy-start | bytes 772
  0.0 46.0 %copy-start.2 = (s32[32,2]{0,1:T(2,128)S(1)}, s32[32,2]{0,1:T(2,128)}, u32[]{:S(2)}) copy-start(s32[32,2]{0,1:T(2,128)} %param.16) | copy-start | bytes 772
  1.8 15.5 %all-to-all-start = ((f32[8,4,16,128]{3,2,1,0:T(8,128)}), f32[8,4,16,128]{3,2,1,0:T(8,128)S(1)}, u32[]{:S(2)}, u32[]{:S(2)}) async-start(f32[8,4,16,128]{3,2,1,0:T(8,128)} %get-tuple-element.19), calls=%async_computation | async-start | bytes 524288 | tf_op jit(solution)/shard_map/all_to_all | solution.py:399
  17.2 36.4 %all-to-all-start.1 = ((f32[8,4,16,128]{3,2,1,0:T(8,128)}), f32[8,4,16,128]{3,2,1,0:T(8,128)S(1)}, u32[]{:S(2)}, u32[]{:S(2)}) async-start(f32[8,4,16,128]{3,2,1,0:T(8,128)} %get-tuple-element.22), calls=%async_computation.1 | async-start | bytes 524288 | tf_op jit(solution)/shard_map/all_to_all | solution.py:399
  25.0 16.0 %collective-permute-start = (f32[8,3,32,128]{3,2,1,0:T(8,128)S(1)}, f32[8,3,32,128]{3,2,1,0:T(8,128)S(1)}, u32[]{:S(2)}, u32[]{:S(2)}) collective-permute-start(f32[8,3,32,128]{3,2,1,0:T(8,128)S(1)} %get-tuple-element.17), channel_id=1, source_target_pairs={{0,1},{1,0},{2,3},{3,2},{4,5},{5,4},{6,7},{7,6},{8,9},{9,8},{10,11... | collective-permute-start | bytes 1179656 | tf_op jit(solution)/shard_map/ppermute | solution.py:389
  29.5 12.4 %collective-permute-start.1 = (f32[8,3,32,128]{3,2,1,0:T(8,128)S(1)}, f32[8,3,32,128]{3,2,1,0:T(8,128)S(1)}, u32[]{:S(2)}, u32[]{:S(2)}) collective-permute-start(f32[8,3,32,128]{3,2,1,0:T(8,128)S(1)} %get-tuple-element.18), channel_id=1, source_target_pairs={{1,2},{2,1},{3,4},{4,3},{5,6},{6,5},{7,8},{8,7},{9,10},{10,9},{11,... | collective-permute-start | bytes 1179656 | tf_op jit(solution)/shard_map/ppermute | solution.py:395
  35.1 6.8 %collective-permute-start.2 = (f32[8,16,128]{2,1,0:T(8,128)S(1)}, f32[8,16,128]{2,1,0:T(8,128)S(1)}, u32[]{:S(2)}, u32[]{:S(2)}) collective-permute-start(f32[8,16,128]{2,1,0:T(8,128)S(1)} %get-tuple-element.20), channel_id=1, source_target_pairs={{0,1},{1,0},{2,3},{3,2},{4,5},{5,4},{6,7},{7,6},{8,9},{9,8},{10,11... | collective-permute-start | bytes 196616 | tf_op jit(solution)/shard_map/ppermute | solution.py:389
  37.1 8.9 %collective-permute-start.3 = (f32[8,16,128]{2,1,0:T(8,128)S(1)}, f32[8,16,128]{2,1,0:T(8,128)S(1)}, u32[]{:S(2)}, u32[]{:S(2)}) collective-permute-start(f32[8,16,128]{2,1,0:T(8,128)S(1)} %get-tuple-element.21), channel_id=1, source_target_pairs={{1,2},{2,1},{3,4},{4,3},{5,6},{6,5},{7,8},{8,7},{9,10},{10,9},{11,... | collective-permute-start | bytes 196616 | tf_op jit(solution)/shard_map/ppermute | solution.py:395
  46.0 7.6 %copy-start.1 = (s32[4,8,16,128]{3,2,1,0:T(8,128)S(1)}, s32[4,8,16,128]{3,2,1,0:T(8,128)}, u32[]{:S(2)}) copy-start(s32[4,8,16,128]{3,2,1,0:T(8,128)} %pilot_ref.1) | copy-start | bytes 786436
  75.4 3.1 %collective-permute-start.4 = (f32[64,128]{1,0:T(8,128)S(1)}, f32[64,128]{1,0:T(8,128)S(1)}, u32[]{:S(2)}, u32[]{:S(2)}) collective-permute-start(f32[64,128]{1,0:T(8,128)S(1)} %get-tuple-element.25), channel_id=1, source_target_pairs={{0,1},{1,0},{2,3},{3,2},{4,5},{5,4},{6,7},{7,6},{8,9},{9,8},{10,11... | collective-permute-start | bytes 98312 | tf_op jit(solution)/shard_map/ppermute | solution.py:389
  78.5 8.9 %collective-permute-start.5 = (f32[128,128]{1,0:T(8,128)S(1)}, f32[128,128]{1,0:T(8,128)S(1)}, u32[]{:S(2)}, u32[]{:S(2)}) collective-permute-start(f32[128,128]{1,0:T(8,128)S(1)} %pad_maximum_fusion), channel_id=1, source_target_pairs={{1,2},{2,1},{3,4},{4,3},{5,6},{6,5},{7,8},{8,7},{9,10},{10,9},{11,... | collective-permute-start | bytes 196616 | tf_op jit(solution)/shard_map/ppermute | solution.py:395
  87.4 3.1 %collective-permute-start.6 = (f32[64,128]{1,0:T(8,128)S(1)}, f32[64,128]{1,0:T(8,128)S(1)}, u32[]{:S(2)}, u32[]{:S(2)}) collective-permute-start(f32[64,128]{1,0:T(8,128)S(1)} %slice_add_fusion), channel_id=1, source_target_pairs={{0,1},{1,0},{2,3},{3,2},{4,5},{5,4},{6,7},{7,6},{8,9},{9,8},{10,11... | collective-permute-start | bytes 98312 | tf_op jit(solution)/shard_map/ppermute | solution.py:389

commit v4 on v3

--- a/solution.py
+++ b/solution.py
@@ -28,9 +28,7 @@
 HBM = pl.BlockSpec(memory_space=pltpu.HBM)
 
 
-def spread_kernel(
-    cond_ref, storage_ref, head_ref, krig_ref, med_ref, share_ref, own_ref, in_ref, out_ref
-):
+def spread_kernel(cond_ref, storage_ref, head_ref, krig_ref, med_ref, own_ref, in_ref, out_ref):
     parts = (
         (cond_ref.at[:, 0], own_ref.at[pl.ds(0, 2)]),
         (storage_ref, own_ref.at[pl.ds(2, 1)]),
@@ -44,14 +42,10 @@
         load.start()
     for load in loads:
         load.wait()
-    stores = []
-    for layer in range(LAY):
-        for i, ref in enumerate((med_ref, share_ref)):
-            stores.append(
-                pltpu.make_async_copy(
-                    own_ref.at[pl.ds(4 * i, 4)], ref.at[layer], out_ref.at[2 * layer + i]
-                )
-            )
+    stores = [
+        pltpu.make_async_copy(own_ref, med_ref.at[layer], out_ref.at[layer])
+        for layer in range(LAY)
+    ]
     for store in stores:
         store.start()
     for store in stores:
@@ -112,15 +106,13 @@
     med_other_ref,
     cell_ref,
     weight_ref,
-    sens_ref,
+    out_ref,
     ext_ref,
     coef_ref,
     grad_ref,
     halo_ref,
     one_ref,
     two_ref,
-    out_ref,
-    sem_ref,
 ):
     tile = tile_ref[0, 0]
     n_tiles = tile_ref[0, 1]
@@ -267,10 +259,6 @@
     sweep(start, one_ref, 2)
     sweep(lambda layer, j: one_ref[layer, j], two_ref, 1)
 
-    def store(layer):
-        part = pl.ds(layer * (TX // 2), TX // 2)
-        return pltpu.make_async_copy(out_ref.at[part], sens_ref.at[part], sem_ref.at[layer])
-
     def sense(layer, carry):
         down = jnp.maximum(layer - 1, 0)
         up = jnp.minimum(layer + 1, LAY - 1)
@@ -287,30 +275,20 @@
             half = pl.ds((x % 2) * TY, TY)
             out_ref[chunk, pl.ds(0, OBS), half] = horiz
             out_ref[chunk, pl.ds(OBS, OBS), half] = vert
-        store(layer).start()
         return carry
 
     lax.fori_loop(0, LAY, sense, 0)
-    for layer in range(LAY):
-        store(layer).wait()
-
-
-def krig_kernel(tile_ref, far_ref, pilot_ref, weight_ref, *rest):
-    swap_ref, send_ref, late_ref, own_ref, index_ref, share_ref, total_ref, sens_ref, sem_ref = rest
-
-    def fetch(chunk):
-        part = pl.ds(chunk * (KX // 2), KX // 2)
-        return pltpu.make_async_copy(far_ref.at[part], sens_ref.at[part], sem_ref.at[chunk])
-
-    for chunk in range(LAY * TX // KX):
-        fetch(chunk).start()
+
+
+def krig_kernel(tile_ref, sens_ref, pilot_ref, med_ref, *rest):
+    swap_ref, send_ref, late_ref, own_ref, index_ref, share_ref, total_ref = rest
     tile = tile_ref[0, 0]
     base = (tile - RADIUS) * P_DEV
     chunks = LAY * TX // KX
 
     for layer in range(LAY):
         index = [pilot_ref[k, layer] - base for k in range(NK)]
-        share = [weight_ref[layer, k] for k in range(NK)]
+        share = [med_ref[layer, 4 + k] for k in range(NK)]
         for k in range(1, NK):
             for j in range(k):
                 same = index[j] == index[k]
@@ -352,7 +330,6 @@
                 uppers.append(upper)
                 lowers.append(lower)
             columns.append(jnp.concatenate(uppers + lowers, axis=0))
-        fetch(chunk).wait()
         sens = []
         for q in range(KX // 2):
             sens.append(jnp.concatenate(split(sens_ref[chunk * (KX // 2) + q]), axis=0))
@@ -413,20 +390,20 @@
     sds = jax.ShapeDtypeStruct
     tile = jnp.stack([lax.axis_index("grid"), jnp.int32(lax.axis_size("grid"))]).reshape(1, 2)
 
-    copies = pltpu.HBM((LAY, 4, TX, TY), F32)
-    med_copies, share_copies = pl.pallas_call(
+    copies = pltpu.HBM((LAY, 4 + NK, TX, TY), F32)
+    copies = pl.pallas_call(
         spread_kernel,
-        out_shape=(copies, copies),
+        out_shape=copies,
         in_specs=[HBM] * 4,
-        out_specs=(HBM, HBM),
+        out_specs=HBM,
         scratch_shapes=[
             pltpu.VMEM((4 + NK, TX, TY), F32),
             pltpu.SemaphoreType.DMA((4,)),
-            pltpu.SemaphoreType.DMA((2 * LAY,)),
+            pltpu.SemaphoreType.DMA((LAY,)),
         ],
         compiler_params=pltpu.CompilerParams(vmem_limit_bytes=4 * 2**20),
     )(*map(in_hbm, (conductance, storage, head, krig_weight)))
-    medium = gathered(med_copies, "obs")
+    medium = gathered(copies, "obs")
 
     edge = sds((LAY, HALO, OBS, TY), F32)
     turned, pair, other = pl.pallas_call(
@@ -453,13 +430,12 @@
     )(tile, medium, layer_open)
     med_other = crossed(med_other)
     med_pair = swapped(med_pair)
-    share = gathered(share_copies, "obs")
 
     sens = pl.pallas_call(
         stencil_kernel,
-        out_shape=pltpu.HBM((LAY * TX // 2, 2 * OBS, 2 * TY), F32),
+        out_shape=sds((LAY * TX // 2, 2 * OBS, 2 * TY), F32),
         in_specs=[SMEM] + [VMEM] * 9,
-        out_specs=HBM,
+        out_specs=VMEM,
         scratch_shapes=[
             pltpu.VMEM((5, LAY, EXT, TY), F32),
             pltpu.VMEM((7, LAY, EXT, TY), F32),
@@ -467,27 +443,34 @@
             pltpu.VMEM((LAY, 2 * HALO, OBS, TY), F32),
             pltpu.VMEM((LAY, TX + 4, OBS, TY), F32),
             pltpu.VMEM((LAY, TX + 2, OBS, TY), F32),
-            pltpu.VMEM((LAY * TX // 2, 2 * OBS, 2 * TY), F32),
-            pltpu.SemaphoreType.DMA((LAY,)),
         ],
         compiler_params=pltpu.CompilerParams(vmem_limit_bytes=24 * 2**20),
-    )(tile, turned, pair, other, medium, layer_open, med_pair, med_other, obs_cell.T, obs_weight.T)
+    )(
+        tile,
+        turned,
+        pair,
+        other,
+        medium,
+        layer_open,
+        med_pair,
+        med_other,
+        obs_cell.T,
+        obs_weight.T,
+    )
 
     piece = sds((2 * OBS, P_DEV), F32)
     swap, send, late, owned = pl.pallas_call(
         krig_kernel,
         out_shape=(piece, sds((4 * OBS, P_DEV), F32), piece, piece),
-        in_specs=[SMEM, HBM, VMEM, VMEM],
+        in_specs=[SMEM] + [VMEM] * 3,
         out_specs=(VMEM,) * 4,
         scratch_shapes=[
             pltpu.VMEM((NK, LAY * TX, TY), jnp.int32),
             pltpu.VMEM((NK, LAY * TX, TY), F32),
             pltpu.VMEM((2 * SPAN, 4 * OBS), F32),
-            pltpu.VMEM((LAY * TX // 2, 2 * OBS, 2 * TY), F32),
-            pltpu.SemaphoreType.DMA((LAY * TX // KX,)),
         ],
         compiler_params=pltpu.CompilerParams(vmem_limit_bytes=24 * 2**20),
-    )(tile, in_hbm(sens), krig_pilot, share)
+    )(tile, sens, krig_pilot, medium)
 
     half = 2 * OBS
     arrived = crossed(jnp.concatenate([send[:half] + swapped(swap), send[half:]], axis=0))

time: 91.6 us -> 76.7 us (0.84)
  the two profiles are of different devices: /device:TPU:207 before, /device:TPU:199 now
where the time goes in v4:
time: 76.7 us; the launch traced here: 76.3 us
  starting transfers between devices  31 us (40%)
  Pallas kernels  27.6 us (36%)
  waiting for transfers between devices  16.8 us (22%)
    pallas_call x1, Pallas kernels, local(): pl.pallas_call(krig_kernel, out_shape=(piece, sds((4 * OBS, P_DEV), F32),...  15.2 us
    ppermute x3, starting transfers between devices, crossed(): return lax.ppermute(block, 'grid', pairs)  15.1 us
    ppermute x4, starting transfers between devices, swapped(): return lax.ppermute(block, 'grid', [(i, i ^ 1) for i in range(count)])  9.09 us
    ppermute x3, waiting for transfers between devices, crossed(): return lax.ppermute(block, 'grid', pairs)  7.71 us
    pallas_call x1, Pallas kernels, local(): pl.pallas_call(stencil_kernel, out_shape=sds((LAY * TX // 2, 2 * OBS, 2 *...  6.88 us
    all_to_all x1, starting transfers between devices, gathered(): return lax.all_to_all(copies, axis, 0, 0, tiled=False)  6.83 us
    all_to_all x1, waiting for transfers between devices, gathered(): return lax.all_to_all(copies, axis, 0, 0, tiled=False)  6.78 us
    pallas_call x1, Pallas kernels, local(): pl.pallas_call(turn_kernel, out_shape=(sds((LAY, TX, OBS, TY), F32), edge...  3.19 us
  transfers between devices with their start and end apart: 8, of which 5 were waited for; matrix products, arithmetic and copies ran while one was open for 0% of the time, Pallas kernels for 5%

profile of v4, /device:TPU:199, one launch (start us, length us, event | category | flops | bytes accessed | tf_op | source)
XLA Modules:
  0.0 76.3 jit_solution(12103196139555003169)
XLA Ops:
  0.0 0.0 copy-start
  0.0 0.0 copy-start.3
  0.0 0.0 copy-start.2
  0.0 1.7 %shard_map.92 = f32[8,8,16,128]{3,2,1,0:T(8,128)} custom-call(f32[2,1,16,128]{3,2,1,0:T(8,128)} %cond_ref.1, f32[1,16,128]{2,1,0:T(8,128)} %storage_ref.1, f32[1,16,128]{2,1,0:T(8,128)} %head_ref.1, f32[4,1,16,128]{3,2,1,0:T(8,128)} %krig_ref.1), custom_call_target="tpu_custom_call" | custom-call | tf_op jit(solution)/shard_map/pallas_call | solution.py:394
  1.8 6.8 %all-to-all-start = ((f32[8,8,16,128]{3,2,1,0:T(8,128)}), f32[8,8,16,128]{3,2,1,0:T(8,128)S(1)}, u32[]{:S(2)}, u32[]{:S(2)}) async-start(f32[8,8,16,128]{3,2,1,0:T(8,128)} %shard_map.92), calls=%async_computation | async-start | bytes 1048576 | tf_op jit(solution)/shard_map/all_to_all | solution.py:376
  8.6 0.1 add_bitcast_fusion.tile_ref
  8.7 3.2 %shard_map.91 = (f32[8,16,32,128]{3,2,1,0:T(8,128)S(1)}, f32[8,3,32,128]{3,2,1,0:T(8,128)}, f32[8,3,32,128]{3,2,1,0:T(8,128)}) custom-call(s32[1,2]{1,0:T(1,128)S(1)} %add_bitcast_fusion.tile_ref, f32[32,8,16,128]{3,2,1,0:T(8,128)} %adj_ref.1), custom_call_target="tpu_custom_call" | custom-call | tf_op jit(solution)/shard_map/pallas_call | solution.py:409
  11.9 2.9 %collective-permute-start = (f32[8,3,32,128]{3,2,1,0:T(8,128)}, f32[8,3,32,128]{3,2,1,0:T(8,128)S(1)}, u32[]{:S(2)}, u32[]{:S(2)}) collective-permute-start(f32[8,3,32,128]{3,2,1,0:T(8,128)} %get-tuple-element.15), channel_id=1, source_target_pairs={{0,1},{1,0},{2,3},{3,2},{4,5},{5,4},{6,7},{7,6},{8,9},{9,8},{10,11... | collective-permute-start | bytes 1179656 | tf_op jit(solution)/shard_map/ppermute | solution.py:366
  14.7 5.0 %collective-permute-start.1 = (f32[8,3,32,128]{3,2,1,0:T(8,128)}, f32[8,3,32,128]{3,2,1,0:T(8,128)S(1)}, u32[]{:S(2)}, u32[]{:S(2)}) collective-permute-start(f32[8,3,32,128]{3,2,1,0:T(8,128)} %get-tuple-element.16), channel_id=1, source_target_pairs={{1,2},{2,1},{3,4},{4,3},{5,6},{6,5},{7,8},{8,7},{9,10},{10,9},{11,... | collective-permute-start | bytes 1179656 | tf_op jit(solution)/shard_map/ppermute | solution.py:372
  19.8 6.8 %all-to-all-done.med_ref = f32[8,8,16,128]{3,2,1,0:T(8,128)S(1)} async-done(((f32[8,8,16,128]{3,2,1,0:T(8,128)}), f32[8,8,16,128]{3,2,1,0:T(8,128)S(1)}, u32[]{:S(2)}, u32[]{:S(2)}) %all-to-all-start) | async-done | bytes 524320 | tf_op jit(solution)/shard_map/all_to_all | solution.py:376
  26.5 0.0 copy-done
  26.5 0.6 shard_map.93
  27.1 2.4 %collective-permute-start.2 = (f32[8,16,128]{2,1,0:T(8,128)S(1)}, f32[8,16,128]{2,1,0:T(8,128)S(1)}, u32[]{:S(2)}, u32[]{:S(2)}) collective-permute-start(f32[8,16,128]{2,1,0:T(8,128)S(1)} %get-tuple-element.17), channel_id=1, source_target_pairs={{0,1},{1,0},{2,3},{3,2},{4,5},{5,4},{6,7},{7,6},{8,9},{9,8},{10,11... | collective-permute-start | bytes 196616 | tf_op jit(solution)/shard_map/ppermute | solution.py:366
  29.5 5.0 %collective-permute-start.3 = (f32[8,16,128]{2,1,0:T(8,128)S(1)}, f32[8,16,128]{2,1,0:T(8,128)S(1)}, u32[]{:S(2)}, u32[]{:S(2)}) collective-permute-start(f32[8,16,128]{2,1,0:T(8,128)S(1)} %get-tuple-element.18), channel_id=1, source_target_pairs={{1,2},{2,1},{3,4},{4,3},{5,6},{6,5},{7,8},{8,7},{9,10},{10,9},{11,... | collective-permute-start | bytes 196616 | tf_op jit(solution)/shard_map/ppermute | solution.py:372
  34.6 0.0 collective-permute-done.pair_ref
  34.6 0.0 collective-permute-done.1.other_ref
  34.6 0.0 collective-permute-done.2.med_pair_ref
  34.6 3.8 %collective-permute-done.3.med_other_ref = f32[8,16,128]{2,1,0:T(8,128)S(1)} collective-permute-done((f32[8,16,128]{2,1,0:T(8,128)S(1)}, f32[8,16,128]{2,1,0:T(8,128)S(1)}, u32[]{:S(2)}, u32[]{:S(2)}) %collective-permute-start.3) | collective-permute-done | bytes 65568 | tf_op jit(solution)/shard_map/ppermute | solution.py:372
  38.4 0.0 copy-done.3
  38.5 0.0 copy-done.2
  38.5 0.0 copy-start.1
  38.5 6.9 %shard_map.94.sens_ref = f32[64,64,256]{2,1,0:T(8,128)S(1)} custom-call(s32[1,2]{1,0:T(1,128)S(1)} %add_bitcast_fusion.tile_ref, f32[8,16,32,128]{3,2,1,0:T(8,128)S(1)} %get-tuple-element.14.turned_ref, f32[8,3,32,128]{3,2,1,0:T(8,128)S(1)} %collective-permute-done.pair_ref, f32[8,3,32,128]{3,2,1,0:T(8,128)S(1)} %collective-permute-done.1.other_ref, ...), custom_call_target="tpu_custom_call" | custom-call | tf_op jit(solution)/shard_map/pallas_call | solution.py:434
  45.3 0.0 copy-done.1
  45.4 15.2 %shard_map.95 = (f32[64,128]{1,0:T(8,128)S(1)}, f32[128,128]{1,0:T(8,128)S(1)}, f32[64,128]{1,0:T(8,128)S(1)}, f32[64,128]{1,0:T(8,128)S(1)}) custom-call(s32[1,2]{1,0:T(1,128)S(1)} %add_bitcast_fusion.tile_ref, f32[64,64,256]{2,1,0:T(8,128)S(1)} %shard_map.94.sens_ref, s32[4,8,16,128]{3,2,1,0:T(8,128)S(1)} %copy-done.1, ...), custom_call_target="tpu_custom_call" | custom-call | tf_op jit(solution)/shard_map/pallas_call | solution.py:462
  60.6 1.9 %collective-permute-start.4 = (f32[64,128]{1,0:T(8,128)S(1)}, f32[64,128]{1,0:T(8,128)S(1)}, u32[]{:S(2)}, u32[]{:S(2)}) collective-permute-start(f32[64,128]{1,0:T(8,128)S(1)} %get-tuple-element.21), channel_id=1, source_target_pairs={{0,1},{1,0},{2,3},{3,2},{4,5},{5,4},{6,7},{7,6},{8,9},{9,8},{10,11... | collective-permute-start | bytes 98312 | tf_op jit(solution)/shard_map/ppermute | solution.py:366
  62.5 1.2 %collective-permute-done.4 = f32[64,128]{1,0:T(8,128)S(1)} collective-permute-done((f32[64,128]{1,0:T(8,128)S(1)}, f32[64,128]{1,0:T(8,128)S(1)}, u32[]{:S(2)}, u32[]{:S(2)}) %collective-permute-start.4) | collective-permute-done | bytes 32800 | tf_op jit(solution)/shard_map/ppermute | solution.py:366
  63.7 5.0 %collective-permute-start.5 = (f32[128,128]{1,0:T(8,128)S(1)}, f32[128,128]{1,0:T(8,128)S(1)}, u32[]{:S(2)}, u32[]{:S(2)}) collective-permute-start(f32[128,128]{1,0:T(8,128)S(1)} %pad_maximum_fusion), channel_id=1, source_target_pairs={{1,2},{2,1},{3,4},{4,3},{5,6},{6,5},{7,8},{8,7},{9,10},{10,9},{11,... | collective-permute-start | bytes 196616 | tf_op jit(solution)/shard_map/ppermute | solution.py:372
  68.7 3.9 %collective-permute-done.5 = f32[128,128]{1,0:T(8,128)S(1)} collective-permute-done((f32[128,128]{1,0:T(8,128)S(1)}, f32[128,128]{1,0:T(8,128)S(1)}, u32[]{:S(2)}, u32[]{:S(2)}) %collective-permute-start.5) | collective-permute-done | bytes 65568 | tf_op jit(solution)/shard_map/ppermute | solution.py:372
  72.6 1.9 %collective-permute-start.6 = (f32[64,128]{1,0:T(8,128)S(1)}, f32[64,128]{1,0:T(8,128)S(1)}, u32[]{:S(2)}, u32[]{:S(2)}) collective-permute-start(f32[64,128]{1,0:T(8,128)S(1)} %slice_add_fusion), channel_id=1, source_target_pairs={{0,1},{1,0},{2,3},{3,2},{4,5},{5,4},{6,7},{7,6},{8,9},{9,8},{10,11... | collective-permute-start | bytes 98312 | tf_op jit(solution)/shard_map/ppermute | solution.py:366
  74.5 1.2 %collective-permute-done.6 = f32[64,128]{1,0:T(8,128)S(1)} collective-permute-done((f32[64,128]{1,0:T(8,128)S(1)}, f32[64,128]{1,0:T(8,128)S(1)}, u32[]{:S(2)}, u32[]{:S(2)}) %collective-permute-start.6) | collective-permute-done | bytes 32800 | tf_op jit(solution)/shard_map/ppermute | solution.py:366
  75.7 0.6 fusion
  (3 shorter events, 0.0 us)
Async XLA Ops:
  0.0 26.5 %copy-start = (s32[8,16,128]{2,1,0:T(8,128)S(1)}, s32[8,16,128]{2,1,0:T(8,128)}, u32[]{:S(2)}) copy-start(s32[8,16,128]{2,1,0:T(8,128)} %open_ref.3) | copy-start | bytes 196612
  0.0 38.4 %copy-start.3 = (f32[32,2]{0,1:T(2,128)S(1)}, f32[32,2]{0,1:T(2,128)}, u32[]{:S(2)}) copy-start(f32[32,2]{0,1:T(2,128)} %param.17) | copy-start | bytes 772
  0.0 38.4 %copy-start.2 = (s32[32,2]{0,1:T(2,128)S(1)}, s32[32,2]{0,1:T(2,128)}, u32[]{:S(2)}) copy-start(s32[32,2]{0,1:T(2,128)} %param.16) | copy-start | bytes 772
  1.8 24.8 %all-to-all-start = ((f32[8,8,16,128]{3,2,1,0:T(8,128)}), f32[8,8,16,128]{3,2,1,0:T(8,128)S(1)}, u32[]{:S(2)}, u32[]{:S(2)}) async-start(f32[8,8,16,128]{3,2,1,0:T(8,128)} %shard_map.92), calls=%async_computation | async-start | bytes 1048576 | tf_op jit(solution)/shard_map/all_to_all | solution.py:376
  11.9 22.7 %collective-permute-start = (f32[8,3,32,128]{3,2,1,0:T(8,128)}, f32[8,3,32,128]{3,2,1,0:T(8,128)S(1)}, u32[]{:S(2)}, u32[]{:S(2)}) collective-permute-start(f32[8,3,32,128]{3,2,1,0:T(8,128)} %get-tuple-element.15), channel_id=1, source_target_pairs={{0,1},{1,0},{2,3},{3,2},{4,5},{5,4},{6,7},{7,6},{8,9},{9,8},{10,11... | collective-permute-start | bytes 1179656 | tf_op jit(solution)/shard_map/ppermute | solution.py:366
  14.7 19.9 %collective-permute-start.1 = (f32[8,3,32,128]{3,2,1,0:T(8,128)}, f32[8,3,32,128]{3,2,1,0:T(8,128)S(1)}, u32[]{:S(2)}, u32[]{:S(2)}) collective-permute-start(f32[8,3,32,128]{3,2,1,0:T(8,128)} %get-tuple-element.16), channel_id=1, source_target_pairs={{1,2},{2,1},{3,4},{4,3},{5,6},{6,5},{7,8},{8,7},{9,10},{10,9},{11,... | collective-permute-start | bytes 1179656 | tf_op jit(solution)/shard_map/ppermute | solution.py:372
  27.1 7.5 %collective-permute-start.2 = (f32[8,16,128]{2,1,0:T(8,128)S(1)}, f32[8,16,128]{2,1,0:T(8,128)S(1)}, u32[]{:S(2)}, u32[]{:S(2)}) collective-permute-start(f32[8,16,128]{2,1,0:T(8,128)S(1)} %get-tuple-element.17), channel_id=1, source_target_pairs={{0,1},{1,0},{2,3},{3,2},{4,5},{5,4},{6,7},{7,6},{8,9},{9,8},{10,11... | collective-permute-start | bytes 196616 | tf_op jit(solution)/shard_map/ppermute | solution.py:366
  29.5 8.9 %collective-permute-start.3 = (f32[8,16,128]{2,1,0:T(8,128)S(1)}, f32[8,16,128]{2,1,0:T(8,128)S(1)}, u32[]{:S(2)}, u32[]{:S(2)}) collective-permute-start(f32[8,16,128]{2,1,0:T(8,128)S(1)} %get-tuple-element.18), channel_id=1, source_target_pairs={{1,2},{2,1},{3,4},{4,3},{5,6},{6,5},{7,8},{8,7},{9,10},{10,9},{11,... | collective-permute-start | bytes 196616 | tf_op jit(solution)/shard_map/ppermute | solution.py:372
  38.5 6.9 %copy-start.1 = (s32[4,8,16,128]{3,2,1,0:T(8,128)S(1)}, s32[4,8,16,128]{3,2,1,0:T(8,128)}, u32[]{:S(2)}) copy-start(s32[4,8,16,128]{3,2,1,0:T(8,128)} %pilot_ref.1) | copy-start | bytes 786436
  60.6 3.1 %collective-permute-start.4 = (f32[64,128]{1,0:T(8,128)S(1)}, f32[64,128]{1,0:T(8,128)S(1)}, u32[]{:S(2)}, u32[]{:S(2)}) collective-permute-start(f32[64,128]{1,0:T(8,128)S(1)} %get-tuple-element.21), channel_id=1, source_target_pairs={{0,1},{1,0},{2,3},{3,2},{4,5},{5,4},{6,7},{7,6},{8,9},{9,8},{10,11... | collective-permute-start | bytes 98312 | tf_op jit(solution)/shard_map/ppermute | solution.py:366
  63.7 8.9 %collective-permute-start.5 = (f32[128,128]{1,0:T(8,128)S(1)}, f32[128,128]{1,0:T(8,128)S(1)}, u32[]{:S(2)}, u32[]{:S(2)}) collective-permute-start(f32[128,128]{1,0:T(8,128)S(1)} %pad_maximum_fusion), channel_id=1, source_target_pairs={{1,2},{2,1},{3,4},{4,3},{5,6},{6,5},{7,8},{8,7},{9,10},{10,9},{11,... | collective-permute-start | bytes 196616 | tf_op jit(solution)/shard_map/ppermute | solution.py:372
  72.6 3.1 %collective-permute-start.6 = (f32[64,128]{1,0:T(8,128)S(1)}, f32[64,128]{1,0:T(8,128)S(1)}, u32[]{:S(2)}, u32[]{:S(2)}) collective-permute-start(f32[64,128]{1,0:T(8,128)S(1)} %slice_add_fusion), channel_id=1, source_target_pairs={{0,1},{1,0},{2,3},{3,2},{4,5},{5,4},{6,7},{7,6},{8,9},{9,8},{10,11... | collective-permute-start | bytes 98312 | tf_op jit(solution)/shard_map/ppermute | solution.py:366

commit v5 on v4

--- a/solution.py
+++ b/solution.py
@@ -28,28 +28,27 @@
 HBM = pl.BlockSpec(memory_space=pltpu.HBM)
 
 
-def spread_kernel(cond_ref, storage_ref, head_ref, krig_ref, med_ref, own_ref, in_ref, out_ref):
+def spread_kernel(cond_ref, storage_ref, head_ref, krig_ref, med_ref, sem_ref):
     parts = (
-        (cond_ref.at[:, 0], own_ref.at[pl.ds(0, 2)]),
-        (storage_ref, own_ref.at[pl.ds(2, 1)]),
-        (head_ref, own_ref.at[pl.ds(3, 1)]),
-        (krig_ref.at[:, 0], own_ref.at[pl.ds(4, NK)]),
+        (cond_ref.at[:, 0], 0, 2),
+        (storage_ref, 2, 1),
+        (head_ref, 3, 1),
+        (krig_ref.at[:, 0], 4, NK),
     )
-    loads = [
-        pltpu.make_async_copy(part, place, in_ref.at[i]) for i, (part, place) in enumerate(parts)
-    ]
-    for load in loads:
-        load.start()
-    for load in loads:
-        load.wait()
-    stores = [
-        pltpu.make_async_copy(own_ref, med_ref.at[layer], out_ref.at[layer])
-        for layer in range(LAY)
-    ]
-    for store in stores:
-        store.start()
-    for store in stores:
-        store.wait()
+    copies = []
+    for layer in range(LAY):
+        for i, (part, first, count) in enumerate(parts):
+            copies.append(
+                pltpu.make_async_copy(
+                    part,
+                    med_ref.at[layer, pl.ds(first, count)],
+                    sem_ref.at[len(parts) * layer + i],
+                )
+            )
+    for copy in copies:
+        copy.start()
+    for copy in copies:
+        copy.wait()
 
 
 def turn_kernel(tile_ref, adj_ref, turned_ref, pair_ref, other_ref, buf_ref, sem_ref):
@@ -95,24 +94,17 @@
         other_ref[layer, pl.ds(15, 1), :] = jnp.zeros((1, TY), F32)
 
 
-def stencil_kernel(
+def sweeper(
     tile_ref,
-    turned_ref,
-    pair_ref,
-    other_ref,
     med_ref,
     open_ref,
     med_pair_ref,
     med_other_ref,
     cell_ref,
     weight_ref,
-    out_ref,
     ext_ref,
     coef_ref,
     grad_ref,
-    halo_ref,
-    one_ref,
-    two_ref,
 ):
     tile = tile_ref[0, 0]
     n_tiles = tile_ref[0, 1]
@@ -132,18 +124,12 @@
             ext_ref[field, layer, pl.ds(OFF + TX, OFF), :] = fill
             own = med_ref[layer, field] if field < 4 else open_ref[layer].astype(F32)
             ext_ref[field, layer, pl.ds(OFF, TX), :] = own
+            if med_pair_ref is None:
+                continue
             pair = med_pair_ref[layer, pl.ds(field * HALO, HALO), :]
             other = med_other_ref[layer, pl.ds(field * HALO, HALO), :]
             ext_ref[field, layer, pl.ds(OFF - HALO, HALO), :] = jnp.where(odd == 1, pair, other)
             ext_ref[field, layer, pl.ds(OFF + TX, HALO), :] = jnp.where(odd == 1, other, pair)
-
-    def place(layer, carry):
-        for j in range(HALO):
-            halo_ref[layer, HALO * (1 - odd) + j] = pair_ref[layer, j]
-            halo_ref[layer, HALO * odd + j] = other_ref[layer, j]
-        return carry
-
-    lax.fori_loop(0, LAY, place, 0)
 
     def medium(field, layer):
         value = ext_ref[field, layer]
@@ -202,6 +188,8 @@
         for n, value in enumerate((fxm, fxp, fym, fyp, fzm, fzp)):
             coef_ref[n, layer] = value * scale
         coef_ref[6, layer] = scale
+        if grad_ref is None:
+            continue
         grad_ref[0, layer] = gxm * before * (head - below(head))
         grad_ref[1, layer] = gxp * both * (head - above(head))
         grad_ref[2, layer] = gym * has_west * (head - west(head))
@@ -226,38 +214,109 @@
     def rows(ref, n, layer, x):
         return jnp.broadcast_to(ref[n, layer, pl.ds(x + OFF, 1), :], (OBS, TY))
 
-    def start(layer, j):
-        if j < HALO:
-            return halo_ref[layer, j]
-        if j < HALO + TX:
-            return turned_ref[layer, j - HALO]
-        return halo_ref[layer, j - TX]
-
-    def sweep(src, dst_ref, margin):
+    def sweep(src, columns, store):
         def body(layer, carry):
             down = jnp.maximum(layer - 1, 0)
             up = jnp.minimum(layer + 1, LAY - 1)
-            for x in range(-margin, TX + margin):
-                j = x + margin + 1
-                mid = src(layer, j)
+            for x in columns:
+                mid = src(layer, x)
                 base = (layer * whole_x + tile * TX + x) * TY
                 source = jnp.where(target[0] == base, amount[0], 0.0) + jnp.where(
                     target[1] == base, amount[1], 0.0
                 )
                 value = (1.0 - OMEGA) * mid + rows(coef_ref, 6, layer, x) * source
-                value += rows(coef_ref, 0, layer, x) * src(layer, j - 1)
-                value += rows(coef_ref, 1, layer, x) * src(layer, j + 1)
+                value += rows(coef_ref, 0, layer, x) * src(layer, x - 1)
+                value += rows(coef_ref, 1, layer, x) * src(layer, x + 1)
                 value += rows(coef_ref, 2, layer, x) * pltpu.roll(mid, 1, 1)
                 value += rows(coef_ref, 3, layer, x) * pltpu.roll(mid, TY - 1, 1)
-                value += rows(coef_ref, 4, layer, x) * src(down, j)
-                value += rows(coef_ref, 5, layer, x) * src(up, j)
-                dst_ref[layer, j - 1] = value
+                value += rows(coef_ref, 4, layer, x) * src(down, x)
+                value += rows(coef_ref, 5, layer, x) * src(up, x)
+                store(layer, x, value)
             return carry
 
         lax.fori_loop(0, LAY, body, 0)
 
-    sweep(start, one_ref, 2)
-    sweep(lambda layer, j: one_ref[layer, j], two_ref, 1)
+    return rows, sweep
+
+
+def interior_kernel(
+    tile_ref, turned_ref, med_ref, open_ref, cell_ref, weight_ref, out_ref, ext_ref, coef_ref
+):
+    _, sweep = sweeper(
+        tile_ref, med_ref, open_ref, None, None, cell_ref, weight_ref, ext_ref, coef_ref, None
+    )
+
+    def store(layer, x, value):
+        out_ref[layer, x - 1] = value
+
+    sweep(lambda layer, x: turned_ref[layer, x], range(1, TX - 1), store)
+
+
+def stencil_kernel(
+    tile_ref,
+    turned_ref,
+    pair_ref,
+    other_ref,
+    med_ref,
+    open_ref,
+    med_pair_ref,
+    med_other_ref,
+    cell_ref,
+    weight_ref,
+    inner_ref,
+    out_ref,
+    ext_ref,
+    coef_ref,
+    grad_ref,
+    halo_ref,
+    rim_ref,
+    two_ref,
+):
+    odd = tile_ref[0, 0] % 2
+    rows, sweep = sweeper(
+        tile_ref,
+        med_ref,
+        open_ref,
+        med_pair_ref,
+        med_other_ref,
+        cell_ref,
+        weight_ref,
+        ext_ref,
+        coef_ref,
+        grad_ref,
+    )
+
+    def place(layer, carry):
+        for j in range(HALO):
+            halo_ref[layer, HALO * (1 - odd) + j] = pair_ref[layer, j]
+            halo_ref[layer, HALO * odd + j] = other_ref[layer, j]
+        return carry
+
+    lax.fori_loop(0, LAY, place, 0)
+
+    def start(layer, x):
+        if x < 0:
+            return halo_ref[layer, x + HALO]
+        if x < TX:
+            return turned_ref[layer, x]
+        return halo_ref[layer, x + HALO - TX]
+
+    def rim(x):
+        return x + 2 if x < 1 else x - TX + 4
+
+    def one(layer, x):
+        if 1 <= x < TX - 1:
+            return inner_ref[layer, x - 1]
+        return rim_ref[layer, rim(x)]
+
+    def store_rim(layer, x, value):
+        rim_ref[layer, rim(x)] = value
+
+    def store_two(layer, x, value):
+        two_ref[layer, x + 1] = value
+
+    sweep(start, (-2, -1, 0, TX - 1, TX, TX + 1), store_rim)
+    sweep(one, range(-1, TX + 1), store_two)
 
     def sense(layer, carry):
         down = jnp.maximum(layer - 1, 0)
@@ -396,11 +455,7 @@
         out_shape=copies,
         in_specs=[HBM] * 4,
         out_specs=HBM,
-        scratch_shapes=[
-            pltpu.VMEM((4 + NK, TX, TY), F32),
-            pltpu.SemaphoreType.DMA((4,)),
-            pltpu.SemaphoreType.DMA((LAY,)),
-        ],
+        scratch_shapes=[pltpu.SemaphoreType.DMA((4 * LAY,))],
         compiler_params=pltpu.CompilerParams(vmem_limit_bytes=4 * 2**20),
     )(*map(in_hbm, (conductance, storage, head, krig_weight)))
     medium = gathered(copies, "obs")
@@ -431,17 +486,31 @@
     med_other = crossed(med_other)
     med_pair = swapped(med_pair)
 
+    cells = obs_cell.T
+    amounts = obs_weight.T
+    inner = pl.pallas_call(
+        interior_kernel,
+        out_shape=sds((LAY, TX - 2, OBS, TY), F32),
+        in_specs=[SMEM] + [VMEM] * 5,
+        out_specs=VMEM,
+        scratch_shapes=[
+            pltpu.VMEM((5, LAY, EXT, TY), F32),
+            pltpu.VMEM((7, LAY, EXT, TY), F32),
+        ],
+        compiler_params=pltpu.CompilerParams(vmem_limit_bytes=16 * 2**20),
+    )(tile, turned, medium, layer_open, cells, amounts)
+
     sens = pl.pallas_call(
         stencil_kernel,
         out_shape=sds((LAY * TX // 2, 2 * OBS, 2 * TY), F32),
-        in_specs=[SMEM] + [VMEM] * 9,
+        in_specs=[SMEM] + [VMEM] * 10,
         out_specs=VMEM,
         scratch_shapes=[
             pltpu.VMEM((5, LAY, EXT, TY), F32),
             pltpu.VMEM((7, LAY, EXT, TY), F32),
             pltpu.VMEM((6, LAY, EXT, TY), F32),
             pltpu.VMEM((LAY, 2 * HALO, OBS, TY), F32),
-            pltpu.VMEM((LAY, TX + 4, OBS, TY), F32),
+            pltpu.VMEM((LAY, 2 * HALO, OBS, TY), F32),
             pltpu.VMEM((LAY, TX + 2, OBS, TY), F32),
         ],
         compiler_params=pltpu.CompilerParams(vmem_limit_bytes=24 * 2**20),
@@ -454,8 +523,9 @@
         layer_open,
         med_pair,
         med_other,
-        obs_cell.T,
-        obs_weight.T,
+        cells,
+        amounts,
+        inner,
     )
 
     piece = sds((2 * OBS, P_DEV), F32)

time: 76.7 us -> 91 us (1.19)
  Pallas kernels: 27.6 us -> 44.3 us
  waiting for transfers between devices: 16.8 us -> 14.4 us
    pallas_call x1, Pallas kernels: 1.74 us -> 17.3 us  [local(): pl.pallas_call(spread_kernel, out_shape=copies, in_specs=[HBM] * 4, out_s...]
    ppermute x3, waiting for transfers between devices: 7.71 us -> 5.26 us  [crossed(): return lax.ppermute(block, 'grid', pairs)]
    pallas_call x0 -> x1, Pallas kernels: none -> 2.41 us  [local(): pl.pallas_call(interior_kernel, out_shape=sds((LAY, TX - 2, OBS, TY), F32...]
    pallas_call x1, Pallas kernels: 6.88 us -> 5.6 us  [local(): pl.pallas_call(stencil_kernel, out_shape=sds((LAY * TX // 2, 2 * OBS, 2 *...]
  transfers between devices with their start and end apart: 8 -> 8, of which waited for: 5 -> 5; matrix products, arithmetic and copies ran while one was open for 0% -> 0% of each run, Pallas kernels for 5% -> 7%
where the time goes in v5:
time: 91 us; the launch traced here: 90.6 us
  Pallas kernels  44.3 us (49%)
  starting transfers between devices  31 us (34%)
  waiting for transfers between devices  14.4 us (16%)
    pallas_call x1, Pallas kernels, local(): pl.pallas_call(spread_kernel, out_shape=copies, in_specs=[HBM] * 4, out_s...  17.3 us
    pallas_call x1, Pallas kernels, local(): pl.pallas_call(krig_kernel, out_shape=(piece, sds((4 * OBS, P_DEV), F32),...  15.3 us
    ppermute x3, starting transfers between devices, crossed(): return lax.ppermute(block, 'grid', pairs)  15.1 us
    ppermute x4, starting transfers between devices, swapped(): return lax.ppermute(block, 'grid', [(i, i ^ 1) for i in range(count)])  9.09 us
    all_to_all x1, starting transfers between devices, gathered(): return lax.all_to_all(copies, axis, 0, 0, tiled=False)  6.83 us
    all_to_all x1, waiting for transfers between devices, gathered(): return lax.all_to_all(copies, axis, 0, 0, tiled=False)  6.78 us
    pallas_call x1, Pallas kernels, local(): pl.pallas_call(stencil_kernel, out_shape=sds((LAY * TX // 2, 2 * OBS, 2 *...  5.6 us
    ppermute x3, waiting for transfers between devices, crossed(): return lax.ppermute(block, 'grid', pairs)  5.26 us
  transfers between devices with their start and end apart: 8, of which 5 were waited for; matrix products, arithmetic and copies ran while one was open for 0% of the time, Pallas kernels for 7%

profile of v5, /device:TPU:199, one launch (start us, length us, event | category | flops | bytes accessed | tf_op | source)
XLA Modules:
  0.0 90.6 jit_solution(441030363295709052)
XLA Ops:
  0.0 0.0 copy-start
  0.0 0.0 copy-start.3
  0.0 0.0 copy-start.2
  0.0 17.3 %shard_map.92 = f32[8,8,16,128]{3,2,1,0:T(8,128)} custom-call(f32[2,1,16,128]{3,2,1,0:T(8,128)} %cond_ref.1, f32[1,16,128]{2,1,0:T(8,128)} %storage_ref.1, f32[1,16,128]{2,1,0:T(8,128)} %head_ref.1, f32[4,1,16,128]{3,2,1,0:T(8,128)} %krig_ref.1), custom_call_target="tpu_custom_call" | custom-call | tf_op jit(solution)/shard_map/pallas_call | solution.py:453
  17.3 6.8 %all-to-all-start = ((f32[8,8,16,128]{3,2,1,0:T(8,128)}), f32[8,8,16,128]{3,2,1,0:T(8,128)S(1)}, u32[]{:S(2)}, u32[]{:S(2)}) async-start(f32[8,8,16,128]{3,2,1,0:T(8,128)} %shard_map.92), calls=%async_computation | async-start | bytes 1048576 | tf_op jit(solution)/shard_map/all_to_all | solution.py:435
  24.1 0.1 add_bitcast_fusion.tile_ref
  24.2 3.2 %shard_map.91 = (f32[8,16,32,128]{3,2,1,0:T(8,128)S(1)}, f32[8,3,32,128]{3,2,1,0:T(8,128)}, f32[8,3,32,128]{3,2,1,0:T(8,128)}) custom-call(s32[1,2]{1,0:T(1,128)S(1)} %add_bitcast_fusion.tile_ref, f32[32,8,16,128]{3,2,1,0:T(8,128)} %adj_ref.1), custom_call_target="tpu_custom_call" | custom-call | tf_op jit(solution)/shard_map/pallas_call | solution.py:464
  27.4 2.9 %collective-permute-start = (f32[8,3,32,128]{3,2,1,0:T(8,128)}, f32[8,3,32,128]{3,2,1,0:T(8,128)S(1)}, u32[]{:S(2)}, u32[]{:S(2)}) collective-permute-start(f32[8,3,32,128]{3,2,1,0:T(8,128)} %get-tuple-element.15), channel_id=1, source_target_pairs={{0,1},{1,0},{2,3},{3,2},{4,5},{5,4},{6,7},{7,6},{8,9},{9,8},{10,11... | collective-permute-start | bytes 1179656 | tf_op jit(solution)/shard_map/ppermute | solution.py:425
  30.3 5.0 %collective-permute-start.1 = (f32[8,3,32,128]{3,2,1,0:T(8,128)}, f32[8,3,32,128]{3,2,1,0:T(8,128)S(1)}, u32[]{:S(2)}, u32[]{:S(2)}) collective-permute-start(f32[8,3,32,128]{3,2,1,0:T(8,128)} %get-tuple-element.16), channel_id=1, source_target_pairs={{1,2},{2,1},{3,4},{4,3},{5,6},{6,5},{7,8},{8,7},{9,10},{10,9},{11,... | collective-permute-start | bytes 1179656 | tf_op jit(solution)/shard_map/ppermute | solution.py:431
  35.3 6.8 %all-to-all-done.med_ref = f32[8,8,16,128]{3,2,1,0:T(8,128)S(1)} async-done(((f32[8,8,16,128]{3,2,1,0:T(8,128)}), f32[8,8,16,128]{3,2,1,0:T(8,128)S(1)}, u32[]{:S(2)}, u32[]{:S(2)}) %all-to-all-start) | async-done | bytes 524320 | tf_op jit(solution)/shard_map/all_to_all | solution.py:435
  42.1 0.0 copy-done
  42.1 0.6 shard_map.93
  42.7 2.4 %collective-permute-start.2 = (f32[8,16,128]{2,1,0:T(8,128)S(1)}, f32[8,16,128]{2,1,0:T(8,128)S(1)}, u32[]{:S(2)}, u32[]{:S(2)}) collective-permute-start(f32[8,16,128]{2,1,0:T(8,128)S(1)} %get-tuple-element.17), channel_id=1, source_target_pairs={{0,1},{1,0},{2,3},{3,2},{4,5},{5,4},{6,7},{7,6},{8,9},{9,8},{10,11... | collective-permute-start | bytes 196616 | tf_op jit(solution)/shard_map/ppermute | solution.py:425
  45.1 5.0 %collective-permute-start.3 = (f32[8,16,128]{2,1,0:T(8,128)S(1)}, f32[8,16,128]{2,1,0:T(8,128)S(1)}, u32[]{:S(2)}, u32[]{:S(2)}) collective-permute-start(f32[8,16,128]{2,1,0:T(8,128)S(1)} %get-tuple-element.18), channel_id=1, source_target_pairs={{1,2},{2,1},{3,4},{4,3},{5,6},{6,5},{7,8},{8,7},{9,10},{10,9},{11,... | collective-permute-start | bytes 196616 | tf_op jit(solution)/shard_map/ppermute | solution.py:431
  50.1 0.0 copy-done.3
  50.1 0.0 copy-done.2
  50.1 2.4 %shard_map.94.inner_ref = f32[8,14,32,128]{3,2,1,0:T(8,128)S(1)} custom-call(s32[1,2]{1,0:T(1,128)S(1)} %add_bitcast_fusion.tile_ref, f32[8,16,32,128]{3,2,1,0:T(8,128)S(1)} %get-tuple-element.14.turned_ref, f32[8,8,16,128]{3,2,1,0:T(8,128)S(1)} %all-to-all-done.med_ref, s32[8,16,128]{2,1,0:T(8,128)S(1)} %copy-done, s32[2,32]{1,0:T(2,128)S(1)} %bitcast.6, ...), custom_call_target="tpu_custom_call" | custom-call | tf_op jit(solution)/shard_map/pallas_call | solution.py:491
  52.6 0.0 copy-start.1
  52.6 0.0 collective-permute-done.pair_ref
  52.6 0.0 collective-permute-done.1.other_ref
  52.6 0.0 collective-permute-done.2.med_pair_ref
  52.6 1.4 %collective-permute-done.3.med_other_ref = f32[8,16,128]{2,1,0:T(8,128)S(1)} collective-permute-done((f32[8,16,128]{2,1,0:T(8,128)S(1)}, f32[8,16,128]{2,1,0:T(8,128)S(1)}, u32[]{:S(2)}, u32[]{:S(2)}) %collective-permute-start.3) | collective-permute-done | bytes 65568 | tf_op jit(solution)/shard_map/ppermute | solution.py:431
  54.0 5.6 %shard_map.95.sens_ref = f32[64,64,256]{2,1,0:T(8,128)S(1)} custom-call(s32[1,2]{1,0:T(1,128)S(1)} %add_bitcast_fusion.tile_ref, f32[8,16,32,128]{3,2,1,0:T(8,128)S(1)} %get-tuple-element.14.turned_ref, f32[8,3,32,128]{3,2,1,0:T(8,128)S(1)} %collective-permute-done.pair_ref, f32[8,3,32,128]{3,2,1,0:T(8,128)S(1)} %collective-permute-done.1.other_ref, ...), custom_call_target="tpu_custom_call" | custom-call | tf_op jit(solution)/shard_map/pallas_call | solution.py:503
  59.6 0.0 copy-done.1
  59.6 15.3 %shard_map.96 = (f32[64,128]{1,0:T(8,128)S(1)}, f32[128,128]{1,0:T(8,128)S(1)}, f32[64,128]{1,0:T(8,128)S(1)}, f32[64,128]{1,0:T(8,128)S(1)}) custom-call(s32[1,2]{1,0:T(1,128)S(1)} %add_bitcast_fusion.tile_ref, f32[64,64,256]{2,1,0:T(8,128)S(1)} %shard_map.95.sens_ref, s32[4,8,16,128]{3,2,1,0:T(8,128)S(1)} %copy-done.1, ...), custom_call_target="tpu_custom_call" | custom-call | tf_op jit(solution)/shard_map/pallas_call | solution.py:532
  74.9 1.9 %collective-permute-start.4 = (f32[64,128]{1,0:T(8,128)S(1)}, f32[64,128]{1,0:T(8,128)S(1)}, u32[]{:S(2)}, u32[]{:S(2)}) collective-permute-start(f32[64,128]{1,0:T(8,128)S(1)} %get-tuple-element.21), channel_id=1, source_target_pairs={{0,1},{1,0},{2,3},{3,2},{4,5},{5,4},{6,7},{7,6},{8,9},{9,8},{10,11... | collective-permute-start | bytes 98312 | tf_op jit(solution)/shard_map/ppermute | solution.py:425
  76.8 1.2 %collective-permute-done.4 = f32[64,128]{1,0:T(8,128)S(1)} collective-permute-done((f32[64,128]{1,0:T(8,128)S(1)}, f32[64,128]{1,0:T(8,128)S(1)}, u32[]{:S(2)}, u32[]{:S(2)}) %collective-permute-start.4) | collective-permute-done | bytes 32800 | tf_op jit(solution)/shard_map/ppermute | solution.py:425
  78.0 5.0 %collective-permute-start.5 = (f32[128,128]{1,0:T(8,128)S(1)}, f32[128,128]{1,0:T(8,128)S(1)}, u32[]{:S(2)}, u32[]{:S(2)}) collective-permute-start(f32[128,128]{1,0:T(8,128)S(1)} %pad_maximum_fusion), channel_id=1, source_target_pairs={{1,2},{2,1},{3,4},{4,3},{5,6},{6,5},{7,8},{8,7},{9,10},{10,9},{11,... | collective-permute-start | bytes 196616 | tf_op jit(solution)/shard_map/ppermute | solution.py:431
  83.0 3.9 %collective-permute-done.5 = f32[128,128]{1,0:T(8,128)S(1)} collective-permute-done((f32[128,128]{1,0:T(8,128)S(1)}, f32[128,128]{1,0:T(8,128)S(1)}, u32[]{:S(2)}, u32[]{:S(2)}) %collective-permute-start.5) | collective-permute-done | bytes 65568 | tf_op jit(solution)/shard_map/ppermute | solution.py:431
  86.9 1.9 %collective-permute-start.6 = (f32[64,128]{1,0:T(8,128)S(1)}, f32[64,128]{1,0:T(8,128)S(1)}, u32[]{:S(2)}, u32[]{:S(2)}) collective-permute-start(f32[64,128]{1,0:T(8,128)S(1)} %slice_add_fusion), channel_id=1, source_target_pairs={{0,1},{1,0},{2,3},{3,2},{4,5},{5,4},{6,7},{7,6},{8,9},{9,8},{10,11... | collective-permute-start | bytes 98312 | tf_op jit(solution)/shard_map/ppermute | solution.py:425
  88.8 1.2 %collective-permute-done.6 = f32[64,128]{1,0:T(8,128)S(1)} collective-permute-done((f32[64,128]{1,0:T(8,128)S(1)}, f32[64,128]{1,0:T(8,128)S(1)}, u32[]{:S(2)}, u32[]{:S(2)}) %collective-permute-start.6) | collective-permute-done | bytes 32800 | tf_op jit(solution)/shard_map/ppermute | solution.py:425
  90.0 0.6 fusion
  (3 shorter events, 0.0 us)
Async XLA Ops:
  0.0 42.1 %copy-start = (s32[8,16,128]{2,1,0:T(8,128)S(1)}, s32[8,16,128]{2,1,0:T(8,128)}, u32[]{:S(2)}) copy-start(s32[8,16,128]{2,1,0:T(8,128)} %open_ref.5) | copy-start | bytes 196612
  0.0 50.1 %copy-start.3 = (f32[32,2]{0,1:T(2,128)S(1)}, f32[32,2]{0,1:T(2,128)}, u32[]{:S(2)}) copy-start(f32[32,2]{0,1:T(2,128)} %param.17) | copy-start | bytes 772
  0.0 50.1 %copy-start.2 = (s32[32,2]{0,1:T(2,128)S(1)}, s32[32,2]{0,1:T(2,128)}, u32[]{:S(2)}) copy-start(s32[32,2]{0,1:T(2,128)} %param.16) | copy-start | bytes 772
  17.3 24.8 %all-to-all-start = ((f32[8,8,16,128]{3,2,1,0:T(8,128)}), f32[8,8,16,128]{3,2,1,0:T(8,128)S(1)}, u32[]{:S(2)}, u32[]{:S(2)}) async-start(f32[8,8,16,128]{3,2,1,0:T(8,128)} %shard_map.92), calls=%async_computation | async-start | bytes 1048576 | tf_op jit(solution)/shard_map/all_to_all | solution.py:435
  27.4 25.2 %collective-permute-start = (f32[8,3,32,128]{3,2,1,0:T(8,128)}, f32[8,3,32,128]{3,2,1,0:T(8,128)S(1)}, u32[]{:S(2)}, u32[]{:S(2)}) collective-permute-start(f32[8,3,32,128]{3,2,1,0:T(8,128)} %get-tuple-element.15), channel_id=1, source_target_pairs={{0,1},{1,0},{2,3},{3,2},{4,5},{5,4},{6,7},{7,6},{8,9},{9,8},{10,11... | collective-permute-start | bytes 1179656 | tf_op jit(solution)/shard_map/ppermute | solution.py:425
  30.3 22.3 %collective-permute-start.1 = (f32[8,3,32,128]{3,2,1,0:T(8,128)}, f32[8,3,32,128]{3,2,1,0:T(8,128)S(1)}, u32[]{:S(2)}, u32[]{:S(2)}) collective-permute-start(f32[8,3,32,128]{3,2,1,0:T(8,128)} %get-tuple-element.16), channel_id=1, source_target_pairs={{1,2},{2,1},{3,4},{4,3},{5,6},{6,5},{7,8},{8,7},{9,10},{10,9},{11,... | collective-permute-start | bytes 1179656 | tf_op jit(solution)/shard_map/ppermute | solution.py:431
  42.7 9.9 %collective-permute-start.2 = (f32[8,16,128]{2,1,0:T(8,128)S(1)}, f32[8,16,128]{2,1,0:T(8,128)S(1)}, u32[]{:S(2)}, u32[]{:S(2)}) collective-permute-start(f32[8,16,128]{2,1,0:T(8,128)S(1)} %get-tuple-element.17), channel_id=1, source_target_pairs={{0,1},{1,0},{2,3},{3,2},{4,5},{5,4},{6,7},{7,6},{8,9},{9,8},{10,11... | collective-permute-start | bytes 196616 | tf_op jit(solution)/shard_map/ppermute | solution.py:425
  45.1 8.9 %collective-permute-start.3 = (f32[8,16,128]{2,1,0:T(8,128)S(1)}, f32[8,16,128]{2,1,0:T(8,128)S(1)}, u32[]{:S(2)}, u32[]{:S(2)}) collective-permute-start(f32[8,16,128]{2,1,0:T(8,128)S(1)} %get-tuple-element.18), channel_id=1, source_target_pairs={{1,2},{2,1},{3,4},{4,3},{5,6},{6,5},{7,8},{8,7},{9,10},{10,9},{11,... | collective-permute-start | bytes 196616 | tf_op jit(solution)/shard_map/ppermute | solution.py:431
  52.6 7.0 %copy-start.1 = (s32[4,8,16,128]{3,2,1,0:T(8,128)S(1)}, s32[4,8,16,128]{3,2,1,0:T(8,128)}, u32[]{:S(2)}) copy-start(s32[4,8,16,128]{3,2,1,0:T(8,128)} %pilot_ref.1) | copy-start | bytes 786436
  74.9 3.1 %collective-permute-start.4 = (f32[64,128]{1,0:T(8,128)S(1)}, f32[64,128]{1,0:T(8,128)S(1)}, u32[]{:S(2)}, u32[]{:S(2)}) collective-permute-start(f32[64,128]{1,0:T(8,128)S(1)} %get-tuple-element.21), channel_id=1, source_target_pairs={{0,1},{1,0},{2,3},{3,2},{4,5},{5,4},{6,7},{7,6},{8,9},{9,8},{10,11... | collective-permute-start | bytes 98312 | tf_op jit(solution)/shard_map/ppermute | solution.py:425
  78.0 8.9 %collective-permute-start.5 = (f32[128,128]{1,0:T(8,128)S(1)}, f32[128,128]{1,0:T(8,128)S(1)}, u32[]{:S(2)}, u32[]{:S(2)}) collective-permute-start(f32[128,128]{1,0:T(8,128)S(1)} %pad_maximum_fusion), channel_id=1, source_target_pairs={{1,2},{2,1},{3,4},{4,3},{5,6},{6,5},{7,8},{8,7},{9,10},{10,9},{11,... | collective-permute-start | bytes 196616 | tf_op jit(solution)/shard_map/ppermute | solution.py:431
  86.9 3.1 %collective-permute-start.6 = (f32[64,128]{1,0:T(8,128)S(1)}, f32[64,128]{1,0:T(8,128)S(1)}, u32[]{:S(2)}, u32[]{:S(2)}) collective-permute-start(f32[64,128]{1,0:T(8,128)S(1)} %slice_add_fusion), channel_id=1, source_target_pairs={{0,1},{1,0},{2,3},{3,2},{4,5},{5,4},{6,7},{7,6},{8,9},{9,8},{10,11... | collective-permute-start | bytes 98312 | tf_op jit(solution)/shard_map/ppermute | solution.py:425

commit v6 on v5

--- a/solution.py
+++ b/solution.py
@@ -28,27 +28,28 @@
 HBM = pl.BlockSpec(memory_space=pltpu.HBM)
 
 
-def spread_kernel(cond_ref, storage_ref, head_ref, krig_ref, med_ref, sem_ref):
+def spread_kernel(cond_ref, storage_ref, head_ref, krig_ref, med_ref, own_ref, in_ref, out_ref):
     parts = (
-        (cond_ref.at[:, 0], 0, 2),
-        (storage_ref, 2, 1),
-        (head_ref, 3, 1),
-        (krig_ref.at[:, 0], 4, NK),
+        (cond_ref.at[:, 0], own_ref.at[pl.ds(0, 2)]),
+        (storage_ref, own_ref.at[pl.ds(2, 1)]),
+        (head_ref, own_ref.at[pl.ds(3, 1)]),
+        (krig_ref.at[:, 0], own_ref.at[pl.ds(4, NK)]),
     )
-    copies = []
-    for layer in range(LAY):
-        for i, (part, first, count) in enumerate(parts):
-            copies.append(
-                pltpu.make_async_copy(
-                    part,
-                    med_ref.at[layer, pl.ds(first, count)],
-                    sem_ref.at[len(parts) * layer + i],
-                )
-            )
-    for copy in copies:
-        copy.start()
-    for copy in copies:
-        copy.wait()
+    loads = [
+        pltpu.make_async_copy(part, place, in_ref.at[i]) for i, (part, place) in enumerate(parts)
+    ]
+    for load in loads:
+        load.start()
+    for load in loads:
+        load.wait()
+    stores = [
+        pltpu.make_async_copy(own_ref, med_ref.at[layer], out_ref.at[layer])
+        for layer in range(LAY)
+    ]
+    for store in stores:
+        store.start()
+    for store in stores:
+        store.wait()
 
 
 def turn_kernel(tile_ref, adj_ref, turned_ref, pair_ref, other_ref, buf_ref, sem_ref):
@@ -77,12 +78,18 @@
     lax.fori_loop(0, LAY, body, 0)
 
 
+def place_of(layer, odd):
+    return layer + odd * (LAY - 1 - 2 * layer)
+
+
 def medium_edges_kernel(tile_ref, med_ref, open_ref, pair_ref, other_ref):
-    odd = tile_ref[0, 0] % 2 == 1
+    parity = tile_ref[0, 0] % 2
+    odd = parity == 1
     for layer in range(LAY):
+        place = place_of(layer, parity)
         for field in range(5):
             if field < 4:
-                tile = med_ref[layer, field]
+                tile = med_ref[place, field]
             else:
                 tile = open_ref[layer].astype(F32)
             low = tile[:HALO]
@@ -122,7 +129,7 @@
             fill = jnp.ones((OFF, TY), F32)
             ext_ref[field, layer, pl.ds(0, OFF), :] = fill
             ext_ref[field, layer, pl.ds(OFF + TX, OFF), :] = fill
-            own = med_ref[layer, field] if field < 4 else open_ref[layer].astype(F32)
+            own = med_ref[place_of(layer, odd), field] if field < 4 else open_ref[layer].astype(F32)
             ext_ref[field, layer, pl.ds(OFF, TX), :] = own
             if med_pair_ref is None:
                 continue
@@ -347,7 +354,8 @@
 
     for layer in range(LAY):
         index = [pilot_ref[k, layer] - base for k in range(NK)]
-        share = [med_ref[layer, 4 + k] for k in range(NK)]
+        place = place_of(layer, tile % 2)
+        share = [med_ref[place, 4 + k] for k in range(NK)]
         for k in range(1, NK):
             for j in range(k):
                 same = index[j] == index[k]
@@ -431,8 +439,14 @@
     return lax.ppermute(block, "grid", pairs)
 
 
-def gathered(copies, axis):
-    return lax.all_to_all(copies, axis, 0, 0, tiled=False)
+def gathered(copies):
+    layers = lax.axis_size("obs")
+    tiles = lax.axis_size("grid")
+    groups = [
+        [place_of(layer, tile % 2) * tiles + tile for layer in range(layers)]
+        for tile in range(tiles)
+    ]
+    return lax.all_to_all(copies, ("obs", "grid"), 0, 0, axis_index_groups=groups, tiled=False)
 
 
 def local(
@@ -455,10 +469,14 @@
         out_shape=copies,
         in_specs=[HBM] * 4,
         out_specs=HBM,
-        scratch_shapes=[pltpu.SemaphoreType.DMA((4 * LAY,))],
+        scratch_shapes=[
+            pltpu.VMEM((4 + NK, TX, TY), F32),
+            pltpu.SemaphoreType.DMA((4,)),
+            pltpu.SemaphoreType.DMA((LAY,)),
+        ],
         compiler_params=pltpu.CompilerParams(vmem_limit_bytes=4 * 2**20),
     )(*map(in_hbm, (conductance, storage, head, krig_weight)))
-    medium = gathered(copies, "obs")
+    medium = gathered(copies)
 
     edge = sds((LAY, HALO, OBS, TY), F32)
     turned, pair, other = pl.pallas_call(

time: 91 us -> 72.4 us (0.80)
  Pallas kernels: 44.3 us -> 28.8 us
  waiting for transfers between devices: 14.4 us -> 7.62 us
  starting transfers between devices: 31 us -> 34.7 us
    pallas_call x1, Pallas kernels: 17.3 us -> 1.74 us  [local(): pl.pallas_call(spread_kernel, out_shape=copies, in_specs=[HBM] * 4, out_s...]
    all_to_all x1, waiting for transfers between devices: 6.78 us -> 0.01 us  [gathered(): lax.all_to_all(copies, ('obs', 'grid'), 0, 0, axis_index_groups=groups, t...]
    ppermute x4, starting transfers between devices: 9.09 us -> 12.5 us  [swapped(): return lax.ppermute(block, 'grid', [(i, i ^ 1) for i in range(count)])]
  transfers between devices with their start and end apart: 8 -> 8, of which waited for: 5 -> 4; matrix products, arithmetic and copies ran while one was open for 0% -> 0% of each run, Pallas kernels for 7% -> 9%
where the time goes in v6:
time: 72.4 us; the launch traced here: 72 us
  starting transfers between devices  34.7 us (48%)
  Pallas kernels  28.8 us (40%)
  waiting for transfers between devices  7.62 us (11%)
    pallas_call x1, Pallas kernels, local(): pl.pallas_call(krig_kernel, out_shape=(piece, sds((4 * OBS, P_DEV), F32),...  15.3 us
    ppermute x3, starting transfers between devices, crossed(): return lax.ppermute(block, 'grid', pairs)  15.1 us
    ppermute x4, starting transfers between devices, swapped(): return lax.ppermute(block, 'grid', [(i, i ^ 1) for i in range(count)])  12.5 us
    all_to_all x1, starting transfers between devices, gathered(): lax.all_to_all(copies, ('obs', 'grid'), 0, 0, axis_index_groups=groups, t...  7.11 us
    pallas_call x1, Pallas kernels, local(): pl.pallas_call(stencil_kernel, out_shape=sds((LAY * TX // 2, 2 * OBS, 2 *...  5.6 us
    ppermute x3, waiting for transfers between devices, crossed(): return lax.ppermute(block, 'grid', pairs)  5.26 us
    pallas_call x1, Pallas kernels, local(): pl.pallas_call(turn_kernel, out_shape=(sds((LAY, TX, OBS, TY), F32), edge...  3.19 us
    pallas_call x1, Pallas kernels, local(): pl.pallas_call(interior_kernel, out_shape=sds((LAY, TX - 2, OBS, TY), F32...  2.41 us
  transfers between devices with their start and end apart: 8, of which 4 were waited for; matrix products, arithmetic and copies ran while one was open for 0% of the time, Pallas kernels for 9%

profile of v6, /device:TPU:199, one launch (start us, length us, event | category | flops | bytes accessed | tf_op | source)
XLA Modules:
  0.0 72.0 jit_solution(1282163208406863518)
XLA Ops:
  0.0 0.0 copy-start
  0.0 0.0 copy-start.3
  0.0 0.0 copy-start.2
  0.0 1.7 %shard_map.92 = f32[8,8,16,128]{3,2,1,0:T(8,128)} custom-call(f32[2,1,16,128]{3,2,1,0:T(8,128)} %cond_ref.1, f32[1,16,128]{2,1,0:T(8,128)} %storage_ref.1, f32[1,16,128]{2,1,0:T(8,128)} %head_ref.1, f32[4,1,16,128]{3,2,1,0:T(8,128)} %krig_ref.1), custom_call_target="tpu_custom_call" | custom-call | tf_op jit(solution)/shard_map/pallas_call | solution.py:467
  1.8 7.1 %all-to-all-start = ((f32[8,8,16,128]{3,2,1,0:T(8,128)}), f32[8,8,16,128]{3,2,1,0:T(8,128)S(1)}, u32[]{:S(2)}, u32[]{:S(2)}) async-start(f32[8,8,16,128]{3,2,1,0:T(8,128)} %shard_map.92), calls=%async_computation | async-start | bytes 1048576 | tf_op jit(solution)/shard_map/all_to_all | solution.py:449
  8.9 0.1 add_bitcast_fusion.tile_ref
  8.9 3.2 %shard_map.91 = (f32[8,16,32,128]{3,2,1,0:T(8,128)S(1)}, f32[8,3,32,128]{3,2,1,0:T(8,128)}, f32[8,3,32,128]{3,2,1,0:T(8,128)}) custom-call(s32[1,2]{1,0:T(1,128)S(1)} %add_bitcast_fusion.tile_ref, f32[32,8,16,128]{3,2,1,0:T(8,128)} %adj_ref.1), custom_call_target="tpu_custom_call" | custom-call | tf_op jit(solution)/shard_map/pallas_call | solution.py:482
  12.1 2.6 %collective-permute-start = (f32[8,3,32,128]{3,2,1,0:T(8,128)}, f32[8,3,32,128]{3,2,1,0:T(8,128)S(1)}, u32[]{:S(2)}, u32[]{:S(2)}) collective-permute-start(f32[8,3,32,128]{3,2,1,0:T(8,128)} %get-tuple-element.15), channel_id=1, source_target_pairs={{0,1},{1,0},{2,3},{3,2},{4,5},{5,4},{6,7},{7,6},{8,9},{9,8},{10,11... | collective-permute-start | bytes 1179656 | tf_op jit(solution)/shard_map/ppermute | solution.py:433
  14.7 5.0 %collective-permute-start.1 = (f32[8,3,32,128]{3,2,1,0:T(8,128)}, f32[8,3,32,128]{3,2,1,0:T(8,128)S(1)}, u32[]{:S(2)}, u32[]{:S(2)}) collective-permute-start(f32[8,3,32,128]{3,2,1,0:T(8,128)} %get-tuple-element.16), channel_id=1, source_target_pairs={{1,2},{2,1},{3,4},{4,3},{5,6},{6,5},{7,8},{8,7},{9,10},{10,9},{11,... | collective-permute-start | bytes 1179656 | tf_op jit(solution)/shard_map/ppermute | solution.py:439
  19.8 0.0 all-to-all-done.med_ref
  19.8 0.0 copy-done
  19.8 0.6 shard_map.93
  20.4 6.1 %collective-permute-start.2 = (f32[8,16,128]{2,1,0:T(8,128)S(1)}, f32[8,16,128]{2,1,0:T(8,128)S(1)}, u32[]{:S(2)}, u32[]{:S(2)}) collective-permute-start(f32[8,16,128]{2,1,0:T(8,128)S(1)} %get-tuple-element.17), channel_id=1, source_target_pairs={{0,1},{1,0},{2,3},{3,2},{4,5},{5,4},{6,7},{7,6},{8,9},{9,8},{10,11... | collective-permute-start | bytes 196616 | tf_op jit(solution)/shard_map/ppermute | solution.py:433
  26.5 5.0 %collective-permute-start.3 = (f32[8,16,128]{2,1,0:T(8,128)S(1)}, f32[8,16,128]{2,1,0:T(8,128)S(1)}, u32[]{:S(2)}, u32[]{:S(2)}) collective-permute-start(f32[8,16,128]{2,1,0:T(8,128)S(1)} %get-tuple-element.18), channel_id=1, source_target_pairs={{1,2},{2,1},{3,4},{4,3},{5,6},{6,5},{7,8},{8,7},{9,10},{10,9},{11,... | collective-permute-start | bytes 196616 | tf_op jit(solution)/shard_map/ppermute | solution.py:439
  31.5 0.0 copy-done.3
  31.5 0.0 copy-done.2
  31.5 2.4 %shard_map.94.inner_ref = f32[8,14,32,128]{3,2,1,0:T(8,128)S(1)} custom-call(s32[1,2]{1,0:T(1,128)S(1)} %add_bitcast_fusion.tile_ref, f32[8,16,32,128]{3,2,1,0:T(8,128)S(1)} %get-tuple-element.14.turned_ref, f32[8,8,16,128]{3,2,1,0:T(8,128)S(1)} %all-to-all-done.med_ref, s32[8,16,128]{2,1,0:T(8,128)S(1)} %copy-done, s32[2,32]{1,0:T(2,128)S(1)} %bitcast.6, ...), custom_call_target="tpu_custom_call" | custom-call | tf_op jit(solution)/shard_map/pallas_call | solution.py:509
  34.0 0.0 copy-start.1
  34.0 0.0 collective-permute-done.pair_ref
  34.0 0.0 collective-permute-done.1.other_ref
  34.0 0.0 collective-permute-done.2.med_pair_ref
  34.0 1.4 %collective-permute-done.3.med_other_ref = f32[8,16,128]{2,1,0:T(8,128)S(1)} collective-permute-done((f32[8,16,128]{2,1,0:T(8,128)S(1)}, f32[8,16,128]{2,1,0:T(8,128)S(1)}, u32[]{:S(2)}, u32[]{:S(2)}) %collective-permute-start.3) | collective-permute-done | bytes 65568 | tf_op jit(solution)/shard_map/ppermute | solution.py:439
  35.4 5.6 %shard_map.95.sens_ref = f32[64,64,256]{2,1,0:T(8,128)S(1)} custom-call(s32[1,2]{1,0:T(1,128)S(1)} %add_bitcast_fusion.tile_ref, f32[8,16,32,128]{3,2,1,0:T(8,128)S(1)} %get-tuple-element.14.turned_ref, f32[8,3,32,128]{3,2,1,0:T(8,128)S(1)} %collective-permute-done.pair_ref, f32[8,3,32,128]{3,2,1,0:T(8,128)S(1)} %collective-permute-done.1.other_ref, ...), custom_call_target="tpu_custom_call" | custom-call | tf_op jit(solution)/shard_map/pallas_call | solution.py:521
  41.0 0.0 copy-done.1
  41.0 15.3 %shard_map.96 = (f32[64,128]{1,0:T(8,128)S(1)}, f32[128,128]{1,0:T(8,128)S(1)}, f32[64,128]{1,0:T(8,128)S(1)}, f32[64,128]{1,0:T(8,128)S(1)}) custom-call(s32[1,2]{1,0:T(1,128)S(1)} %add_bitcast_fusion.tile_ref, f32[64,64,256]{2,1,0:T(8,128)S(1)} %shard_map.95.sens_ref, s32[4,8,16,128]{3,2,1,0:T(8,128)S(1)} %copy-done.1, ...), custom_call_target="tpu_custom_call" | custom-call | tf_op jit(solution)/shard_map/pallas_call | solution.py:550
  56.3 1.9 %collective-permute-start.4 = (f32[64,128]{1,0:T(8,128)S(1)}, f32[64,128]{1,0:T(8,128)S(1)}, u32[]{:S(2)}, u32[]{:S(2)}) collective-permute-start(f32[64,128]{1,0:T(8,128)S(1)} %get-tuple-element.21), channel_id=1, source_target_pairs={{0,1},{1,0},{2,3},{3,2},{4,5},{5,4},{6,7},{7,6},{8,9},{9,8},{10,11... | collective-permute-start | bytes 98312 | tf_op jit(solution)/shard_map/ppermute | solution.py:433
  58.2 1.2 %collective-permute-done.4 = f32[64,128]{1,0:T(8,128)S(1)} collective-permute-done((f32[64,128]{1,0:T(8,128)S(1)}, f32[64,128]{1,0:T(8,128)S(1)}, u32[]{:S(2)}, u32[]{:S(2)}) %collective-permute-start.4) | collective-permute-done | bytes 32800 | tf_op jit(solution)/shard_map/ppermute | solution.py:433
  59.4 5.0 %collective-permute-start.5 = (f32[128,128]{1,0:T(8,128)S(1)}, f32[128,128]{1,0:T(8,128)S(1)}, u32[]{:S(2)}, u32[]{:S(2)}) collective-permute-start(f32[128,128]{1,0:T(8,128)S(1)} %pad_maximum_fusion), channel_id=1, source_target_pairs={{1,2},{2,1},{3,4},{4,3},{5,6},{6,5},{7,8},{8,7},{9,10},{10,9},{11,... | collective-permute-start | bytes 196616 | tf_op jit(solution)/shard_map/ppermute | solution.py:439
  64.4 3.9 %collective-permute-done.5 = f32[128,128]{1,0:T(8,128)S(1)} collective-permute-done((f32[128,128]{1,0:T(8,128)S(1)}, f32[128,128]{1,0:T(8,128)S(1)}, u32[]{:S(2)}, u32[]{:S(2)}) %collective-permute-start.5) | collective-permute-done | bytes 65568 | tf_op jit(solution)/shard_map/ppermute | solution.py:439
  68.3 1.9 %collective-permute-start.6 = (f32[64,128]{1,0:T(8,128)S(1)}, f32[64,128]{1,0:T(8,128)S(1)}, u32[]{:S(2)}, u32[]{:S(2)}) collective-permute-start(f32[64,128]{1,0:T(8,128)S(1)} %slice_add_fusion), channel_id=1, source_target_pairs={{0,1},{1,0},{2,3},{3,2},{4,5},{5,4},{6,7},{7,6},{8,9},{9,8},{10,11... | collective-permute-start | bytes 98312 | tf_op jit(solution)/shard_map/ppermute | solution.py:433
  70.2 1.2 %collective-permute-done.6 = f32[64,128]{1,0:T(8,128)S(1)} collective-permute-done((f32[64,128]{1,0:T(8,128)S(1)}, f32[64,128]{1,0:T(8,128)S(1)}, u32[]{:S(2)}, u32[]{:S(2)}) %collective-permute-start.6) | collective-permute-done | bytes 32800 | tf_op jit(solution)/shard_map/ppermute | solution.py:433
  71.4 0.6 fusion
  (3 shorter events, 0.0 us)
Async XLA Ops:
  0.0 19.8 %copy-start = (s32[8,16,128]{2,1,0:T(8,128)S(1)}, s32[8,16,128]{2,1,0:T(8,128)}, u32[]{:S(2)}) copy-start(s32[8,16,128]{2,1,0:T(8,128)} %open_ref.5) | copy-start | bytes 196612
  0.0 31.5 %copy-start.3 = (f32[32,2]{0,1:T(2,128)S(1)}, f32[32,2]{0,1:T(2,128)}, u32[]{:S(2)}) copy-start(f32[32,2]{0,1:T(2,128)} %param.17) | copy-start | bytes 772
  0.0 31.5 %copy-start.2 = (s32[32,2]{0,1:T(2,128)S(1)}, s32[32,2]{0,1:T(2,128)}, u32[]{:S(2)}) copy-start(s32[32,2]{0,1:T(2,128)} %param.16) | copy-start | bytes 772
  1.8 18.0 %all-to-all-start = ((f32[8,8,16,128]{3,2,1,0:T(8,128)}), f32[8,8,16,128]{3,2,1,0:T(8,128)S(1)}, u32[]{:S(2)}, u32[]{:S(2)}) async-start(f32[8,8,16,128]{3,2,1,0:T(8,128)} %shard_map.92), calls=%async_computation | async-start | bytes 1048576 | tf_op jit(solution)/shard_map/all_to_all | solution.py:449
  12.1 21.8 %collective-permute-start = (f32[8,3,32,128]{3,2,1,0:T(8,128)}, f32[8,3,32,128]{3,2,1,0:T(8,128)S(1)}, u32[]{:S(2)}, u32[]{:S(2)}) collective-permute-start(f32[8,3,32,128]{3,2,1,0:T(8,128)} %get-tuple-element.15), channel_id=1, source_target_pairs={{0,1},{1,0},{2,3},{3,2},{4,5},{5,4},{6,7},{7,6},{8,9},{9,8},{10,11... | collective-permute-start | bytes 1179656 | tf_op jit(solution)/shard_map/ppermute | solution.py:433
  14.7 19.3 %collective-permute-start.1 = (f32[8,3,32,128]{3,2,1,0:T(8,128)}, f32[8,3,32,128]{3,2,1,0:T(8,128)S(1)}, u32[]{:S(2)}, u32[]{:S(2)}) collective-permute-start(f32[8,3,32,128]{3,2,1,0:T(8,128)} %get-tuple-element.16), channel_id=1, source_target_pairs={{1,2},{2,1},{3,4},{4,3},{5,6},{6,5},{7,8},{8,7},{9,10},{10,9},{11,... | collective-permute-start | bytes 1179656 | tf_op jit(solution)/shard_map/ppermute | solution.py:439
  20.4 13.6 %collective-permute-start.2 = (f32[8,16,128]{2,1,0:T(8,128)S(1)}, f32[8,16,128]{2,1,0:T(8,128)S(1)}, u32[]{:S(2)}, u32[]{:S(2)}) collective-permute-start(f32[8,16,128]{2,1,0:T(8,128)S(1)} %get-tuple-element.17), channel_id=1, source_target_pairs={{0,1},{1,0},{2,3},{3,2},{4,5},{5,4},{6,7},{7,6},{8,9},{9,8},{10,11... | collective-permute-start | bytes 196616 | tf_op jit(solution)/shard_map/ppermute | solution.py:433
  26.5 8.9 %collective-permute-start.3 = (f32[8,16,128]{2,1,0:T(8,128)S(1)}, f32[8,16,128]{2,1,0:T(8,128)S(1)}, u32[]{:S(2)}, u32[]{:S(2)}) collective-permute-start(f32[8,16,128]{2,1,0:T(8,128)S(1)} %get-tuple-element.18), channel_id=1, source_target_pairs={{1,2},{2,1},{3,4},{4,3},{5,6},{6,5},{7,8},{8,7},{9,10},{10,9},{11,... | collective-permute-start | bytes 196616 | tf_op jit(solution)/shard_map/ppermute | solution.py:439
  34.0 7.0 %copy-start.1 = (s32[4,8,16,128]{3,2,1,0:T(8,128)S(1)}, s32[4,8,16,128]{3,2,1,0:T(8,128)}, u32[]{:S(2)}) copy-start(s32[4,8,16,128]{3,2,1,0:T(8,128)} %pilot_ref.1) | copy-start | bytes 786436
  56.3 3.1 %collective-permute-start.4 = (f32[64,128]{1,0:T(8,128)S(1)}, f32[64,128]{1,0:T(8,128)S(1)}, u32[]{:S(2)}, u32[]{:S(2)}) collective-permute-start(f32[64,128]{1,0:T(8,128)S(1)} %get-tuple-element.21), channel_id=1, source_target_pairs={{0,1},{1,0},{2,3},{3,2},{4,5},{5,4},{6,7},{7,6},{8,9},{9,8},{10,11... | collective-permute-start | bytes 98312 | tf_op jit(solution)/shard_map/ppermute | solution.py:433
  59.4 8.9 %collective-permute-start.5 = (f32[128,128]{1,0:T(8,128)S(1)}, f32[128,128]{1,0:T(8,128)S(1)}, u32[]{:S(2)}, u32[]{:S(2)}) collective-permute-start(f32[128,128]{1,0:T(8,128)S(1)} %pad_maximum_fusion), channel_id=1, source_target_pairs={{1,2},{2,1},{3,4},{4,3},{5,6},{6,5},{7,8},{8,7},{9,10},{10,9},{11,... | collective-permute-start | bytes 196616 | tf_op jit(solution)/shard_map/ppermute | solution.py:439
  68.3 3.1 %collective-permute-start.6 = (f32[64,128]{1,0:T(8,128)S(1)}, f32[64,128]{1,0:T(8,128)S(1)}, u32[]{:S(2)}, u32[]{:S(2)}) collective-permute-start(f32[64,128]{1,0:T(8,128)S(1)} %slice_add_fusion), channel_id=1, source_target_pairs={{0,1},{1,0},{2,3},{3,2},{4,5},{5,4},{6,7},{7,6},{8,9},{9,8},{10,11... | collective-permute-start | bytes 98312 | tf_op jit(solution)/shard_map/ppermute | solution.py:433
